TPU v7x, 256 devices: a whole 4x4x8 slice. The times are simulated.
256 devices in a mesh: energy: 4 (over z_lo), cluster: 16 (over x, y), tile: 4 (over z_hi, core).
Axes of the slice: x: 4, y: 4, z: 8 (z_hi: 2, z_lo: 4; z = z_hi * 4 + z_lo), core: 2. Of those that a mesh axis runs over, the one named last changes fastest.
Arguments:
- boundary: bfloat16 [16, 2, 512, 8, 2, 1024], P('cluster', None, 'tile', 'energy'), may hold values from -5 to 5
- column_source: int32 [16, 1024], P('cluster'), may hold values from 0 to 1023, as said below
- energy_weights: float32 [8], P('energy'), may hold values from 0.2 to 2
Outputs:
- final_rows: float32 [16, 256, 8, 2, 1024], P('cluster', 'tile', 'energy')
- density: float32 [16, 256], P('cluster', 'tile')
Inputs may be any that keep to these rules, and one draw needn't show every extreme that they name: `column_source`: for each cluster, every index 0 to 1023 appears once.
All inputs are finite; a program needn't handle non-finite values.
Results may differ from a plain program's by a relative error of at most 0.015.
Values may be sent and summed in bfloat16 or wider, within the bound.
No kernel may reach another device: no remote copies, remote signals or barrier semaphores. Data moves between devices by JAX's collectives and lax.ppermute only.
A program may use at most 64 MiB of HBM per device.

v0:
```python
import jax
import jax.numpy as jnp
from jax import lax
from jax.sharding import PartitionSpec as P


def swapped(shard, axis, distance):
    return lax.ppermute(shard, axis, [(i, i ^ 1 << distance) for i in range(lax.axis_size(axis))])


def complex_product(left, right):

    def single(first_part, second_part):
        return jnp.einsum(
            "mek,ken->men", first_part, second_part, preferred_element_type=jnp.float32
        )

    real_part = single(left[:, :, 0], right[:, :, 0]) - single(left[:, :, 1], right[:, :, 1])
    imag_part = single(left[:, :, 0], right[:, :, 1]) + single(left[:, :, 1], right[:, :, 0])
    return jnp.stack([real_part, imag_part], axis=2)


def inverse_guess(interior):
    values = interior.astype(jnp.float32)
    diagonal = jnp.diagonal(values, axis1=0, axis2=3)
    denom = diagonal[:, 0] * diagonal[:, 0] + diagonal[:, 1] * diagonal[:, 1]
    inv_real = diagonal[:, 0] / denom
    inv_imag = -diagonal[:, 1] / denom
    column_real = inv_real[None, :, :]
    column_imag = inv_imag[None, :, :]
    row_real = inv_real.T[:, :, None]
    row_imag = inv_imag.T[:, :, None]
    values_real = values[:, :, 0]
    values_imag = values[:, :, 1]
    temp_real = values_real * column_real - values_imag * column_imag
    temp_imag = values_real * column_imag + values_imag * column_real
    prod_real = row_real * temp_real - row_imag * temp_imag
    prod_imag = row_real * temp_imag + row_imag * temp_real
    ident = jnp.eye(values.shape[0], dtype=jnp.float32)[:, None, :]
    guess_real = 2.0 * ident * row_real - prod_real
    guess_imag = 2.0 * ident * row_imag - prod_imag
    return jnp.stack([guess_real, guess_imag], axis=2).astype(jnp.bfloat16)


def place_block(block, is_low):
    zeros = jnp.zeros_like(block)
    return jnp.where(
        is_low, jnp.concatenate([block, zeros], axis=3), jnp.concatenate([zeros, block], axis=3)
    )


def swap_separator(separator, level_index):
    return swapped(separator, "cluster", level_index)


def eliminate(outer_coupling, start_block, interior, approx_inverse, coupling_rows):
    applied = complex_product(outer_coupling.astype(jnp.bfloat16), approx_inverse)
    middle = complex_product(applied.astype(jnp.bfloat16), interior).astype(jnp.bfloat16)
    reduced = (2.0 * applied - complex_product(middle, approx_inverse)).astype(jnp.bfloat16)
    row_piece = lax.all_gather(coupling_rows, "tile", axis=0, tiled=True)
    columns = lax.slice_in_dim(reduced, 0, row_piece.shape[0], axis=3)
    return start_block - complex_product(columns, row_piece)


def per_device(boundary, column_source, energy_weights):
    stored = boundary[0]
    canonical = jnp.take(stored, column_source[0], axis=4)
    separator = canonical[0]
    outer_rows = canonical[1]
    interior_width = separator.shape[3] // 2
    row_count = separator.shape[0]
    levels = min(2, lax.axis_size("cluster") // 2)
    cluster_index = lax.axis_index("cluster")
    tile_index = lax.axis_index("tile")
    for level_index in range(levels):
        side_bit = cluster_index // 2**level_index % 2
        is_low = side_bit == 0
        final_level = level_index == levels - 1
        if final_level:
            partner_outer = outer_rows
            partner_sep = swap_separator(separator, level_index)
        else:
            partner_sep, partner_outer = swapped((separator, outer_rows), "cluster", level_index)
            separator = separator.astype(jnp.float32)
            outer_rows = outer_rows.astype(jnp.float32)
            partner_sep = partner_sep.astype(jnp.float32)
            partner_outer = partner_outer.astype(jnp.float32)
        interior_rows = (
            separator[..., :interior_width] + partner_sep[..., :interior_width]
        ).astype(jnp.bfloat16)
        interior = lax.all_gather(interior_rows, "tile", axis=0, tiled=True)
        approx_inverse = inverse_guess(interior)
        low_sep = jnp.where(is_low, separator, partner_sep)
        high_sep = jnp.where(is_low, partner_sep, separator)
        coupling_rows = jnp.concatenate(
            [low_sep[..., interior_width:], high_sep[..., interior_width:]], axis=3
        ).astype(jnp.bfloat16)
        if final_level:
            share = row_count // 2**level_index
            within = cluster_index % 2**level_index
            own_rows = lax.dynamic_slice_in_dim(outer_rows, within * share, share, 0)
            new_rows = eliminate(
                own_rows[..., :interior_width],
                place_block(own_rows[..., interior_width:], is_low),
                interior,
                approx_inverse,
                coupling_rows,
            )
            columns = (
                side_bit * interior_width
                + tile_index * row_count
                + within * share
                + jnp.arange(share, dtype=jnp.int32)
            )
            selector = (
                jnp.arange(new_rows.shape[3], dtype=jnp.int32)[None, :] == columns[:, None]
            ).astype(jnp.float32)
            diagonal = jnp.sum(new_rows[:, :, 1, :] * selector[:, None, :], axis=2)
            partial_sum = jnp.sum(diagonal * energy_weights[None, :], axis=1)
            density = lax.psum(partial_sum, "energy")
            return (new_rows[None], density[None])
        else:
            low_outer = jnp.where(is_low, outer_rows, partner_outer)
            high_outer = jnp.where(is_low, partner_outer, outer_rows)
            outer_coupling = jnp.concatenate(
                [low_outer[..., :interior_width], high_outer[..., :interior_width]], axis=0
            )
            start_block = jnp.concatenate(
                [
                    place_block(low_outer[..., interior_width:], True),
                    place_block(high_outer[..., interior_width:], False),
                ],
                axis=0,
            )
            merged = eliminate(outer_coupling, start_block, interior, approx_inverse, coupling_rows)
            separator = merged[:row_count]
            outer_rows = merged[row_count:]


def solution(mesh):
    placed = (P("cluster", None, "tile", "energy", None, None), P("cluster", None), P("energy"))
    return jax.shard_map(
        per_device,
        mesh=mesh,
        in_specs=placed,
        out_specs=(P("cluster", "tile", "energy", None, None), P("cluster", "tile")),
        check_vma=False,
    )
```

profile of v0, /device:TPU:2, one launch (start us, length us, event | category | flops | bytes accessed | tf_op | source)
XLA Modules:
  0.0 364.8 jit_solution(14689596253726604121)
XLA Ops:
  7.2 8.9 %copy.65 = bf16[1,2,128,2,2,1024]{2,4,5,3,1,0:T(2,128)(2,1)S(1)} copy(bf16[1,2,128,2,2,1024]{5,4,3,2,1,0:T(2,128)(2,1)} %param.3) | data formatting | bytes 4194304 | tf_op args[0]
  16.2 12.1 %gather_fusion = bf16[1024,2,128,2,2]{2,4,3,1,0:T(2,128)(2,1)} fusion(bf16[2,128,2,2,1024]{1,3,4,2,0:T(2,128)(2,1)S(1)} %bitcast.255, s32[1024]{0:T(1024)S(1)} %broadcast_clamp_fusion), kind=kCustom, calls=%fused_computation | custom fusion | bytes 4198400 | tf_op jit(solution)/shard_map/jit(_take)/gather | solution.py:67
  28.3 6.1 %copy.66 = bf16[1024,2,128,2,2]{0,2,3,4,1:T(8,128)(2,1)} copy(bf16[1024,2,128,2,2]{2,4,3,1,0:T(2,128)(2,1)} %gather_fusion) | data formatting | bytes 4194304 | tf_op jit(solution)/shard_map/jit(_take)/gather | solution.py:67
  39.2 23.3 %collective-permute-done.1 = bf16[128,2,2,1024]{3,0,1,2:T(8,128)(2,1)S(1)} collective-permute-done((bf16[128,2,2,1024]{3,0,1,2:T(8,128)(2,1)S(1)}, bf16[128,2,2,1024]{3,0,1,2:T(8,128)(2,1)S(1)}, u32[]{:S(2)}, u32[]{:S(2)}) %collective-permute-start.1) | collective-permute-done | bytes 1048608 | tf_op jit(solution)/shard_map/ppermute | solution.py:8
  69.9 19.8 %collective-permute-done = bf16[128,2,2,1024]{3,0,1,2:T(8,128)(2,1)} collective-permute-done((bf16[128,2,2,1024]{3,0,1,2:T(8,128)(2,1)}, bf16[128,2,2,1024]{3,0,1,2:T(8,128)(2,1)}, u32[]{:S(2)}, u32[]{:S(2)}) %collective-permute-start) | collective-permute-done | bytes 1048608 | tf_op jit(solution)/shard_map/ppermute | solution.py:8
  89.6 1.8 convert_select_fusion.1
  93.7 17.7 %all-gather.7.cloned.1.call-done = bf16[512,2,2,512]{3,0,1,2:T(8,128)(2,1)} async-done(((bf16[128,2,2,512]{3,0,1,2:T(8,128)(2,1)}), bf16[512,2,2,512]{3,0,1,2:T(8,128)(2,1)}) %all-gather.7.cloned.1.call-update) | async-done | bytes 2097168 | tf_op jit(solution)/shard_map/all_gather | solution.py:91
  111.5 4.3 %fusion.65 = (f32[512,2,2,512]{3,0,1,2:T(8,128)}, f32[2,2,512,512]{3,2,0,1:T(8,128)S(1)}) fusion(bf16[512,2,2,512]{3,0,1,2:T(8,128)(2,1)} %all-gather.7.cloned.1.call-done), kind=kLoop, calls=%fused_computation.154 | loop fusion | flops 1048576 | bytes 10485760 | tf_op jit(solution)/shard_map/convert_element_type | solution.py:24
  115.7 5.2 %copy.67 = f32[2,2,512,512]{3,1,2,0:T(2,128)} copy(f32[2,2,512,512]{3,2,0,1:T(8,128)S(1)} %get-tuple-element.23) | data formatting | bytes 8388608 | tf_op jit(solution)/shard_map/jit(diagonal)/transpose | solution.py:25
  121.0 7.5 %gather_fusion.1 = f32[512,2,2]{0,2,1:T(2,128)S(1)} fusion(f32[2,2,512,512]{3,1,2,0:T(2,128)} %copy.67, s32[512]{0:T(512)S(1)} %bitcast.253), kind=kCustom, calls=%fused_computation.1 | custom fusion | bytes 20480 | tf_op jit(solution)/shard_map/jit(diagonal)/gather | solution.py:25
  128.5 2.9 fusion.31
  139.9 36.3 %all-gather.5.cloned.1.call-done = bf16[512,2,2,1024]{3,0,1,2:T(8,128)(2,1)} async-done(((bf16[128,2,2,1024]{3,0,1,2:T(8,128)(2,1)}), bf16[512,2,2,1024]{3,0,1,2:T(8,128)(2,1)}) %all-gather.5.cloned.1.call-update) | async-done | bytes 4194320 | tf_op jit(solution)/shard_map/all_gather | solution.py:60
  176.1 2.5 fusion.3
  184.8 3.0 collective-permute-start.2
  187.9 46.3 %collective-permute-done.2 = f32[128,2,2,1024]{3,0,1,2:T(8,128)S(1)} collective-permute-done((f32[128,2,2,1024]{3,0,1,2:T(8,128)S(1)}, f32[128,2,2,1024]{3,0,1,2:T(8,128)S(1)}, u32[]{:S(2)}, u32[]{:S(2)}) %collective-permute-start.2) | collective-permute-done | bytes 2097184 | tf_op jit(solution)/shard_map/ppermute | solution.py:8
  241.4 34.5 %all-gather.11.cloned.1.call-done = bf16[512,2,2,512]{3,0,1,2:T(8,128)(2,1)} async-done(((bf16[128,2,2,512]{3,0,1,2:T(8,128)(2,1)}), bf16[512,2,2,512]{3,0,1,2:T(8,128)(2,1)}) %all-gather.11.cloned.1.call-update) | async-done | bytes 2097168 | tf_op jit(solution)/shard_map/all_gather | solution.py:91
  275.9 4.3 %fusion.64 = (f32[512,2,2,512]{3,0,1,2:T(8,128)}, f32[2,2,512,512]{3,2,0,1:T(8,128)S(1)}) fusion(bf16[512,2,2,512]{3,0,1,2:T(8,128)(2,1)} %all-gather.11.cloned.1.call-done), kind=kLoop, calls=%fused_computation.153 | loop fusion | flops 1048576 | bytes 10485760 | tf_op jit(solution)/shard_map/convert_element_type | solution.py:24
  280.2 5.2 %copy.95 = f32[2,2,512,512]{3,1,2,0:T(2,128)} copy(f32[2,2,512,512]{3,2,0,1:T(8,128)S(1)} %get-tuple-element.21) | data formatting | bytes 8388608 | tf_op jit(solution)/shard_map/jit(diagonal)/transpose | solution.py:25
  285.4 7.2 %gather_fusion.2 = f32[512,2,2]{0,2,1:T(2,128)S(1)} fusion(f32[2,2,512,512]{3,1,2,0:T(2,128)} %copy.95, s32[512]{0:T(512)S(1)} %bitcast.254), kind=kCustom, calls=%fused_computation.2 | custom fusion | bytes 20480 | tf_op jit(solution)/shard_map/jit(diagonal)/gather | solution.py:25
  292.7 2.9 fusion.33
  300.3 40.8 %all-gather.9.cloned.1.call-done = bf16[512,2,2,1024]{3,0,1,2:T(8,128)(2,1)} async-done(((bf16[128,2,2,1024]{3,0,1,2:T(8,128)(2,1)}), bf16[512,2,2,1024]{3,0,1,2:T(8,128)(2,1)}) %all-gather.9.cloned.1.call-update) | async-done | bytes 4194320 | tf_op jit(solution)/shard_map/all_gather | solution.py:60
  341.0 2.2 fusion.6
  343.3 2.1 fusion.7
  347.2 9.2 %psum.7 = f32[1,64]{1,0:T(1,128)} all-reduce(f32[1,64]{1,0:T(1,128)S(1)} %bitcast.264), channel_id=1, replica_groups=mesh['energy'=4,'cluster'=16,'tile'=4] {'energy'}, use_global_device_ids=true, to_apply=%region_2.3 | all-reduce | flops 64 | bytes 512 | tf_op jit(solution)/shard_map/psum | solution.py:120
  (104 shorter events, 44.3 us)
Async XLA Ops:
  7.2 9.0 %copy-start.12 = (s32[1,1024]{1,0:T(1,128)S(1)}, s32[1,1024]{1,0:T(1,128)}, u32[]{:S(2)}) copy-start(s32[1,1024]{1,0:T(1,128)} %param.4) | copy-start | bytes 12292
  7.2 104.3 %all-gather.7.cloned.1.call-start = ((), (), s32[]{:S(2)}) async-start(), calls=%async_computation.1 | async-start | bytes 2621440 | tf_op jit(solution)/shard_map/all_gather | solution.py:91
  37.7 25.2 %copy-start.4 = (f32[128,2,2,1024]{3,0,1,2:T(8,128)}, f32[128,2,2,1024]{3,0,1,2:T(8,128)S(1)}, u32[]{:S(2)}) copy-start(f32[128,2,2,1024]{3,0,1,2:T(8,128)S(1)} %get-tuple-element.24) | copy-start | bytes 6291460
  37.7 24.9 %collective-permute-start.1 = (bf16[128,2,2,1024]{3,0,1,2:T(8,128)(2,1)S(1)}, bf16[128,2,2,1024]{3,0,1,2:T(8,128)(2,1)S(1)}, u32[]{:S(2)}, u32[]{:S(2)}) collective-permute-start(bf16[128,2,2,1024]{3,0,1,2:T(8,128)(2,1)S(1)} %get-tuple-element.25), channel_id=1, source_target_pairs={{0,4},{4,0},{8,12},{12,8},{16,20},{20,16},{24,28},{28,24},{32,36},... | collective-permute-start | bytes 3145736 | tf_op jit(solution)/shard_map/ppermute | solution.py:8
  62.8 1.4 copy-start.5
  65.1 111.0 %all-gather.5.cloned.1.call-start = ((), (), s32[]{:S(2)}) async-start(), calls=%async_computation | async-start | bytes 5242880 | tf_op jit(solution)/shard_map/all_gather | solution.py:60
  65.2 24.4 %collective-permute-start = (bf16[128,2,2,1024]{3,0,1,2:T(8,128)(2,1)}, bf16[128,2,2,1024]{3,0,1,2:T(8,128)(2,1)}, u32[]{:S(2)}, u32[]{:S(2)}) collective-permute-start(bf16[128,2,2,1024]{3,0,1,2:T(8,128)(2,1)} %get-tuple-element.26), channel_id=1, source_target_pairs={{0,4},{4,0},{8,12},{12,8},{16,20},{20,16},{24,28},{28,24},{32,36},... | collective-permute-start | bytes 3145736 | tf_op jit(solution)/shard_map/ppermute | solution.py:8
  69.7 206.3 %all-gather.11.cloned.1.call-start = ((), (), s32[]{:S(2)}) async-start(), calls=%async_computation.3 | async-start | bytes 2621440 | tf_op jit(solution)/shard_map/all_gather | solution.py:91
  133.5 1.6 copy-start
  176.1 2.8 copy-start.3
  180.5 1.2 copy-start.7
  180.5 1.5 copy-start.8
  183.5 1.4 copy-start.9
  183.5 55.9 %copy-start.6 = (f32[128,2,2,1024]{3,0,1,2:T(8,128)}, f32[128,2,2,1024]{3,0,1,2:T(8,128)S(1)}, u32[]{:S(2)}) copy-start(f32[128,2,2,1024]{3,0,1,2:T(8,128)S(1)} %get-tuple-element.12) | copy-start | bytes 6291460
  184.8 49.3 %collective-permute-start.2 = (f32[128,2,2,1024]{3,0,1,2:T(8,128)S(1)}, f32[128,2,2,1024]{3,0,1,2:T(8,128)S(1)}, u32[]{:S(2)}, u32[]{:S(2)}) collective-permute-start(f32[128,2,2,1024]{3,0,1,2:T(8,128)S(1)} %get-tuple-element.13), channel_id=1, source_target_pairs={{0,8},{4,12},{8,0},{12,4},{16,24},{20,28},{24,16},{28,20},{32,40},... | collective-permute-start | bytes 6291464 | tf_op jit(solution)/shard_map/ppermute | solution.py:8
  234.1 1.3 copy-start.11
  236.4 104.6 %all-gather.9.cloned.1.call-start = ((), (), s32[]{:S(2)}) async-start(), calls=%async_computation.2 | async-start | bytes 5242880 | tf_op jit(solution)/shard_map/all_gather | solution.py:60
  292.6 2.9 copy-start.10
  296.2 1.6 copy-start.1
  341.0 4.3 %copy-start.2 = (bf16[512,2,2,1024]{3,0,1,2:T(8,128)(2,1)S(1)}, bf16[512,2,2,1024]{3,0,1,2:T(8,128)(2,1)}, u32[]{:S(2)}) copy-start(bf16[512,2,2,1024]{3,0,1,2:T(8,128)(2,1)} %all-gather.9.cloned.1.call-done) | copy-start | bytes 12582916
  346.5 0.7 copy-start.13
Sparse Core Ops, SparseCore 0:
  65.3 46.1 all-gather.6
  113.3 62.8 all-gather.4
  236.6 39.3 all-gather.10
  278.2 62.8 all-gather.8
where the time goes:
time: 366 us; the launch traced here: 365 us
  waiting for transfers between devices  219 us (60%)
  local copies, waits for them, and re-layouts  66.6 us (18%)
  other arithmetic  29.4 us (8%)
  matrix products  20.1 us (5%)
  between operations  14.3 us (4%)
  blocking collectives  9.25 us (3%)
  starting transfers between devices  6.41 us (2%)
    ppermute x3, waiting for transfers between devices, swapped(): lax.ppermute(shard, axis, [(i, i ^ 1 << distance) for i in range(lax.axis...  89.4 us
    all_gather x2, waiting for transfers between devices, eliminate(): row_piece = lax.all_gather(coupling_rows, 'tile', axis=0, tiled=True)  77 us
    all_gather x2, waiting for transfers between devices, per_device(): interior = lax.all_gather(interior_rows, 'tile', axis=0, tiled=True)  52.2 us
    dot_general x32, matrix products, single(): jnp.einsum('mek,ken->men', first_part, second_part, preferred_element_typ...  20.1 us
    unnamed x30, local copies, waits for them, and re-layouts  18.5 us
    gather x2, local copies, waits for them, and re-layouts, per_device(): canonical = jnp.take(stored, column_source[0], axis=4)  18.3 us
    gather x2, local copies, waits for them, and re-layouts, inverse_guess(): diagonal = jnp.diagonal(values, axis1=0, axis2=3)  14.7 us
    transpose x2, local copies, waits for them, and re-layouts, inverse_guess(): diagonal = jnp.diagonal(values, axis1=0, axis2=3)  10.5 us
  transfers between devices with their start and end apart: 7, of which 7 were waited for; matrix products, arithmetic and copies ran while one was open for 17% of the time, Pallas kernels for 0%

commit v1 on v0

v1 whole, which is shorter than its diff:
```python
import jax
import jax.numpy as jnp
from jax import lax
from jax.experimental import pallas as pl
from jax.experimental.pallas import tpu as pltpu
from jax.sharding import PartitionSpec as P


F32 = jnp.float32
BF16 = jnp.bfloat16
LANES = 128


def exchange(x, axis, distance):
    return lax.ppermute(x, axis, [(i, i ^ distance) for i in range(lax.axis_size(axis))])


def dot(x, y):
    return jnp.dot(x, y, preferred_element_type=F32)


def stacked(x):
    return x.reshape(2 * x.shape[1], x.shape[2])


def product(x, y_real, y_imag):
    rows = x.shape[0] // 2
    by_real, by_imag = dot(x, y_real), dot(x, y_imag)
    return by_real[:rows] - by_imag[rows:], by_imag[:rows] + by_real[rows:]


def halved(pair):
    return jnp.concatenate([pair[0].astype(BF16), pair[1].astype(BF16)], axis=0)


def at(start, size):
    return pl.ds(pl.multiple_of(start, size), size)


class Copies:
    def __init__(self, sems):
        self.sems = sems
        self.made = []

    def start(self, source, target):
        copy = pltpu.make_async_copy(source, target, self.sems.at[len(self.made)])
        copy.start()
        self.made.append(copy)
        return copy


def wait(copies):
    for copy in copies:
        copy.wait()


def call(body, out_shape, scratch, copies, flops, *args, in_vmem=(), in_smem=(), grant=40):
    spaces = [pltpu.HBM] * len(args)
    for i in in_vmem:
        spaces[i] = pltpu.VMEM
    for i in in_smem:
        spaces[i] = pltpu.SMEM
    return pl.pallas_call(
        body,
        out_shape=out_shape,
        in_specs=[pl.BlockSpec(memory_space=space) for space in spaces],
        out_specs=[pl.BlockSpec(memory_space=pltpu.VMEM)] * len(out_shape),
        scratch_shapes=scratch + [pltpu.SemaphoreType.DMA((copies,))],
        compiler_params=pltpu.CompilerParams(vmem_limit_bytes=grant << 20),
        cost_estimate=pl.CostEstimate(flops=flops, bytes_accessed=4 << 20, transcendentals=0),
    )(*args)


def places():
    cluster = lax.axis_index("cluster")
    tile = lax.axis_index("tile")
    return cluster % 2, tile // 2, tile % 2, cluster // 2 % 2


def fill_selector(column_ref, selector):
    size = selector.shape[0]
    source = lax.broadcasted_iota(jnp.int32, (size, size), 0)
    selector[...] = jnp.where(source == column_ref[...], 1.0, 0.0).astype(BF16)


def reorder(stage, selector, parted):
    count, _, nodes = stage.shape
    flat = stage[...].reshape(2 * count, nodes)
    wide = 2 * LANES
    for first in range(0, nodes, wide):
        ordered = dot(flat, selector[:, first : first + wide])
        for turn in range(2):
            parted[first // LANES + turn] = ordered[:, turn * LANES : (turn + 1) * LANES]


def lane_block(parted, block, part, first, count):
    return parted[block, pl.ds(2 * first + part, count, stride=2), :].astype(BF16)


def order_far(column_ref, raw, far_out, column, stage, selector, parted, sems):
    _, depth, _, _ = places()
    copies = Copies(sems)
    first = copies.start(column_ref, column)
    copy = copies.start(raw.at[0, 0, :, 1 - depth], stage)
    first.wait()
    fill_selector(column, selector)
    copy.wait()
    reorder(stage, selector, parted)
    count = stage.shape[0]
    for block in range(parted.shape[0]):
        for part in range(2):
            far_out[part, :, block * LANES : (block + 1) * LANES] = lane_block(
                parted, block, part, 0, count
            )


def order_rest(
    column_ref, raw, near_out, keep_out, keep_far_out, send_out,
    column, near_stage, outer_stage, selector, near_parted, outer_parted, sems,
):
    side, depth, _, _ = places()
    copies = Copies(sems)
    first = copies.start(column_ref, column)
    few = outer_stage.shape[0] // 4
    outer = []
    for row, (half, energy) in enumerate(((1, 0), (1, 1), (0, 0), (0, 1))):
        rows = at((side ^ half) * few, few)
        outer.append(
            copies.start(raw.at[0, 1, rows, depth ^ energy], outer_stage.at[pl.ds(row * few, few)])
        )
    near = copies.start(raw.at[0, 0, :, depth], near_stage)
    first.wait()
    fill_selector(column, selector)
    wait(outer)
    reorder(outer_stage, selector, outer_parted)
    blocks = outer_parted.shape[0]
    for block in range(blocks):
        lanes = slice(block * LANES, (block + 1) * LANES)
        for part in range(2):
            for energy in range(2):
                send_out[energy, part, :, lanes] = lane_block(
                    outer_parted, block, part, energy * few, few
                )
            keep_out[part, :, lanes] = lane_block(outer_parted, block, part, 2 * few, few)
            keep_far_out[part, :, lanes] = lane_block(outer_parted, block, part, 3 * few, few)
    near.wait()
    reorder(near_stage, selector, near_parted)
    for block in range(blocks):
        for part in range(2):
            near_out[part, :, block * LANES : (block + 1) * LANES] = lane_block(
                near_parted, block, part, 0, near_stage.shape[0]
            )


def assemble(parts, interior):
    for part in range(2):
        interior[part] = (parts[0, part].astype(F32) + parts[1, part].astype(F32)).astype(BF16)


def guess(interior, approx):
    size = interior.shape[1]
    real = interior[0].astype(F32)
    imag = interior[1].astype(F32)

    def on_diagonal(count):
        return lax.broadcasted_iota(jnp.int32, (count, count), 0) == lax.broadcasted_iota(
            jnp.int32, (count, count), 1
        )

    block_diag = on_diagonal(LANES)

    def diagonal(values, axis):
        found = []
        for first in range(0, size, LANES):
            span = slice(first, first + LANES)
            block = jnp.where(block_diag, values[span, span], 0.0)
            found.append(jnp.sum(block, axis=axis, keepdims=True))
        return jnp.concatenate(found, axis=1 - axis)

    def reciprocal(axis):
        diag_real = diagonal(real, axis)
        diag_imag = diagonal(imag, axis)
        denom = diag_real * diag_real + diag_imag * diag_imag
        return diag_real / denom, -diag_imag / denom

    col_real, col_imag = reciprocal(0)
    row_real, row_imag = reciprocal(1)
    temp_real = real * col_real - imag * col_imag
    temp_imag = real * col_imag + imag * col_real
    prod_real = row_real * temp_real - row_imag * temp_imag
    prod_imag = row_real * temp_imag + row_imag * temp_real
    on_diag = on_diagonal(size)
    approx[0] = (jnp.where(on_diag, 2.0 * row_real, 0.0) - prod_real).astype(BF16)
    approx[1] = (jnp.where(on_diag, 2.0 * row_imag, 0.0) - prod_imag).astype(BF16)


def eliminate(left, interior, approx):
    applied = product(left, approx[0], approx[1])
    middle = halved(product(halved(applied), interior[0], interior[1]))
    second = product(middle, approx[0], approx[1])
    return halved((2.0 * applied[0] - second[0], 2.0 * applied[1] - second[1]))


def first_level(*refs):
    near, far = refs[0:4], refs[4:8]
    keep, got, deep = refs[8:11]
    sep_out, left_out, corner_out = refs[11:14]
    parts, interior, approx, right, left, start, sems = refs[14:]
    side, depth, core, _ = places()
    copies = Copies(sems)
    width = interior.shape[1]
    rows = near[0].shape[1]
    few = rows // 2
    lows, highs = pl.ds(0, width), pl.ds(width, width)

    def sep(columns, target):
        made = []
        for turn in range(2):
            for core_step in range(2):
                who = core_step * 2 + turn
                for step, pieces in enumerate((near, far)):
                    row = at(((depth ^ step) * 2 + (core ^ core_step)) * rows, rows)
                    made.append(
                        copies.start(pieces[who].at[:, :, columns], target.at[side ^ turn, :, row])
                    )
        return made

    def outer(columns, target):
        near_rows, far_rows = at(depth * few, few), at((1 - depth) * few, few)
        return [
            copies.start(keep.at[:, :, columns], target.at[side, :, near_rows]),
            copies.start(got.at[0, :, :, columns], target.at[1 - side, :, near_rows]),
            copies.start(deep.at[0, :, :, columns], target.at[side, :, far_rows]),
            copies.start(deep.at[1, :, :, columns], target.at[1 - side, :, far_rows]),
        ]

    from_inner = sep(lows, parts)
    from_left = outer(lows, left)
    from_cross = sep(highs, right)
    from_start = outer(highs, start)
    wait(from_inner)
    assemble(parts, interior)
    guess(interior, approx)
    wait(from_left)
    both = jnp.concatenate([left[0, 0], left[1, 0], left[0, 1], left[1, 1]], axis=0)
    reduced = eliminate(both, interior, approx)
    wait(from_cross)
    wait(from_start)
    low_taken = product(reduced, right[0, 0], right[0, 1])
    high_taken = product(reduced, right[1, 0], right[1, 1])
    for part in range(2):
        sep_out[part, :, :width] = (
            start[0, part].astype(F32) - low_taken[part][:rows]
        ).astype(BF16)
        sep_out[part, :, width:] = (-high_taken[part][:rows]).astype(BF16)
        left_out[part] = (-low_taken[part][rows:]).astype(BF16)
        corner_out[part] = start[1, part].astype(F32) - high_taken[part][rows:]


def last_level(*refs):
    pieces = refs[:8]
    left, corner, weights = refs[8:11]
    keep_out, send_out, keep_diag_out, send_diag_out = refs[11:15]
    parts, interior, approx, right, total, diag, sems = refs[15:]
    side, depth, core, pair = places()
    copies = Copies(sems)
    width = interior.shape[1]
    rows = corner.shape[1]
    few = rows // 2

    def spread(columns, target):
        made = []
        for who, piece in enumerate(pieces):
            core_step, pair_step, side_step = who // 4, who // 2 % 2, who % 2
            for deep in range(2):
                row = (deep * 2 + (core ^ core_step)) * rows + (side ^ side_step) * few
                made.append(
                    copies.start(
                        piece.at[:, pl.ds(deep * few, few), columns],
                        target.at[pair ^ pair_step, :, at(row, few)],
                    )
                )
        return made

    from_inner = spread(pl.ds(0, width), parts)
    from_cross = spread(pl.ds(width, width), right)
    wait(from_inner)
    assemble(parts, interior)
    guess(interior, approx)
    reduced = eliminate(stacked(left[...]), interior, approx)
    wait(from_cross)
    for owner in range(2):
        taken = product(reduced, right[owner, 0], right[owner, 1])
        for part in range(2):
            start = jnp.where(pair == owner, corner[part], 0.0)
            total[part, :, owner * width : (owner + 1) * width] = start - taken[part]
    own = total[1, :, at(pair * width, width)]
    row_of = lax.broadcasted_iota(jnp.int32, (few, LANES), 0) + side * few
    lane_of = lax.broadcasted_iota(jnp.int32, (few, LANES), 1)
    for deep in range(2):
        for_core = [
            own[deep * few : (deep + 1) * few, tile * LANES : (tile + 1) * LANES]
            for tile in (deep * 2, deep * 2 + 1)
        ]
        block = jnp.where(core == 0, for_core[0], for_core[1])
        found = jnp.sum(jnp.where(row_of == lane_of, block, 0.0), axis=0, keepdims=True)
        diag[deep] = found * weights[depth]
    keep_diag_out[...] = diag[depth]
    send_diag_out[...] = diag[1 - depth]
    near_rows, far_rows = at(depth * few, few), at((1 - depth) * few, few)
    for part in range(2):
        send_out[part] = total[part, far_rows, :].astype(BF16)
        keep_out[part] = total[part, near_rows, :]


def after(x, *others):
    return lax.optimization_barrier((x,) + others)[0]


def compute(boundary, column_source, energy_weights):
    _, _, rows, _, _, nodes = boundary.shape
    half = nodes // 2
    few = rows // 2
    depth = lax.axis_index("tile") // 2

    def bf16(*shape):
        return jax.ShapeDtypeStruct(shape, BF16)

    def f32(*shape):
        return jax.ShapeDtypeStruct(shape, F32)

    selector = pltpu.VMEM((nodes, nodes), BF16)
    column = pltpu.VMEM((1, nodes), jnp.int32)
    lane_blocks = nodes // LANES
    (far_raw,) = call(
        order_far,
        [bf16(2, rows, nodes)],
        [
            column,
            pltpu.VMEM((rows, 2, nodes), BF16),
            selector,
            pltpu.VMEM((lane_blocks, 2 * rows, LANES), F32),
        ],
        2,
        int(1e9),
        column_source,
        boundary,
        grant=63,
    )
    far = exchange(far_raw, "tile", 2)
    near, keep, keep_far, send = call(
        order_rest,
        [bf16(2, rows, nodes), bf16(2, few, nodes), bf16(2, few, nodes), bf16(2, 2, few, nodes)],
        [
            column,
            pltpu.VMEM((rows, 2, nodes), BF16),
            pltpu.VMEM((4 * few, 2, nodes), BF16),
            selector,
            pltpu.VMEM((lane_blocks, 2 * rows, LANES), F32),
            pltpu.VMEM((lane_blocks, 8 * few, LANES), F32),
        ],
        6,
        int(2e9),
        after(column_source, far_raw),
        boundary,
        grant=56,
    )
    got = exchange(send, "cluster", 1)
    near_core = exchange(near, "tile", 1)
    near_side = exchange(after(near, got), "cluster", 1)
    to_deep = jnp.stack([keep_far, got[1]])
    deep = exchange(to_deep, "tile", 2)
    near_side_core = exchange(near_side, "tile", 1)
    far = after(far, to_deep)
    far_side = exchange(far, "cluster", 1)
    far_core = exchange(far, "tile", 1)
    far_side_core = exchange(far_side, "tile", 1)

    weights = jnp.concatenate([energy_weights, energy_weights])

    weights = jnp.concatenate([energy_weights, energy_weights])

    weights = jnp.concatenate([energy_weights, energy_weights])

    square = pltpu.VMEM((2, half, half), BF16)
    squares = pltpu.VMEM((2, 2, half, half), BF16)
    sep_rows, left, corner = call(
        first_level,
        [bf16(2, rows, nodes), bf16(2, rows, half), f32(2, rows, half)],
        [
            squares,
            square,
            square,
            squares,
            pltpu.VMEM((2, 2, rows, half), BF16),
            pltpu.VMEM((2, 2, rows, half), BF16),
        ],
        24,
        int(2.7e9),
        near,
        near_side,
        near_core,
        near_side_core,
        far,
        far_side,
        far_core,
        far_side_core,
        keep,
        got,
        deep,
    )
    mine = [sep_rows] + [exchange(sep_rows, "cluster", distance) for distance in (1, 2, 3)]
    kept, sent, kept_diag, sent_diag = call(
        last_level,
        [f32(2, few, nodes), bf16(2, few, nodes), f32(1, LANES), f32(1, LANES)],
        [
            squares,
            square,
            square,
            squares,
            pltpu.VMEM((2, rows, nodes), F32),
            pltpu.VMEM((2, 1, LANES), F32),
        ],
        32,
        int(1.4e9),
        *mine,
        *[exchange(x, "tile", 1) for x in mine],
        left,
        corner,
        weights,
        in_vmem=(8, 9),
        in_smem=(10,),
    )
    got_diag = exchange(sent_diag, "tile", 2)
    got_rows = exchange(sent, "tile", 2).astype(F32)
    density = lax.psum(kept_diag + got_diag, "energy")
    density = density[:, :few] + density[:, few:]
    low = jnp.where(depth == 0, kept, got_rows)
    high = jnp.where(depth == 0, got_rows, kept)
    final_rows = jnp.stack([low, high]).transpose(2, 0, 1, 3)
    return final_rows[None], density


def solution(mesh):
    placed = (P("cluster", None, "tile", "energy", None, None), P("cluster", None), P("energy"))
    return jax.shard_map(
        compute,
        mesh=mesh,
        in_specs=placed,
        out_specs=(P("cluster", "tile", "energy", None, None), P("cluster", "tile")),
        check_vma=False,
    )
```

time: 366 us -> 137 us (0.37)
  waiting for transfers between devices: 219 us -> 59.5 us
  local copies, waits for them, and re-layouts: 66.6 us -> 3.8 us
  starting transfers between devices: 6.41 us -> 37 us
  other arithmetic: 29.4 us -> 1.84 us
  matrix products: 20.1 us -> 0 us
  Pallas kernels: 0 us -> 16.7 us
  between operations: 14.3 us -> 0.73 us
  blocking collectives: 9.25 us -> 17.2 us
    all_gather x4 -> x0, waiting for transfers between devices: 129 us -> none  [the longest x2 77 us: eliminate(): row_piece = lax.all_gather(coupling_rows, 'tile', axis=0, tiled=True)]
    gather x4 -> x0, local copies, waits for them, and re-layouts: 32.9 us -> none  [the longest x2 18.3 us: per_device(): canonical = jnp.take(stored, column_source[0], axis=4)]
    ppermute x3 -> x18, starting transfers between devices: 6.25 us -> 37 us  [exchange(): lax.ppermute(x, axis, [(i, i ^ distance) for i in range(lax.axis_size(axi...]
    ppermute x3 -> x18, waiting for transfers between devices: 89.4 us -> 59.5 us  [exchange(): lax.ppermute(x, axis, [(i, i ^ distance) for i in range(lax.axis_size(axi...]
    dot_general x32 -> x0, matrix products: 20.1 us -> none  [single(): jnp.einsum('mek,ken->men', first_part, second_part, preferred_element_typ...]
    pallas_call x0 -> x4, Pallas kernels: none -> 16.7 us  [call(): pl.pallas_call(body, out_shape=out_shape, in_specs=[pl.BlockSpec(memory_s...]
    unnamed x30 -> x9, local copies, waits for them, and re-layouts: 18.5 us -> 3.78 us
    convert_element_type x11 -> x0, other arithmetic: 12.9 us -> none  [the longest x2 8.54 us: inverse_guess(): values = interior.astype(jnp.float32)]
  transfers between devices with their start and end apart: 7 -> 18, of which waited for: 7 -> 9; matrix products, arithmetic and copies ran while one was open for 17% -> 1% of each run, Pallas kernels for 0% -> 0%
where the time goes in v1:
time: 137 us
  waiting for transfers between devices  59.5 us (43%)
  starting transfers between devices  37 us (27%)
  blocking collectives  17.2 us (13%)
  Pallas kernels  16.7 us (12%)
  local copies, waits for them, and re-layouts  3.8 us (3%)
  other arithmetic  1.84 us (1%)
    ppermute x18, waiting for transfers between devices, exchange(): lax.ppermute(x, axis, [(i, i ^ distance) for i in range(lax.axis_size(axi...  59.5 us
    ppermute x18, starting transfers between devices, exchange(): lax.ppermute(x, axis, [(i, i ^ distance) for i in range(lax.axis_size(axi...  37 us
    psum x1, blocking collectives, compute(): density = lax.psum(kept_diag + got_diag, 'energy')  17.2 us
    pallas_call x4, Pallas kernels, call(): pl.pallas_call(body, out_shape=out_shape, in_specs=[pl.BlockSpec(memory_s...  16.7 us
    unnamed x9, local copies, waits for them, and re-layouts  3.78 us
  transfers between devices with their start and end apart: 18, of which 9 were waited for; matrix products, arithmetic and copies ran while one was open for 1% of the time, Pallas kernels for 0%

profile of v1, /device:TPU:2, one launch (start us, length us, event | category | flops | bytes accessed | tf_op | source)
XLA Modules:
  0.0 136.8 jit_solution(2491390329326197461)
XLA Ops:
  0.6 2.9 %shard_map.50 = bf16[2,128,1024]{2,1,0:T(8,128)(2,1)} custom-call(s32[1,1024]{1,0:T(1,128)} %column_ref.2, bf16[1,2,128,2,2,1024]{5,4,3,2,1,0:T(2,128)(2,1)} %raw.3), custom_call_target="tpu_custom_call" | custom-call | flops 1000000000 | bytes 4194304 | tf_op jit(solution)/shard_map/pallas_call | solution.py:63
  3.5 4.4 %shard_map.51 = (bf16[2,128,1024]{2,1,0:T(8,128)(2,1)}, bf16[2,64,1024]{2,1,0:T(8,128)(2,1)}, bf16[2,64,1024]{2,1,0:T(8,128)(2,1)}, bf16[2,2,64,1024]{3,2,1,0:T(8,128)(2,1)}) custom-call(s32[1,1024]{1,0:T(1,128)} %column_ref.2, bf16[1,2,128,2,2,1024]{5,4,3,2,1,0:T(2,128)(2,1)} %raw.3), custom_call_target="tpu_custom_call" | custom-call | flops 2000000000 | bytes 4194304 | tf_op jit(solution)/shard_map/pallas_call | solution.py:63
  8.0 1.7 %collective-permute-start = (bf16[2,2,64,1024]{3,2,1,0:T(8,128)(2,1)}, bf16[2,2,64,1024]{3,2,1,0:T(8,128)(2,1)S(1)}, u32[]{:S(2)}, u32[]{:S(2)}) collective-permute-start(bf16[2,2,64,1024]{3,2,1,0:T(8,128)(2,1)} %get-tuple-element.18), channel_id=1, source_target_pairs={{0,4},{4,0},{8,12},{12,8},{16,20},{20,16},{24,28},{28,24},{32,36},... | collective-permute-start | bytes 1572872 | tf_op jit(solution)/shard_map/ppermute | solution.py:15
  9.6 7.2 %collective-permute-start.4 = (bf16[2,128,1024]{2,1,0:T(8,128)(2,1)S(1)}, bf16[2,128,1024]{2,1,0:T(8,128)(2,1)S(1)}, u32[]{:S(2)}, u32[]{:S(2)}) collective-permute-start(bf16[2,128,1024]{2,1,0:T(8,128)(2,1)S(1)} %copy-done.2), channel_id=1, source_target_pairs={{0,2},{1,3},{2,0},{3,1},{4,6},{5,7},{6,4},{7,5},{8,10},{9,11},{10,... | collective-permute-start | bytes 1572872 | tf_op jit(solution)/shard_map/ppermute | solution.py:15
  16.8 5.1 %collective-permute-done.refs_9_ = bf16[2,2,64,1024]{3,2,1,0:T(8,128)(2,1)S(1)} collective-permute-done((bf16[2,2,64,1024]{3,2,1,0:T(8,128)(2,1)}, bf16[2,2,64,1024]{3,2,1,0:T(8,128)(2,1)S(1)}, u32[]{:S(2)}, u32[]{:S(2)}) %collective-permute-start) | collective-permute-done | bytes 524320 | tf_op jit(solution)/shard_map/ppermute | solution.py:15
  21.9 1.0 pad_maximum_fusion
  22.9 7.8 %collective-permute-done.4.refs_4_ = bf16[2,128,1024]{2,1,0:T(8,128)(2,1)S(1)} collective-permute-done((bf16[2,128,1024]{2,1,0:T(8,128)(2,1)S(1)}, bf16[2,128,1024]{2,1,0:T(8,128)(2,1)S(1)}, u32[]{:S(2)}, u32[]{:S(2)}) %collective-permute-start.4) | collective-permute-done | bytes 524320 | tf_op jit(solution)/shard_map/ppermute | solution.py:15
  31.2 1.6 %collective-permute-start.1 = (bf16[2,128,1024]{2,1,0:T(8,128)(2,1)}, bf16[2,128,1024]{2,1,0:T(8,128)(2,1)S(1)}, u32[]{:S(2)}, u32[]{:S(2)}) collective-permute-start(bf16[2,128,1024]{2,1,0:T(8,128)(2,1)} %get-tuple-element.19.refs_0_), channel_id=1, source_target_pairs={{0,4},{4,0},{8,12},{12,8},{16,20},{20,16},{24,28},{28,24},{32,36},... | collective-permute-start | bytes 1572872 | tf_op jit(solution)/shard_map/ppermute | solution.py:15
  33.3 14.0 %collective-permute-start.8 = (bf16[2,2,64,1024]{3,2,1,0:T(8,128)(2,1)S(1)}, bf16[2,2,64,1024]{3,2,1,0:T(8,128)(2,1)S(1)}, u32[]{:S(2)}, u32[]{:S(2)}) collective-permute-start(bf16[2,2,64,1024]{3,2,1,0:T(8,128)(2,1)S(1)} %pad_maximum_fusion), channel_id=1, source_target_pairs={{0,2},{1,3},{2,0},{3,1},{4,6},{5,7},{6,4},{7,5},{8,10},{9,11},{10,... | collective-permute-start | bytes 1572872 | tf_op jit(solution)/shard_map/ppermute | solution.py:15
  47.3 7.3 %collective-permute-done.1.refs_1_ = bf16[2,128,1024]{2,1,0:T(8,128)(2,1)S(1)} collective-permute-done((bf16[2,128,1024]{2,1,0:T(8,128)(2,1)}, bf16[2,128,1024]{2,1,0:T(8,128)(2,1)S(1)}, u32[]{:S(2)}, u32[]{:S(2)}) %collective-permute-start.1) | collective-permute-done | bytes 524320 | tf_op jit(solution)/shard_map/ppermute | solution.py:15
  54.6 6.2 %collective-permute-done.8.refs_10_ = bf16[2,2,64,1024]{3,2,1,0:T(8,128)(2,1)S(1)} collective-permute-done((bf16[2,2,64,1024]{3,2,1,0:T(8,128)(2,1)S(1)}, bf16[2,2,64,1024]{3,2,1,0:T(8,128)(2,1)S(1)}, u32[]{:S(2)}, u32[]{:S(2)}) %collective-permute-start.8) | collective-permute-done | bytes 524320 | tf_op jit(solution)/shard_map/ppermute | solution.py:15
  60.8 1.0 copy-done
  62.8 5.0 %shard_map.52 = (bf16[2,128,1024]{2,1,0:T(8,128)(2,1)S(1)}, bf16[2,128,512]{2,1,0:T(8,128)(2,1)S(1)}, f32[2,128,512]{2,1,0:T(8,128)S(1)}) custom-call(bf16[2,128,1024]{2,1,0:T(8,128)(2,1)S(1)} %copy-done, bf16[2,128,1024]{2,1,0:T(8,128)(2,1)S(1)} %collective-permute-done.1.refs_1_, bf16[2,128,1024]{2,1,0:T(8,128)(2,1)S(1)} %collective-permute-done.2.refs_2_, ...), custom_call_target="tpu_custom_call" | custom-call | flops 2700000000 | bytes 4194304 | tf_op jit(solution)/shard_map/pallas_call | solution.py:63
  68.3 3.2 %collective-permute-start.10 = (bf16[2,128,1024]{2,1,0:T(8,128)(2,1)S(1)}, bf16[2,128,1024]{2,1,0:T(8,128)(2,1)S(1)}, u32[]{:S(2)}, u32[]{:S(2)}) collective-permute-start(bf16[2,128,1024]{2,1,0:T(8,128)(2,1)S(1)} %get-tuple-element.23.refs_0_), channel_id=1, source_target_pairs={{0,8},{4,12},{8,0},{12,4},{16,24},{20,28},{24,16},{28,20},{32,40},... | collective-permute-start | bytes 1572872 | tf_op jit(solution)/shard_map/ppermute | solution.py:15
  71.5 1.1 collective-permute-start.11
  72.6 10.1 %collective-permute-done.9.refs_1_ = bf16[2,128,1024]{2,1,0:T(8,128)(2,1)S(1)} collective-permute-done((bf16[2,128,1024]{2,1,0:T(8,128)(2,1)S(1)}, bf16[2,128,1024]{2,1,0:T(8,128)(2,1)S(1)}, u32[]{:S(2)}, u32[]{:S(2)}) %collective-permute-start.9) | collective-permute-done | bytes 524320 | tf_op jit(solution)/shard_map/ppermute | solution.py:15
  82.7 11.2 %collective-permute-done.10.refs_2_ = bf16[2,128,1024]{2,1,0:T(8,128)(2,1)S(1)} collective-permute-done((bf16[2,128,1024]{2,1,0:T(8,128)(2,1)S(1)}, bf16[2,128,1024]{2,1,0:T(8,128)(2,1)S(1)}, u32[]{:S(2)}, u32[]{:S(2)}) %collective-permute-start.10) | collective-permute-done | bytes 524320 | tf_op jit(solution)/shard_map/ppermute | solution.py:15
  93.9 2.6 %collective-permute-done.11.refs_3_ = bf16[2,128,1024]{2,1,0:T(8,128)(2,1)S(1)} collective-permute-done((bf16[2,128,1024]{2,1,0:T(8,128)(2,1)S(1)}, bf16[2,128,1024]{2,1,0:T(8,128)(2,1)S(1)}, u32[]{:S(2)}, u32[]{:S(2)}) %collective-permute-start.11) | collective-permute-done | bytes 524320 | tf_op jit(solution)/shard_map/ppermute | solution.py:15
  96.6 1.8 %collective-permute-done.15.refs_7_ = bf16[2,128,1024]{2,1,0:T(8,128)(2,1)S(1)} collective-permute-done((bf16[2,128,1024]{2,1,0:T(8,128)(2,1)S(1)}, bf16[2,128,1024]{2,1,0:T(8,128)(2,1)S(1)}, u32[]{:S(2)}, u32[]{:S(2)}) %collective-permute-start.15) | collective-permute-done | bytes 524320 | tf_op jit(solution)/shard_map/ppermute | solution.py:15
  98.4 4.4 %shard_map.53 = (f32[2,64,1024]{2,1,0:T(8,128)S(1)}, bf16[2,64,1024]{2,1,0:T(8,128)(2,1)S(1)}, f32[1,128]{1,0:T(1,128)S(1)}, f32[1,128]{1,0:T(1,128)S(1)}) custom-call(bf16[2,128,1024]{2,1,0:T(8,128)(2,1)S(1)} %get-tuple-element.23.refs_0_, bf16[2,128,1024]{2,1,0:T(8,128)(2,1)S(1)} %collective-permute-done.9.refs_1_, ...), custom_call_target="tpu_custom_call" | custom-call | flops 1400000000 | bytes 4194304 | tf_op jit(solution)/shard_map/pallas_call | solution.py:63
  102.8 6.7 %collective-permute-start.16 = (bf16[2,64,1024]{2,1,0:T(8,128)(2,1)S(1)}, bf16[2,64,1024]{2,1,0:T(8,128)(2,1)S(1)}, u32[]{:S(2)}, u32[]{:S(2)}) collective-permute-start(bf16[2,64,1024]{2,1,0:T(8,128)(2,1)S(1)} %get-tuple-element.27), channel_id=1, source_target_pairs={{0,2},{1,3},{2,0},{3,1},{4,6},{5,7},{6,4},{7,5},{8,10},{9,11},{10,... | collective-permute-start | bytes 786440 | tf_op jit(solution)/shard_map/ppermute | solution.py:15
  109.6 7.4 %collective-permute-done.17 = f32[1,128]{1,0:T(1,128)S(1)} collective-permute-done((f32[1,128]{1,0:T(1,128)S(1)}, f32[1,128]{1,0:T(1,128)S(1)}, u32[]{:S(2)}, u32[]{:S(2)}) %collective-permute-start.17) | collective-permute-done | bytes 544 | tf_op jit(solution)/shard_map/ppermute | solution.py:15
  117.0 17.2 %psum.7 = f32[1,128]{1,0:T(1,128)S(1)} all-reduce(f32[1,128]{1,0:T(1,128)S(1)} %add.9), channel_id=1, replica_groups=mesh['energy'=4,'cluster'=16,'tile'=4] {'energy'}, use_global_device_ids=true, to_apply=%region_0.1 | all-reduce | flops 128 | bytes 1024 | tf_op jit(solution)/shard_map/psum | solution.py:436
  135.0 1.8 %copy.5 = f32[1,64,2,2,1024]{4,3,2,1,0:T(2,128)} copy(f32[1,64,2,2,1024]{4,1,3,2,0:T(8,128)S(1)} %maximum_bitcast_fusion) | data formatting | bytes 2097152
  (33 shorter events, 3.4 us)
Async XLA Ops:
  3.5 6.1 %copy-start.2 = (bf16[2,128,1024]{2,1,0:T(8,128)(2,1)S(1)}, bf16[2,128,1024]{2,1,0:T(8,128)(2,1)}, u32[]{:S(2)}) copy-start(bf16[2,128,1024]{2,1,0:T(8,128)(2,1)} %shard_map.50) | copy-start | bytes 1572868
  8.0 13.9 %collective-permute-start = (bf16[2,2,64,1024]{3,2,1,0:T(8,128)(2,1)}, bf16[2,2,64,1024]{3,2,1,0:T(8,128)(2,1)S(1)}, u32[]{:S(2)}, u32[]{:S(2)}) collective-permute-start(bf16[2,2,64,1024]{3,2,1,0:T(8,128)(2,1)} %get-tuple-element.18), channel_id=1, source_target_pairs={{0,4},{4,0},{8,12},{12,8},{16,20},{20,16},{24,28},{28,24},{32,36},... | collective-permute-start | bytes 1572872 | tf_op jit(solution)/shard_map/ppermute | solution.py:15
  9.6 21.1 %collective-permute-start.4 = (bf16[2,128,1024]{2,1,0:T(8,128)(2,1)S(1)}, bf16[2,128,1024]{2,1,0:T(8,128)(2,1)S(1)}, u32[]{:S(2)}, u32[]{:S(2)}) collective-permute-start(bf16[2,128,1024]{2,1,0:T(8,128)(2,1)S(1)} %copy-done.2), channel_id=1, source_target_pairs={{0,2},{1,3},{2,0},{3,1},{4,6},{5,7},{6,4},{7,5},{8,10},{9,11},{10,... | collective-permute-start | bytes 1572872 | tf_op jit(solution)/shard_map/ppermute | solution.py:15
  30.7 16.6 %collective-permute-start.5 = (bf16[2,128,1024]{2,1,0:T(8,128)(2,1)S(1)}, bf16[2,128,1024]{2,1,0:T(8,128)(2,1)S(1)}, u32[]{:S(2)}, u32[]{:S(2)}) collective-permute-start(bf16[2,128,1024]{2,1,0:T(8,128)(2,1)S(1)} %collective-permute-done.4.refs_4_), channel_id=1, source_target_pairs={{0,4},{4,0},{8,12},{12,8},{16,20},{20,16},{24,28},{28,24},{32,36},... | collective-permute-start | bytes 1572872 | tf_op jit(solution)/shard_map/ppermute | solution.py:15
  31.2 23.4 %collective-permute-start.1 = (bf16[2,128,1024]{2,1,0:T(8,128)(2,1)}, bf16[2,128,1024]{2,1,0:T(8,128)(2,1)S(1)}, u32[]{:S(2)}, u32[]{:S(2)}) collective-permute-start(bf16[2,128,1024]{2,1,0:T(8,128)(2,1)} %get-tuple-element.19.refs_0_), channel_id=1, source_target_pairs={{0,4},{4,0},{8,12},{12,8},{16,20},{20,16},{24,28},{28,24},{32,36},... | collective-permute-start | bytes 1572872 | tf_op jit(solution)/shard_map/ppermute | solution.py:15
  32.7 21.9 %collective-permute-start.2 = (bf16[2,128,1024]{2,1,0:T(8,128)(2,1)}, bf16[2,128,1024]{2,1,0:T(8,128)(2,1)S(1)}, u32[]{:S(2)}, u32[]{:S(2)}) collective-permute-start(bf16[2,128,1024]{2,1,0:T(8,128)(2,1)} %get-tuple-element.19.refs_0_), channel_id=1, source_target_pairs={{0,1},{1,0},{2,3},{3,2},{4,5},{5,4},{6,7},{7,6},{8,9},{9,8},{10,11... | collective-permute-start | bytes 1572872 | tf_op jit(solution)/shard_map/ppermute | solution.py:15
  32.7 21.9 %collective-permute-start.6 = (bf16[2,128,1024]{2,1,0:T(8,128)(2,1)S(1)}, bf16[2,128,1024]{2,1,0:T(8,128)(2,1)S(1)}, u32[]{:S(2)}, u32[]{:S(2)}) collective-permute-start(bf16[2,128,1024]{2,1,0:T(8,128)(2,1)S(1)} %collective-permute-done.4.refs_4_), channel_id=1, source_target_pairs={{0,1},{1,0},{2,3},{3,2},{4,5},{5,4},{6,7},{7,6},{8,9},{9,8},{10,11... | collective-permute-start | bytes 1572872 | tf_op jit(solution)/shard_map/ppermute | solution.py:15
  33.3 27.5 %collective-permute-start.8 = (bf16[2,2,64,1024]{3,2,1,0:T(8,128)(2,1)S(1)}, bf16[2,2,64,1024]{3,2,1,0:T(8,128)(2,1)S(1)}, u32[]{:S(2)}, u32[]{:S(2)}) collective-permute-start(bf16[2,2,64,1024]{3,2,1,0:T(8,128)(2,1)S(1)} %pad_maximum_fusion), channel_id=1, source_target_pairs={{0,2},{1,3},{2,0},{3,1},{4,6},{5,7},{6,4},{7,5},{8,10},{9,11},{10,... | collective-permute-start | bytes 1572872 | tf_op jit(solution)/shard_map/ppermute | solution.py:15
  47.3 13.5 %collective-permute-start.7 = (bf16[2,128,1024]{2,1,0:T(8,128)(2,1)S(1)}, bf16[2,128,1024]{2,1,0:T(8,128)(2,1)S(1)}, u32[]{:S(2)}, u32[]{:S(2)}) collective-permute-start(bf16[2,128,1024]{2,1,0:T(8,128)(2,1)S(1)} %collective-permute-done.5.refs_5_), channel_id=1, source_target_pairs={{0,1},{1,0},{2,3},{3,2},{4,5},{5,4},{6,7},{7,6},{8,9},{9,8},{10,11... | collective-permute-start | bytes 1572872 | tf_op jit(solution)/shard_map/ppermute | solution.py:15
  54.6 6.2 %collective-permute-start.3 = (bf16[2,128,1024]{2,1,0:T(8,128)(2,1)S(1)}, bf16[2,128,1024]{2,1,0:T(8,128)(2,1)S(1)}, u32[]{:S(2)}, u32[]{:S(2)}) collective-permute-start(bf16[2,128,1024]{2,1,0:T(8,128)(2,1)S(1)} %collective-permute-done.1.refs_1_), channel_id=1, source_target_pairs={{0,1},{1,0},{2,3},{3,2},{4,5},{5,4},{6,7},{7,6},{8,9},{9,8},{10,11... | collective-permute-start | bytes 1572872 | tf_op jit(solution)/shard_map/ppermute | solution.py:15
  60.8 1.0 copy-start
  61.8 0.9 copy-start.1
  62.8 33.7 %copy-start.3 = (f32[2]{0:T(128)S(1)}, f32[2]{0:T(128)}, u32[]{:S(2)}) copy-start(f32[2]{0:T(128)} %param.5) | copy-start | bytes 28
  67.8 14.9 %collective-permute-start.9 = (bf16[2,128,1024]{2,1,0:T(8,128)(2,1)S(1)}, bf16[2,128,1024]{2,1,0:T(8,128)(2,1)S(1)}, u32[]{:S(2)}, u32[]{:S(2)}) collective-permute-start(bf16[2,128,1024]{2,1,0:T(8,128)(2,1)S(1)} %get-tuple-element.23.refs_0_), channel_id=1, source_target_pairs={{0,4},{4,0},{8,12},{12,8},{16,20},{20,16},{24,28},{28,24},{32,36},... | collective-permute-start | bytes 1572872 | tf_op jit(solution)/shard_map/ppermute | solution.py:15
  68.3 25.6 %collective-permute-start.10 = (bf16[2,128,1024]{2,1,0:T(8,128)(2,1)S(1)}, bf16[2,128,1024]{2,1,0:T(8,128)(2,1)S(1)}, u32[]{:S(2)}, u32[]{:S(2)}) collective-permute-start(bf16[2,128,1024]{2,1,0:T(8,128)(2,1)S(1)} %get-tuple-element.23.refs_0_), channel_id=1, source_target_pairs={{0,8},{4,12},{8,0},{12,4},{16,24},{20,28},{24,16},{28,20},{32,40},... | collective-permute-start | bytes 1572872 | tf_op jit(solution)/shard_map/ppermute | solution.py:15
  71.5 25.0 %collective-permute-start.11 = (bf16[2,128,1024]{2,1,0:T(8,128)(2,1)S(1)}, bf16[2,128,1024]{2,1,0:T(8,128)(2,1)S(1)}, u32[]{:S(2)}, u32[]{:S(2)}) collective-permute-start(bf16[2,128,1024]{2,1,0:T(8,128)(2,1)S(1)} %get-tuple-element.23.refs_0_), channel_id=1, source_target_pairs={{0,12},{4,8},{8,4},{12,0},{16,28},{20,24},{24,20},{28,16},{32,44},... | collective-permute-start | bytes 1572872 | tf_op jit(solution)/shard_map/ppermute | solution.py:15
  72.6 24.0 %collective-permute-start.12 = (bf16[2,128,1024]{2,1,0:T(8,128)(2,1)S(1)}, bf16[2,128,1024]{2,1,0:T(8,128)(2,1)S(1)}, u32[]{:S(2)}, u32[]{:S(2)}) collective-permute-start(bf16[2,128,1024]{2,1,0:T(8,128)(2,1)S(1)} %get-tuple-element.23.refs_0_), channel_id=1, source_target_pairs={{0,1},{1,0},{2,3},{3,2},{4,5},{5,4},{6,7},{7,6},{8,9},{9,8},{10,11... | collective-permute-start | bytes 1572872 | tf_op jit(solution)/shard_map/ppermute | solution.py:15
  82.7 13.9 %collective-permute-start.13 = (bf16[2,128,1024]{2,1,0:T(8,128)(2,1)S(1)}, bf16[2,128,1024]{2,1,0:T(8,128)(2,1)S(1)}, u32[]{:S(2)}, u32[]{:S(2)}) collective-permute-start(bf16[2,128,1024]{2,1,0:T(8,128)(2,1)S(1)} %collective-permute-done.9.refs_1_), channel_id=1, source_target_pairs={{0,1},{1,0},{2,3},{3,2},{4,5},{5,4},{6,7},{7,6},{8,9},{9,8},{10,11... | collective-permute-start | bytes 1572872 | tf_op jit(solution)/shard_map/ppermute | solution.py:15
  93.9 2.7 %collective-permute-start.14 = (bf16[2,128,1024]{2,1,0:T(8,128)(2,1)S(1)}, bf16[2,128,1024]{2,1,0:T(8,128)(2,1)S(1)}, u32[]{:S(2)}, u32[]{:S(2)}) collective-permute-start(bf16[2,128,1024]{2,1,0:T(8,128)(2,1)S(1)} %collective-permute-done.10.refs_2_), channel_id=1, source_target_pairs={{0,1},{1,0},{2,3},{3,2},{4,5},{5,4},{6,7},{7,6},{8,9},{9,8},{10,11... | collective-permute-start | bytes 1572872 | tf_op jit(solution)/shard_map/ppermute | solution.py:15
  96.5 1.9 %collective-permute-start.15 = (bf16[2,128,1024]{2,1,0:T(8,128)(2,1)S(1)}, bf16[2,128,1024]{2,1,0:T(8,128)(2,1)S(1)}, u32[]{:S(2)}, u32[]{:S(2)}) collective-permute-start(bf16[2,128,1024]{2,1,0:T(8,128)(2,1)S(1)} %collective-permute-done.11.refs_3_), channel_id=1, source_target_pairs={{0,1},{1,0},{2,3},{3,2},{4,5},{5,4},{6,7},{7,6},{8,9},{9,8},{10,11... | collective-permute-start | bytes 1572872 | tf_op jit(solution)/shard_map/ppermute | solution.py:15
  102.8 31.9 %collective-permute-start.16 = (bf16[2,64,1024]{2,1,0:T(8,128)(2,1)S(1)}, bf16[2,64,1024]{2,1,0:T(8,128)(2,1)S(1)}, u32[]{:S(2)}, u32[]{:S(2)}) collective-permute-start(bf16[2,64,1024]{2,1,0:T(8,128)(2,1)S(1)} %get-tuple-element.27), channel_id=1, source_target_pairs={{0,2},{1,3},{2,0},{3,1},{4,6},{5,7},{6,4},{7,5},{8,10},{9,11},{10,... | collective-permute-start | bytes 786440 | tf_op jit(solution)/shard_map/ppermute | solution.py:15
  109.5 7.5 %collective-permute-start.17 = (f32[1,128]{1,0:T(1,128)S(1)}, f32[1,128]{1,0:T(1,128)S(1)}, u32[]{:S(2)}, u32[]{:S(2)}) collective-permute-start(f32[1,128]{1,0:T(1,128)S(1)} %get-tuple-element.29), channel_id=1, source_target_pairs={{0,2},{1,3},{2,0},{3,1},{4,6},{5,7},{6,4},{7,5},{8,10},{9,11},{10,... | collective-permute-start | bytes 1544 | tf_op jit(solution)/shard_map/ppermute | solution.py:15

commit v2 on v1

v2 whole, which is shorter than its diff:
```python
import jax
import jax.numpy as jnp
from jax import lax
from jax.experimental import pallas as pl
from jax.experimental.pallas import tpu as pltpu
from jax.sharding import PartitionSpec as P


F32 = jnp.float32
BF16 = jnp.bfloat16
LANES = 128


def exchange(x, axis, distance):
    return lax.ppermute(x, axis, [(i, i ^ distance) for i in range(lax.axis_size(axis))])


def dot(x, y):
    return jnp.dot(x, y, preferred_element_type=F32)


def stacked(x):
    return x.reshape(2 * x.shape[1], x.shape[2])


def product(x, y_real, y_imag):
    rows = x.shape[0] // 2
    by_real, by_imag = dot(x, y_real), dot(x, y_imag)
    return by_real[:rows] - by_imag[rows:], by_imag[:rows] + by_real[rows:]


def halved(pair):
    return jnp.concatenate([pair[0].astype(BF16), pair[1].astype(BF16)], axis=0)


def at(start, size):
    return pl.ds(pl.multiple_of(start, size), size)


class Copies:
    def __init__(self, sems):
        self.sems = sems
        self.made = []

    def start(self, source, target):
        copy = pltpu.make_async_copy(source, target, self.sems.at[len(self.made)])
        copy.start()
        self.made.append(copy)
        return copy


def wait(copies):
    for copy in copies:
        copy.wait()


def call(body, out_shape, scratch, copies, flops, *args, in_vmem=(), in_smem=(), grant=40):
    spaces = [pltpu.HBM] * len(args)
    for i in in_vmem:
        spaces[i] = pltpu.VMEM
    for i in in_smem:
        spaces[i] = pltpu.SMEM
    return pl.pallas_call(
        body,
        out_shape=out_shape,
        in_specs=[pl.BlockSpec(memory_space=space) for space in spaces],
        out_specs=[pl.BlockSpec(memory_space=pltpu.VMEM)] * len(out_shape),
        scratch_shapes=scratch + [pltpu.SemaphoreType.DMA((copies,))],
        compiler_params=pltpu.CompilerParams(vmem_limit_bytes=grant << 20),
        cost_estimate=pl.CostEstimate(flops=flops, bytes_accessed=4 << 20, transcendentals=0),
    )(*args)


def places():
    cluster = lax.axis_index("cluster")
    tile = lax.axis_index("tile")
    return cluster % 2, tile // 2, tile % 2, cluster // 2 % 2


def fill_selector(column_ref, selector):
    size = selector.shape[0]
    source = lax.broadcasted_iota(jnp.int32, (size, size), 0)
    selector[...] = jnp.where(source == column_ref[...], 1.0, 0.0).astype(BF16)


def reorder(stage, selector, parted):
    count, _, nodes = stage.shape
    flat = stage[...].reshape(2 * count, nodes)
    wide = 2 * LANES
    for first in range(0, nodes, wide):
        ordered = dot(flat, selector[:, first : first + wide])
        for turn in range(2):
            parted[first // LANES + turn] = ordered[:, turn * LANES : (turn + 1) * LANES]


def lane_block(parted, block, part, first, count):
    return parted[block, pl.ds(2 * first + part, count, stride=2), :].astype(BF16)


def order_first(
    column_ref, raw, far_out, send_out,
    column, far_stage, send_stage, selector, far_parted, send_parted, sems,
):
    side, depth, _, _ = places()
    copies = Copies(sems)
    first = copies.start(column_ref, column)
    far = copies.start(raw.at[0, 0, :, 1 - depth], far_stage)
    few = send_stage.shape[0] // 2
    rows = at((1 - side) * few, few)
    sent = [
        copies.start(raw.at[0, 1, rows, depth ^ turn], send_stage.at[pl.ds(turn * few, few)])
        for turn in range(2)
    ]
    first.wait()
    fill_selector(column, selector)
    far.wait()
    reorder(far_stage, selector, far_parted)
    blocks = far_parted.shape[0]
    for block in range(blocks):
        lanes = slice(block * LANES, (block + 1) * LANES)
        for part in range(2):
            far_out[part, :, lanes] = lane_block(far_parted, block, part, 0, far_stage.shape[0])
    wait(sent)
    reorder(send_stage, selector, send_parted)
    for block in range(blocks):
        lanes = slice(block * LANES, (block + 1) * LANES)
        for part in range(2):
            for turn in range(2):
                send_out[turn, part, :, lanes] = lane_block(
                    send_parted, block, part, turn * few, few
                )


def order_near(
    column_ref, raw, near_out, keep_out, keep_far_out,
    column, near_stage, keep_stage, selector, near_parted, keep_parted, sems,
):
    side, depth, _, _ = places()
    copies = Copies(sems)
    first = copies.start(column_ref, column)
    few = keep_stage.shape[0] // 2
    rows = at(side * few, few)
    kept = [
        copies.start(raw.at[0, 1, rows, depth ^ turn], keep_stage.at[pl.ds(turn * few, few)])
        for turn in range(2)
    ]
    near = copies.start(raw.at[0, 0, :, depth], near_stage)
    first.wait()
    fill_selector(column, selector)
    wait(kept)
    reorder(keep_stage, selector, keep_parted)
    near.wait()
    reorder(near_stage, selector, near_parted)
    blocks = near_parted.shape[0]
    for block in range(blocks):
        lanes = slice(block * LANES, (block + 1) * LANES)
        for part in range(2):
            keep_out[part, :, lanes] = lane_block(keep_parted, block, part, 0, few)
            keep_far_out[part, :, lanes] = lane_block(keep_parted, block, part, few, few)
            near_out[part, :, lanes] = lane_block(near_parted, block, part, 0, near_stage.shape[0])


def assemble(parts, interior):
    for part in range(2):
        interior[part] = (parts[0, part].astype(F32) + parts[1, part].astype(F32)).astype(BF16)


def guess(interior, approx):
    size = interior.shape[1]
    real = interior[0].astype(F32)
    imag = interior[1].astype(F32)

    def on_diagonal(count):
        return lax.broadcasted_iota(jnp.int32, (count, count), 0) == lax.broadcasted_iota(
            jnp.int32, (count, count), 1
        )

    block_diag = on_diagonal(LANES)

    def diagonal(values, axis):
        found = []
        for first in range(0, size, LANES):
            span = slice(first, first + LANES)
            block = jnp.where(block_diag, values[span, span], 0.0)
            found.append(jnp.sum(block, axis=axis, keepdims=True))
        return jnp.concatenate(found, axis=1 - axis)

    def reciprocal(axis):
        diag_real = diagonal(real, axis)
        diag_imag = diagonal(imag, axis)
        denom = diag_real * diag_real + diag_imag * diag_imag
        return diag_real / denom, -diag_imag / denom

    col_real, col_imag = reciprocal(0)
    row_real, row_imag = reciprocal(1)
    temp_real = real * col_real - imag * col_imag
    temp_imag = real * col_imag + imag * col_real
    prod_real = row_real * temp_real - row_imag * temp_imag
    prod_imag = row_real * temp_imag + row_imag * temp_real
    on_diag = on_diagonal(size)
    approx[0] = (jnp.where(on_diag, 2.0 * row_real, 0.0) - prod_real).astype(BF16)
    approx[1] = (jnp.where(on_diag, 2.0 * row_imag, 0.0) - prod_imag).astype(BF16)


def eliminate(left, interior, approx):
    applied = product(left, approx[0], approx[1])
    middle = halved(product(halved(applied), interior[0], interior[1]))
    second = product(middle, approx[0], approx[1])
    return halved((2.0 * applied[0] - second[0], 2.0 * applied[1] - second[1]))


def merged(left, start, interior, approx, right, sep_out, left_out, corner_out):
    width = interior.shape[1]
    few = sep_out.shape[1]
    both = jnp.concatenate([left[0, 0], left[1, 0], left[0, 1], left[1, 1]], axis=0)
    reduced = eliminate(both, interior, approx)
    low_taken = product(reduced, right[0, 0], right[0, 1])
    high_taken = product(reduced, right[1, 0], right[1, 1])
    for part in range(2):
        sep_out[part, :, :width] = (start[0, part].astype(F32) - low_taken[part][:few]).astype(BF16)
        sep_out[part, :, width:] = (-high_taken[part][:few]).astype(BF16)
        left_out[part] = (-low_taken[part][few:]).astype(BF16)
        corner_out[part] = start[1, part].astype(F32) - high_taken[part][few:]


def near_level(*refs):
    near, far = refs[0:4], refs[4:8]
    keep, got = refs[8:10]
    sep_out, left_out, corner_out, interior, approx, right = refs[10:16]
    parts, left, start, sems = refs[16:]
    side, depth, core, _ = places()
    copies = Copies(sems)
    width = interior.shape[1]
    rows = near[0].shape[1]
    lows, highs = pl.ds(0, width), pl.ds(width, width)

    def sep(columns, target):
        made = []
        for turn in range(2):
            for core_step in range(2):
                who = core_step * 2 + turn
                for step, pieces in enumerate((near, far)):
                    row = at(((depth ^ step) * 2 + (core ^ core_step)) * rows, rows)
                    made.append(
                        copies.start(pieces[who].at[:, :, columns], target.at[side ^ turn, :, row])
                    )
        return made

    def outer(columns, target):
        return [
            copies.start(keep.at[:, :, columns], target.at[side]),
            copies.start(got.at[0, :, :, columns], target.at[1 - side]),
        ]

    from_inner = sep(lows, parts)
    from_outer = outer(lows, left)
    from_cross = sep(highs, right)
    from_outer += outer(highs, start)
    wait(from_inner)
    assemble(parts, interior)
    guess(interior, approx)
    wait(from_outer)
    wait(from_cross)
    merged(left, start, interior, approx, right, sep_out, left_out, corner_out)


def far_level(*refs):
    deep, interior, approx, right, left_near, corner_near = refs[:6]
    sep_out, left_both, corner_both = refs[6:9]
    left, start, sems = refs[9:]
    few = deep.shape[2]
    left_both[:, :few] = left_near[...]
    corner_both[:, :few] = corner_near[...]
    left_out, corner_out = left_both.at[:, few:], corner_both.at[:, few:]
    side, _, _, _ = places()
    copies = Copies(sems)
    width = interior.shape[1]
    made = []
    for turn in range(2):
        for first, target in ((0, left), (width, start)):
            made.append(
                copies.start(deep.at[turn, :, :, pl.ds(first, width)], target.at[side ^ turn])
            )
    wait(made)
    merged(left, start, interior, approx, right, sep_out, left_out, corner_out)


def last_level(*refs):
    pieces = refs[:16]
    left, corner, weights = refs[16:19]
    keep_out, send_out, keep_diag_out, send_diag_out = refs[19:23]
    parts, interior, approx, right, total, sems = refs[23:]
    side, depth, core, pair = places()
    copies = Copies(sems)
    width = interior.shape[1]
    rows = corner.shape[1]
    few = rows // 2

    def spread(columns, target):
        made = []
        for who, piece in enumerate(pieces):
            core_step, step, pair_step, side_step = who // 8, who // 4 % 2, who // 2 % 2, who % 2
            row = ((depth ^ step) * 2 + (core ^ core_step)) * rows + (side ^ side_step) * few
            made.append(
                copies.start(
                    piece.at[:, :, columns], target.at[pair ^ pair_step, :, at(row, few)]
                )
            )
        return made

    from_inner = spread(pl.ds(0, width), parts)
    from_cross = spread(pl.ds(width, width), right)
    wait(from_inner)
    assemble(parts, interior)
    guess(interior, approx)
    reduced = eliminate(stacked(left[...]), interior, approx)
    wait(from_cross)
    for owner in range(2):
        taken = product(reduced, right[owner, 0], right[owner, 1])
        for part in range(2):
            start = jnp.where(pair == owner, corner[part], 0.0)
            total[part, :, owner * width : (owner + 1) * width] = start - taken[part]
    row_of = lax.broadcasted_iota(jnp.int32, (few, LANES), 0) + side * few
    lane_of = lax.broadcasted_iota(jnp.int32, (few, LANES), 1)
    for step, out in enumerate((keep_diag_out, send_diag_out)):
        column = pair * width + ((depth ^ step) * 2 + core) * LANES
        block = total[1, step * few : (step + 1) * few, at(column, LANES)]
        found = jnp.sum(jnp.where(row_of == lane_of, block, 0.0), axis=0, keepdims=True)
        out[...] = found * weights[depth]
    for part in range(2):
        send_out[part] = total[part, few:, :].astype(BF16)
        keep_out[part] = total[part, :few, :]


def after(x, *others):
    return lax.optimization_barrier((x,) + others)[0]


def compute(boundary, column_source, energy_weights):
    _, _, rows, _, _, nodes = boundary.shape
    half = nodes // 2
    few = rows // 2
    depth = lax.axis_index("tile") // 2

    def bf16(*shape):
        return jax.ShapeDtypeStruct(shape, BF16)

    def f32(*shape):
        return jax.ShapeDtypeStruct(shape, F32)

    selector = pltpu.VMEM((nodes, nodes), BF16)
    column = pltpu.VMEM((1, nodes), jnp.int32)
    stage = pltpu.VMEM((rows, 2, nodes), BF16)
    parted = pltpu.VMEM((nodes // LANES, 2 * rows, LANES), F32)
    far_raw, send = call(
        order_first,
        [bf16(2, rows, nodes), bf16(2, 2, few, nodes)],
        [column, stage, stage, selector, parted, parted],
        4,
        int(2e9),
        column_source,
        boundary,
        grant=62,
    )
    far = exchange(far_raw, "tile", 2)
    got = exchange(send, "cluster", 1)
    near, keep, keep_far = call(
        order_near,
        [bf16(2, rows, nodes), bf16(2, few, nodes), bf16(2, few, nodes)],
        [column, stage, stage, selector, parted, parted],
        4,
        int(2e9),
        after(column_source, far_raw),
        boundary,
        grant=40,
    )
    near_core = exchange(near, "tile", 1)
    near_side = exchange(after(near, got), "cluster", 1)
    to_deep = jnp.stack([keep_far, after(got[1], near_side)])
    deep = exchange(to_deep, "tile", 2)
    near_side_core = exchange(near_side, "tile", 1)
    far = after(far, to_deep)
    far_side = exchange(far, "cluster", 1)
    far_core = exchange(far, "tile", 1)
    far_side_core = exchange(far_side, "tile", 1)
    weights = jnp.concatenate([energy_weights, energy_weights])

    square = pltpu.VMEM((2, half, half), BF16)
    squares = pltpu.VMEM((2, 2, half, half), BF16)
    rim = pltpu.VMEM((2, 2, few, half), BF16)
    results = [bf16(2, few, nodes), bf16(2, few, half), f32(2, few, half)]
    sep_near, left_near, corner_near, interior, approx, right = call(
        near_level,
        results + [bf16(2, half, half), bf16(2, half, half), bf16(2, 2, half, half)],
        [squares, rim, rim],
        20,
        int(2e9),
        near,
        near_side,
        near_core,
        near_side_core,
        far,
        far_side,
        far_core,
        far_side_core,
        keep,
        got,
    )
    sep_far, left, corner = call(
        far_level,
        [bf16(2, few, nodes), bf16(2, rows, half), f32(2, rows, half)],
        [rim, rim],
        4,
        int(1.4e9),
        deep,
        interior,
        approx,
        right,
        left_near,
        corner_near,
        in_vmem=(1, 2, 3, 4, 5),
    )

    def around(x):
        return [x] + [exchange(x, "cluster", distance) for distance in (1, 2, 3)]

    near_mine = around(sep_near)
    far_mine = around(sep_far)
    near_others = [exchange(x, "tile", 1) for x in near_mine]
    far_others = [exchange(x, "tile", 1) for x in far_mine]
    kept, sent, kept_diag, sent_diag = call(
        last_level,
        [f32(2, few, nodes), bf16(2, few, nodes), f32(1, LANES), f32(1, LANES)],
        [
            squares,
            square,
            square,
            squares,
            pltpu.VMEM((2, rows, nodes), F32),
        ],
        32,
        int(1.4e9),
        *near_mine,
        *far_mine,
        *near_others,
        *far_others,
        left,
        corner,
        weights,
        in_vmem=(16, 17),
        in_smem=(18,),
        grant=40,
    )
    mine_diag = kept_diag + exchange(sent_diag, "tile", 2)
    got_rows = exchange(sent, "tile", 2).astype(F32)
    density = mine_diag
    for distance in (1, 2):
        density = density + exchange(density, "energy", distance)
    density = density[:, :few] + density[:, few:]
    low = jnp.where(depth == 0, kept, got_rows)
    high = jnp.where(depth == 0, got_rows, kept)
    final_rows = jnp.stack([low, high]).transpose(2, 0, 1, 3)
    return final_rows[None], density


def solution(mesh):
    placed = (P("cluster", None, "tile", "energy", None, None), P("cluster", None), P("energy"))
    return jax.shard_map(
        compute,
        mesh=mesh,
        in_specs=placed,
        out_specs=(P("cluster", "tile", "energy", None, None), P("cluster", "tile")),
        check_vma=False,
    )
```

time: 137 us -> 150 us (1.095)
  waiting for transfers between devices: 59.5 us -> 83.8 us
  blocking collectives: 17.2 us -> 0 us
  starting transfers between devices: 37 us -> 44.7 us
    ppermute x18 -> x27, waiting for transfers between devices: 59.5 us -> 83.8 us  [exchange(): lax.ppermute(x, axis, [(i, i ^ distance) for i in range(lax.axis_size(axi...]
    psum x1 -> x0, blocking collectives: 17.2 us -> none  [compute(): density = lax.psum(kept_diag + got_diag, 'energy')]
    ppermute x18 -> x27, starting transfers between devices: 37 us -> 44.7 us  [exchange(): lax.ppermute(x, axis, [(i, i ^ distance) for i in range(lax.axis_size(axi...]
    pallas_call x4 -> x5, Pallas kernels: 16.7 us -> 16 us  [call(): pl.pallas_call(body, out_shape=out_shape, in_specs=[pl.BlockSpec(memory_s...]
  transfers between devices with their start and end apart: 18 -> 27, of which waited for: 9 -> 17; matrix products, arithmetic and copies ran while one was open for 1% -> 0% of each run, Pallas kernels for 0% -> 4%
where the time goes in v2:
time: 150 us
  waiting for transfers between devices  83.8 us (56%)
  starting transfers between devices  44.7 us (30%)
  Pallas kernels  16 us (11%)
  local copies, waits for them, and re-layouts  3.4 us (2%)
    ppermute x27, waiting for transfers between devices, exchange(): lax.ppermute(x, axis, [(i, i ^ distance) for i in range(lax.axis_size(axi...  83.8 us
    ppermute x27, starting transfers between devices, exchange(): lax.ppermute(x, axis, [(i, i ^ distance) for i in range(lax.axis_size(axi...  44.7 us
    pallas_call x5, Pallas kernels, call(): pl.pallas_call(body, out_shape=out_shape, in_specs=[pl.BlockSpec(memory_s...  16 us
    unnamed x9, local copies, waits for them, and re-layouts  3.38 us
  transfers between devices with their start and end apart: 27, of which 17 were waited for; matrix products, arithmetic and copies ran while one was open for 0% of the time, Pallas kernels for 4%

profile of v2, /device:TPU:2, one launch (start us, length us, event | category | flops | bytes accessed | tf_op | source)
XLA Modules:
  0.0 149.5 jit_solution(5957446482045539982)
XLA Ops:
  0.6 3.8 %shard_map.50 = (bf16[2,128,1024]{2,1,0:T(8,128)(2,1)}, bf16[2,2,64,1024]{3,2,1,0:T(8,128)(2,1)}) custom-call(s32[1,1024]{1,0:T(1,128)} %column_ref.2, bf16[1,2,128,2,2,1024]{5,4,3,2,1,0:T(2,128)(2,1)} %raw.3), custom_call_target="tpu_custom_call" | custom-call | flops 2000000000 | bytes 4194304 | tf_op jit(solution)/shard_map/pallas_call | solution.py:63
  7.7 2.3 %shard_map.51 = (bf16[2,128,1024]{2,1,0:T(8,128)(2,1)S(1)}, bf16[2,64,1024]{2,1,0:T(8,128)(2,1)S(1)}, bf16[2,64,1024]{2,1,0:T(8,128)(2,1)S(1)}) custom-call(s32[1,1024]{1,0:T(1,128)S(1)} %copy-done.1, bf16[1,2,128,2,2,1024]{5,4,3,2,1,0:T(2,128)(2,1)S(1)} %copy-done), custom_call_target="tpu_custom_call" | custom-call | flops 2000000000 | bytes 4194304 | tf_op jit(solution)/shard_map/pallas_call | solution.py:63
  10.0 8.4 %collective-permute-done.refs_9_ = bf16[2,2,64,1024]{3,2,1,0:T(8,128)(2,1)S(1)} collective-permute-done((bf16[2,2,64,1024]{3,2,1,0:T(8,128)(2,1)}, bf16[2,2,64,1024]{3,2,1,0:T(8,128)(2,1)S(1)}, u32[]{:S(2)}, u32[]{:S(2)}) %collective-permute-start) | collective-permute-done | bytes 524320 | tf_op jit(solution)/shard_map/ppermute | solution.py:15
  20.0 7.2 %collective-permute-start.4 = (bf16[2,128,1024]{2,1,0:T(8,128)(2,1)S(1)}, bf16[2,128,1024]{2,1,0:T(8,128)(2,1)S(1)}, u32[]{:S(2)}, u32[]{:S(2)}) collective-permute-start(bf16[2,128,1024]{2,1,0:T(8,128)(2,1)S(1)} %copy-done.2), channel_id=1, source_target_pairs={{0,2},{1,3},{2,0},{3,1},{4,6},{5,7},{6,4},{7,5},{8,10},{9,11},{10,... | collective-permute-start | bytes 1572872 | tf_op jit(solution)/shard_map/ppermute | solution.py:15
  27.2 4.0 %collective-permute-done.1.refs_1_ = bf16[2,128,1024]{2,1,0:T(8,128)(2,1)S(1)} collective-permute-done((bf16[2,128,1024]{2,1,0:T(8,128)(2,1)S(1)}, bf16[2,128,1024]{2,1,0:T(8,128)(2,1)S(1)}, u32[]{:S(2)}, u32[]{:S(2)}) %collective-permute-start.1) | collective-permute-done | bytes 524320 | tf_op jit(solution)/shard_map/ppermute | solution.py:15
  31.3 9.0 %collective-permute-done.4.refs_4_ = bf16[2,128,1024]{2,1,0:T(8,128)(2,1)S(1)} collective-permute-done((bf16[2,128,1024]{2,1,0:T(8,128)(2,1)S(1)}, bf16[2,128,1024]{2,1,0:T(8,128)(2,1)S(1)}, u32[]{:S(2)}, u32[]{:S(2)}) %collective-permute-start.4) | collective-permute-done | bytes 524320 | tf_op jit(solution)/shard_map/ppermute | solution.py:15
  41.2 10.8 %collective-permute-done.5.refs_5_ = bf16[2,128,1024]{2,1,0:T(8,128)(2,1)S(1)} collective-permute-done((bf16[2,128,1024]{2,1,0:T(8,128)(2,1)S(1)}, bf16[2,128,1024]{2,1,0:T(8,128)(2,1)S(1)}, u32[]{:S(2)}, u32[]{:S(2)}) %collective-permute-start.5) | collective-permute-done | bytes 524320 | tf_op jit(solution)/shard_map/ppermute | solution.py:15
  52.0 11.4 %collective-permute-start.11 = (bf16[2,2,64,1024]{3,2,1,0:T(8,128)(2,1)S(1)}, bf16[2,2,64,1024]{3,2,1,0:T(8,128)(2,1)S(1)}, u32[]{:S(2)}, u32[]{:S(2)}) collective-permute-start(bf16[2,2,64,1024]{3,2,1,0:T(8,128)(2,1)S(1)} %pad_maximum_fusion), channel_id=1, source_target_pairs={{0,2},{1,3},{2,0},{3,1},{4,6},{5,7},{6,4},{7,5},{8,10},{9,11},{10,... | collective-permute-start | bytes 1572872 | tf_op jit(solution)/shard_map/ppermute | solution.py:15
  63.5 3.5 %shard_map.52 = (bf16[2,64,1024]{2,1,0:T(8,128)(2,1)S(1)}, bf16[2,64,512]{2,1,0:T(8,128)(2,1)S(1)}, f32[2,64,512]{2,1,0:T(8,128)S(1)}, bf16[2,512,512]{2,1,0:T(8...) custom-call(bf16[2,128,1024]{2,1,0:T(8,128)(2,1)S(1)} %get-tuple-element.28.refs_0_, ...), custom_call_target="tpu_custom_call" | custom-call | flops 2000000000 | bytes 4194304 | tf_op jit(solution)/shard_map/pallas_call | solution.py:63
  67.0 19.5 %collective-permute-done.11.refs_0_ = bf16[2,2,64,1024]{3,2,1,0:T(8,128)(2,1)S(1)} collective-permute-done((bf16[2,2,64,1024]{3,2,1,0:T(8,128)(2,1)S(1)}, bf16[2,2,64,1024]{3,2,1,0:T(8,128)(2,1)S(1)}, u32[]{:S(2)}, u32[]{:S(2)}) %collective-permute-start.11) | collective-permute-done | bytes 524320 | tf_op jit(solution)/shard_map/ppermute | solution.py:15
  86.6 2.0 %shard_map.53 = (bf16[2,64,1024]{2,1,0:T(8,128)(2,1)S(1)}, bf16[2,128,512]{2,1,0:T(8,128)(2,1)S(1)}, f32[2,128,512]{2,1,0:T(8,128)S(1)}) custom-call(bf16[2,2,64,1024]{3,2,1,0:T(8,128)(2,1)S(1)} %collective-permute-done.11.refs_0_, bf16[2,512,512]{2,1,0:T(8,128)(2,1)S(1)} %get-tuple-element.34.refs_1_, bf16[2,512,512]{2,1,0:T(8,128)(2,1)S(1)} %get-tuple-element.35.refs_2_, ...), custom_call_target="tpu_custom_call" | custom-call | flops 1400000000 | bytes 4194304 | tf_op jit(solution)/shard_map/pallas_call | solution.py:63
  89.1 3.2 %collective-permute-start.13 = (bf16[2,64,1024]{2,1,0:T(8,128)(2,1)S(1)}, bf16[2,64,1024]{2,1,0:T(8,128)(2,1)S(1)}, u32[]{:S(2)}, u32[]{:S(2)}) collective-permute-start(bf16[2,64,1024]{2,1,0:T(8,128)(2,1)S(1)} %get-tuple-element.39.refs_4_), channel_id=1, source_target_pairs={{0,8},{4,12},{8,0},{12,4},{16,24},{20,28},{24,16},{28,20},{32,40},... | collective-permute-start | bytes 786440 | tf_op jit(solution)/shard_map/ppermute | solution.py:15
  95.0 2.9 %collective-permute-start.9 = (bf16[2,64,1024]{2,1,0:T(8,128)(2,1)S(1)}, bf16[2,64,1024]{2,1,0:T(8,128)(2,1)S(1)}, u32[]{:S(2)}, u32[]{:S(2)}) collective-permute-start(bf16[2,64,1024]{2,1,0:T(8,128)(2,1)S(1)} %get-tuple-element.33.refs_0_), channel_id=1, source_target_pairs={{0,8},{4,12},{8,0},{12,4},{16,24},{20,28},{24,16},{28,20},{32,40},... | collective-permute-start | bytes 786440 | tf_op jit(solution)/shard_map/ppermute | solution.py:15
  97.9 2.9 %collective-permute-done.13.refs_6_ = bf16[2,64,1024]{2,1,0:T(8,128)(2,1)S(1)} collective-permute-done((bf16[2,64,1024]{2,1,0:T(8,128)(2,1)S(1)}, bf16[2,64,1024]{2,1,0:T(8,128)(2,1)S(1)}, u32[]{:S(2)}, u32[]{:S(2)}) %collective-permute-start.13) | collective-permute-done | bytes 262176 | tf_op jit(solution)/shard_map/ppermute | solution.py:15
  101.9 1.9 %collective-permute-done.14.refs_7_ = bf16[2,64,1024]{2,1,0:T(8,128)(2,1)S(1)} collective-permute-done((bf16[2,64,1024]{2,1,0:T(8,128)(2,1)S(1)}, bf16[2,64,1024]{2,1,0:T(8,128)(2,1)S(1)}, u32[]{:S(2)}, u32[]{:S(2)}) %collective-permute-start.14) | collective-permute-done | bytes 262176 | tf_op jit(solution)/shard_map/ppermute | solution.py:15
  104.8 6.0 %collective-permute-done.9.refs_2_ = bf16[2,64,1024]{2,1,0:T(8,128)(2,1)S(1)} collective-permute-done((bf16[2,64,1024]{2,1,0:T(8,128)(2,1)S(1)}, bf16[2,64,1024]{2,1,0:T(8,128)(2,1)S(1)}, u32[]{:S(2)}, u32[]{:S(2)}) %collective-permute-start.9) | collective-permute-done | bytes 262176 | tf_op jit(solution)/shard_map/ppermute | solution.py:15
  110.8 2.7 %collective-permute-done.10.refs_3_ = bf16[2,64,1024]{2,1,0:T(8,128)(2,1)S(1)} collective-permute-done((bf16[2,64,1024]{2,1,0:T(8,128)(2,1)S(1)}, bf16[2,64,1024]{2,1,0:T(8,128)(2,1)S(1)}, u32[]{:S(2)}, u32[]{:S(2)}) %collective-permute-start.10) | collective-permute-done | bytes 262176 | tf_op jit(solution)/shard_map/ppermute | solution.py:15
  115.8 4.4 %shard_map.54 = (f32[2,64,1024]{2,1,0:T(8,128)S(1)}, bf16[2,64,1024]{2,1,0:T(8,128)(2,1)S(1)}, f32[1,128]{1,0:T(1,128)S(1)}, f32[1,128]{1,0:T(1,128)S(1)}) custom-call(bf16[2,64,1024]{2,1,0:T(8,128)(2,1)S(1)} %get-tuple-element.33.refs_0_, bf16[2,64,1024]{2,1,0:T(8,128)(2,1)S(1)} %collective-permute-done.8.refs_1_, ...), custom_call_target="tpu_custom_call" | custom-call | flops 1400000000 | bytes 4194304 | tf_op jit(solution)/shard_map/pallas_call | solution.py:63
  120.2 6.4 %collective-permute-start.23 = (bf16[2,64,1024]{2,1,0:T(8,128)(2,1)S(1)}, bf16[2,64,1024]{2,1,0:T(8,128)(2,1)S(1)}, u32[]{:S(2)}, u32[]{:S(2)}) collective-permute-start(bf16[2,64,1024]{2,1,0:T(8,128)(2,1)S(1)} %get-tuple-element.43), channel_id=1, source_target_pairs={{0,2},{1,3},{2,0},{3,1},{4,6},{5,7},{6,4},{7,5},{8,10},{9,11},{10,... | collective-permute-start | bytes 786440 | tf_op jit(solution)/shard_map/ppermute | solution.py:15
  126.7 11.4 %collective-permute-done.24 = f32[1,128]{1,0:T(1,128)S(1)} collective-permute-done((f32[1,128]{1,0:T(1,128)S(1)}, f32[1,128]{1,0:T(1,128)S(1)}, u32[]{:S(2)}, u32[]{:S(2)}) %collective-permute-start.24) | collective-permute-done | bytes 544 | tf_op jit(solution)/shard_map/ppermute | solution.py:15
  138.1 2.8 %collective-permute-start.25 = (f32[1,128]{1,0:T(1,128)S(1)}, f32[1,128]{1,0:T(1,128)S(1)}, u32[]{:S(2)}, u32[]{:S(2)}) collective-permute-start(f32[1,128]{1,0:T(1,128)S(1)} %add.13), channel_id=1, source_target_pairs={{0,64},{64,0},{128,192},{192,128},{1,65},{65,1},{129,193},{193,129... | collective-permute-start | bytes 1544 | tf_op jit(solution)/shard_map/ppermute | solution.py:15
  142.5 2.5 %collective-permute-start.26 = (f32[1,128]{1,0:T(1,128)S(1)}, f32[1,128]{1,0:T(1,128)S(1)}, u32[]{:S(2)}, u32[]{:S(2)}) collective-permute-start(f32[1,128]{1,0:T(1,128)S(1)} %add.14), channel_id=1, source_target_pairs={{0,128},{64,192},{128,0},{192,64},{1,129},{65,193},{129,1},{193,65... | collective-permute-start | bytes 1544 | tf_op jit(solution)/shard_map/ppermute | solution.py:15
  145.0 2.0 %collective-permute-done.26 = f32[1,128]{1,0:T(1,128)S(1)} collective-permute-done((f32[1,128]{1,0:T(1,128)S(1)}, f32[1,128]{1,0:T(1,128)S(1)}, u32[]{:S(2)}, u32[]{:S(2)}) %collective-permute-start.26) | collective-permute-done | bytes 544 | tf_op jit(solution)/shard_map/ppermute | solution.py:15
  147.8 1.8 %copy.5 = f32[1,64,2,2,1024]{4,3,2,1,0:T(2,128)} copy(f32[1,64,2,2,1024]{4,1,3,2,0:T(8,128)S(1)} %maximum_bitcast_fusion) | data formatting | bytes 2097152
  (53 shorter events, 16.0 us)
Async XLA Ops:
  4.4 14.0 %collective-permute-start = (bf16[2,2,64,1024]{3,2,1,0:T(8,128)(2,1)}, bf16[2,2,64,1024]{3,2,1,0:T(8,128)(2,1)S(1)}, u32[]{:S(2)}, u32[]{:S(2)}) collective-permute-start(bf16[2,2,64,1024]{3,2,1,0:T(8,128)(2,1)} %get-tuple-element.27), channel_id=1, source_target_pairs={{0,4},{4,0},{8,12},{12,8},{16,20},{20,16},{24,28},{28,24},{32,36},... | collective-permute-start | bytes 1572872 | tf_op jit(solution)/shard_map/ppermute | solution.py:15
  18.4 12.8 %collective-permute-start.1 = (bf16[2,128,1024]{2,1,0:T(8,128)(2,1)S(1)}, bf16[2,128,1024]{2,1,0:T(8,128)(2,1)S(1)}, u32[]{:S(2)}, u32[]{:S(2)}) collective-permute-start(bf16[2,128,1024]{2,1,0:T(8,128)(2,1)S(1)} %get-tuple-element.28.refs_0_), channel_id=1, source_target_pairs={{0,4},{4,0},{8,12},{12,8},{16,20},{20,16},{24,28},{28,24},{32,36},... | collective-permute-start | bytes 1572872 | tf_op jit(solution)/shard_map/ppermute | solution.py:15
  20.0 20.2 %collective-permute-start.4 = (bf16[2,128,1024]{2,1,0:T(8,128)(2,1)S(1)}, bf16[2,128,1024]{2,1,0:T(8,128)(2,1)S(1)}, u32[]{:S(2)}, u32[]{:S(2)}) collective-permute-start(bf16[2,128,1024]{2,1,0:T(8,128)(2,1)S(1)} %copy-done.2), channel_id=1, source_target_pairs={{0,2},{1,3},{2,0},{3,1},{4,6},{5,7},{6,4},{7,5},{8,10},{9,11},{10,... | collective-permute-start | bytes 1572872 | tf_op jit(solution)/shard_map/ppermute | solution.py:15
  40.2 11.8 %collective-permute-start.5 = (bf16[2,128,1024]{2,1,0:T(8,128)(2,1)S(1)}, bf16[2,128,1024]{2,1,0:T(8,128)(2,1)S(1)}, u32[]{:S(2)}, u32[]{:S(2)}) collective-permute-start(bf16[2,128,1024]{2,1,0:T(8,128)(2,1)S(1)} %collective-permute-done.4.refs_4_), channel_id=1, source_target_pairs={{0,4},{4,0},{8,12},{12,8},{16,20},{20,16},{24,28},{28,24},{32,36},... | collective-permute-start | bytes 1572872 | tf_op jit(solution)/shard_map/ppermute | solution.py:15
  40.7 22.8 %collective-permute-start.2 = (bf16[2,128,1024]{2,1,0:T(8,128)(2,1)S(1)}, bf16[2,128,1024]{2,1,0:T(8,128)(2,1)S(1)}, u32[]{:S(2)}, u32[]{:S(2)}) collective-permute-start(bf16[2,128,1024]{2,1,0:T(8,128)(2,1)S(1)} %get-tuple-element.28.refs_0_), channel_id=1, source_target_pairs={{0,1},{1,0},{2,3},{3,2},{4,5},{5,4},{6,7},{7,6},{8,9},{9,8},{10,11... | collective-permute-start | bytes 1572872 | tf_op jit(solution)/shard_map/ppermute | solution.py:15
  40.7 22.8 %collective-permute-start.6 = (bf16[2,128,1024]{2,1,0:T(8,128)(2,1)S(1)}, bf16[2,128,1024]{2,1,0:T(8,128)(2,1)S(1)}, u32[]{:S(2)}, u32[]{:S(2)}) collective-permute-start(bf16[2,128,1024]{2,1,0:T(8,128)(2,1)S(1)} %collective-permute-done.4.refs_4_), channel_id=1, source_target_pairs={{0,1},{1,0},{2,3},{3,2},{4,5},{5,4},{6,7},{7,6},{8,9},{9,8},{10,11... | collective-permute-start | bytes 1572872 | tf_op jit(solution)/shard_map/ppermute | solution.py:15
  41.2 22.3 %collective-permute-start.3 = (bf16[2,128,1024]{2,1,0:T(8,128)(2,1)S(1)}, bf16[2,128,1024]{2,1,0:T(8,128)(2,1)S(1)}, u32[]{:S(2)}, u32[]{:S(2)}) collective-permute-start(bf16[2,128,1024]{2,1,0:T(8,128)(2,1)S(1)} %collective-permute-done.1.refs_1_), channel_id=1, source_target_pairs={{0,1},{1,0},{2,3},{3,2},{4,5},{5,4},{6,7},{7,6},{8,9},{9,8},{10,11... | collective-permute-start | bytes 1572872 | tf_op jit(solution)/shard_map/ppermute | solution.py:15
  52.0 11.4 %collective-permute-start.7 = (bf16[2,128,1024]{2,1,0:T(8,128)(2,1)S(1)}, bf16[2,128,1024]{2,1,0:T(8,128)(2,1)S(1)}, u32[]{:S(2)}, u32[]{:S(2)}) collective-permute-start(bf16[2,128,1024]{2,1,0:T(8,128)(2,1)S(1)} %collective-permute-done.5.refs_5_), channel_id=1, source_target_pairs={{0,1},{1,0},{2,3},{3,2},{4,5},{5,4},{6,7},{7,6},{8,9},{9,8},{10,11... | collective-permute-start | bytes 1572872 | tf_op jit(solution)/shard_map/ppermute | solution.py:15
  52.0 34.5 %collective-permute-start.11 = (bf16[2,2,64,1024]{3,2,1,0:T(8,128)(2,1)S(1)}, bf16[2,2,64,1024]{3,2,1,0:T(8,128)(2,1)S(1)}, u32[]{:S(2)}, u32[]{:S(2)}) collective-permute-start(bf16[2,2,64,1024]{3,2,1,0:T(8,128)(2,1)S(1)} %pad_maximum_fusion), channel_id=1, source_target_pairs={{0,2},{1,3},{2,0},{3,1},{4,6},{5,7},{6,4},{7,5},{8,10},{9,11},{10,... | collective-permute-start | bytes 1572872 | tf_op jit(solution)/shard_map/ppermute | solution.py:15
  88.5 6.5 %collective-permute-start.12 = (bf16[2,64,1024]{2,1,0:T(8,128)(2,1)S(1)}, bf16[2,64,1024]{2,1,0:T(8,128)(2,1)S(1)}, u32[]{:S(2)}, u32[]{:S(2)}) collective-permute-start(bf16[2,64,1024]{2,1,0:T(8,128)(2,1)S(1)} %get-tuple-element.39.refs_4_), channel_id=1, source_target_pairs={{0,4},{4,0},{8,12},{12,8},{16,20},{20,16},{24,28},{28,24},{32,36},... | collective-permute-start | bytes 786440 | tf_op jit(solution)/shard_map/ppermute | solution.py:15
  89.1 11.7 %collective-permute-start.13 = (bf16[2,64,1024]{2,1,0:T(8,128)(2,1)S(1)}, bf16[2,64,1024]{2,1,0:T(8,128)(2,1)S(1)}, u32[]{:S(2)}, u32[]{:S(2)}) collective-permute-start(bf16[2,64,1024]{2,1,0:T(8,128)(2,1)S(1)} %get-tuple-element.39.refs_4_), channel_id=1, source_target_pairs={{0,8},{4,12},{8,0},{12,4},{16,24},{20,28},{24,16},{28,20},{32,40},... | collective-permute-start | bytes 786440 | tf_op jit(solution)/shard_map/ppermute | solution.py:15
  92.3 11.5 %collective-permute-start.14 = (bf16[2,64,1024]{2,1,0:T(8,128)(2,1)S(1)}, bf16[2,64,1024]{2,1,0:T(8,128)(2,1)S(1)}, u32[]{:S(2)}, u32[]{:S(2)}) collective-permute-start(bf16[2,64,1024]{2,1,0:T(8,128)(2,1)S(1)} %get-tuple-element.39.refs_4_), channel_id=1, source_target_pairs={{0,12},{4,8},{8,4},{12,0},{16,28},{20,24},{24,20},{28,16},{32,44},... | collective-permute-start | bytes 786440 | tf_op jit(solution)/shard_map/ppermute | solution.py:15
  93.3 10.4 %collective-permute-start.19 = (bf16[2,64,1024]{2,1,0:T(8,128)(2,1)S(1)}, bf16[2,64,1024]{2,1,0:T(8,128)(2,1)S(1)}, u32[]{:S(2)}, u32[]{:S(2)}) collective-permute-start(bf16[2,64,1024]{2,1,0:T(8,128)(2,1)S(1)} %get-tuple-element.39.refs_4_), channel_id=1, source_target_pairs={{0,1},{1,0},{2,3},{3,2},{4,5},{5,4},{6,7},{7,6},{8,9},{9,8},{10,11... | collective-permute-start | bytes 786440 | tf_op jit(solution)/shard_map/ppermute | solution.py:15
  93.3 11.5 %collective-permute-start.8 = (bf16[2,64,1024]{2,1,0:T(8,128)(2,1)S(1)}, bf16[2,64,1024]{2,1,0:T(8,128)(2,1)S(1)}, u32[]{:S(2)}, u32[]{:S(2)}) collective-permute-start(bf16[2,64,1024]{2,1,0:T(8,128)(2,1)S(1)} %get-tuple-element.33.refs_0_), channel_id=1, source_target_pairs={{0,4},{4,0},{8,12},{12,8},{16,20},{20,16},{24,28},{28,24},{32,36},... | collective-permute-start | bytes 786440 | tf_op jit(solution)/shard_map/ppermute | solution.py:15
  95.0 15.8 %collective-permute-start.9 = (bf16[2,64,1024]{2,1,0:T(8,128)(2,1)S(1)}, bf16[2,64,1024]{2,1,0:T(8,128)(2,1)S(1)}, u32[]{:S(2)}, u32[]{:S(2)}) collective-permute-start(bf16[2,64,1024]{2,1,0:T(8,128)(2,1)S(1)} %get-tuple-element.33.refs_0_), channel_id=1, source_target_pairs={{0,8},{4,12},{8,0},{12,4},{16,24},{20,28},{24,16},{28,20},{32,40},... | collective-permute-start | bytes 786440 | tf_op jit(solution)/shard_map/ppermute | solution.py:15
  100.8 12.7 %collective-permute-start.10 = (bf16[2,64,1024]{2,1,0:T(8,128)(2,1)S(1)}, bf16[2,64,1024]{2,1,0:T(8,128)(2,1)S(1)}, u32[]{:S(2)}, u32[]{:S(2)}) collective-permute-start(bf16[2,64,1024]{2,1,0:T(8,128)(2,1)S(1)} %get-tuple-element.33.refs_0_), channel_id=1, source_target_pairs={{0,12},{4,8},{8,4},{12,0},{16,28},{20,24},{24,20},{28,16},{32,44},... | collective-permute-start | bytes 786440 | tf_op jit(solution)/shard_map/ppermute | solution.py:15
  103.7 9.7 %collective-permute-start.15 = (bf16[2,64,1024]{2,1,0:T(8,128)(2,1)S(1)}, bf16[2,64,1024]{2,1,0:T(8,128)(2,1)S(1)}, u32[]{:S(2)}, u32[]{:S(2)}) collective-permute-start(bf16[2,64,1024]{2,1,0:T(8,128)(2,1)S(1)} %get-tuple-element.33.refs_0_), channel_id=1, source_target_pairs={{0,1},{1,0},{2,3},{3,2},{4,5},{5,4},{6,7},{7,6},{8,9},{9,8},{10,11... | collective-permute-start | bytes 786440 | tf_op jit(solution)/shard_map/ppermute | solution.py:15
  103.7 10.3 %collective-permute-start.20 = (bf16[2,64,1024]{2,1,0:T(8,128)(2,1)S(1)}, bf16[2,64,1024]{2,1,0:T(8,128)(2,1)S(1)}, u32[]{:S(2)}, u32[]{:S(2)}) collective-permute-start(bf16[2,64,1024]{2,1,0:T(8,128)(2,1)S(1)} %collective-permute-done.12.refs_5_), channel_id=1, source_target_pairs={{0,1},{1,0},{2,3},{3,2},{4,5},{5,4},{6,7},{7,6},{8,9},{9,8},{10,11... | collective-permute-start | bytes 786440 | tf_op jit(solution)/shard_map/ppermute | solution.py:15
  104.8 9.6 %collective-permute-start.21 = (bf16[2,64,1024]{2,1,0:T(8,128)(2,1)S(1)}, bf16[2,64,1024]{2,1,0:T(8,128)(2,1)S(1)}, u32[]{:S(2)}, u32[]{:S(2)}) collective-permute-start(bf16[2,64,1024]{2,1,0:T(8,128)(2,1)S(1)} %collective-permute-done.13.refs_6_), channel_id=1, source_target_pairs={{0,1},{1,0},{2,3},{3,2},{4,5},{5,4},{6,7},{7,6},{8,9},{9,8},{10,11... | collective-permute-start | bytes 786440 | tf_op jit(solution)/shard_map/ppermute | solution.py:15
  110.8 3.6 %collective-permute-start.22 = (bf16[2,64,1024]{2,1,0:T(8,128)(2,1)S(1)}, bf16[2,64,1024]{2,1,0:T(8,128)(2,1)S(1)}, u32[]{:S(2)}, u32[]{:S(2)}) collective-permute-start(bf16[2,64,1024]{2,1,0:T(8,128)(2,1)S(1)} %collective-permute-done.14.refs_7_), channel_id=1, source_target_pairs={{0,1},{1,0},{2,3},{3,2},{4,5},{5,4},{6,7},{7,6},{8,9},{9,8},{10,11... | collective-permute-start | bytes 786440 | tf_op jit(solution)/shard_map/ppermute | solution.py:15
  120.2 27.4 %collective-permute-start.23 = (bf16[2,64,1024]{2,1,0:T(8,128)(2,1)S(1)}, bf16[2,64,1024]{2,1,0:T(8,128)(2,1)S(1)}, u32[]{:S(2)}, u32[]{:S(2)}) collective-permute-start(bf16[2,64,1024]{2,1,0:T(8,128)(2,1)S(1)} %get-tuple-element.43), channel_id=1, source_target_pairs={{0,2},{1,3},{2,0},{3,1},{4,6},{5,7},{6,4},{7,5},{8,10},{9,11},{10,... | collective-permute-start | bytes 786440 | tf_op jit(solution)/shard_map/ppermute | solution.py:15
  126.6 11.5 %collective-permute-start.24 = (f32[1,128]{1,0:T(1,128)S(1)}, f32[1,128]{1,0:T(1,128)S(1)}, u32[]{:S(2)}, u32[]{:S(2)}) collective-permute-start(f32[1,128]{1,0:T(1,128)S(1)} %get-tuple-element.45), channel_id=1, source_target_pairs={{0,2},{1,3},{2,0},{3,1},{4,6},{5,7},{6,4},{7,5},{8,10},{9,11},{10,... | collective-permute-start | bytes 1544 | tf_op jit(solution)/shard_map/ppermute | solution.py:15
  138.1 4.4 %collective-permute-start.25 = (f32[1,128]{1,0:T(1,128)S(1)}, f32[1,128]{1,0:T(1,128)S(1)}, u32[]{:S(2)}, u32[]{:S(2)}) collective-permute-start(f32[1,128]{1,0:T(1,128)S(1)} %add.13), channel_id=1, source_target_pairs={{0,64},{64,0},{128,192},{192,128},{1,65},{65,1},{129,193},{193,129... | collective-permute-start | bytes 1544 | tf_op jit(solution)/shard_map/ppermute | solution.py:15
  142.5 4.5 %collective-permute-start.26 = (f32[1,128]{1,0:T(1,128)S(1)}, f32[1,128]{1,0:T(1,128)S(1)}, u32[]{:S(2)}, u32[]{:S(2)}) collective-permute-start(f32[1,128]{1,0:T(1,128)S(1)} %add.14), channel_id=1, source_target_pairs={{0,128},{64,192},{128,0},{192,64},{1,129},{65,193},{129,1},{193,65... | collective-permute-start | bytes 1544 | tf_op jit(solution)/shard_map/ppermute | solution.py:15
  (7 other events, 52.3 us)

commit v3 on v1

v3 whole, which is shorter than its diff:
```python
import jax
import jax.numpy as jnp
from jax import lax
from jax.experimental import pallas as pl
from jax.experimental.pallas import tpu as pltpu
from jax.sharding import PartitionSpec as P


F32 = jnp.float32
BF16 = jnp.bfloat16
LANES = 128


def exchange(x, axis, distance):
    return lax.ppermute(x, axis, [(i, i ^ distance) for i in range(lax.axis_size(axis))])


def dot(x, y):
    return jnp.dot(x, y, preferred_element_type=F32)


def stacked(x):
    return x.reshape(2 * x.shape[1], x.shape[2])


def product(x, y_real, y_imag):
    rows = x.shape[0] // 2
    by_real, by_imag = dot(x, y_real), dot(x, y_imag)
    return by_real[:rows] - by_imag[rows:], by_imag[:rows] + by_real[rows:]


def halved(pair):
    return jnp.concatenate([pair[0].astype(BF16), pair[1].astype(BF16)], axis=0)


def at(start, size):
    return pl.ds(pl.multiple_of(start, size), size)


class Copies:
    def __init__(self, sems):
        self.sems = sems
        self.made = []

    def start(self, source, target):
        copy = pltpu.make_async_copy(source, target, self.sems.at[len(self.made)])
        copy.start()
        self.made.append(copy)
        return copy


def wait(copies):
    for copy in copies:
        copy.wait()


def call(body, out_shape, scratch, copies, flops, *args, in_vmem=(), in_smem=(), grant=40):
    spaces = [pltpu.HBM] * len(args)
    for i in in_vmem:
        spaces[i] = pltpu.VMEM
    for i in in_smem:
        spaces[i] = pltpu.SMEM
    return pl.pallas_call(
        body,
        out_shape=out_shape,
        in_specs=[pl.BlockSpec(memory_space=space) for space in spaces],
        out_specs=[pl.BlockSpec(memory_space=pltpu.VMEM)] * len(out_shape),
        scratch_shapes=scratch + [pltpu.SemaphoreType.DMA((copies,))],
        compiler_params=pltpu.CompilerParams(vmem_limit_bytes=grant << 20),
        cost_estimate=pl.CostEstimate(flops=flops, bytes_accessed=4 << 20, transcendentals=0),
    )(*args)


def places():
    cluster = lax.axis_index("cluster")
    tile = lax.axis_index("tile")
    return cluster % 2, tile // 2, tile % 2, cluster // 2 % 2


def fill_selector(column_ref, selector):
    size = selector.shape[0]
    source = lax.broadcasted_iota(jnp.int32, (size, size), 0)
    selector[...] = jnp.where(source == column_ref[...], 1.0, 0.0).astype(BF16)


def reorder(stage, selector, parted):
    count, _, nodes = stage.shape
    flat = stage[...].reshape(2 * count, nodes)
    wide = 2 * LANES
    for first in range(0, nodes, wide):
        ordered = dot(flat, selector[:, first : first + wide])
        for turn in range(2):
            parted[first // LANES + turn] = ordered[:, turn * LANES : (turn + 1) * LANES]


def lane_block(parted, block, part, first, count):
    return parted[block, pl.ds(2 * first + part, count, stride=2), :].astype(BF16)


def order_first(
    column_ref, raw, send_out, inner_out, cross_out,
    column, send_stage, own_stage, selector, send_parted, own_parted, sems,
):
    side, _, _, _ = places()
    copies = Copies(sems)
    first = copies.start(column_ref, column)
    sent = copies.start(raw.at[0, 0, :, 1 - side], send_stage)
    owned = copies.start(raw.at[0, 0, :, side], own_stage)
    first.wait()
    fill_selector(column, selector)
    sent.wait()
    reorder(send_stage, selector, send_parted)
    owned.wait()
    reorder(own_stage, selector, own_parted)
    blocks = send_parted.shape[0]
    count = send_stage.shape[0]
    for block in range(blocks):
        lanes = slice(block * LANES, (block + 1) * LANES)
        out = (inner_out, cross_out)[2 * block // blocks]
        column_at = block % (blocks // 2) * LANES
        for part in range(2):
            send_out[part, :, lanes] = lane_block(send_parted, block, part, 0, count)
            out[part, :, column_at : column_at + LANES] = lane_block(
                own_parted, block, part, 0, count
            )


def order_second(
    column_ref, raw, send_out, keep_out,
    column, send_stage, own_stage, selector, send_parted, own_parted, sems,
):
    side, _, _, _ = places()
    copies = Copies(sems)
    first = copies.start(column_ref, column)
    sent = copies.start(raw.at[0, 1, :, 1 - side], send_stage)
    owned = copies.start(raw.at[0, 1, :, side], own_stage)
    first.wait()
    fill_selector(column, selector)
    sent.wait()
    reorder(send_stage, selector, send_parted)
    owned.wait()
    reorder(own_stage, selector, own_parted)
    count = send_stage.shape[0]
    for block in range(send_parted.shape[0]):
        lanes = slice(block * LANES, (block + 1) * LANES)
        for part in range(2):
            send_out[part, :, lanes] = lane_block(send_parted, block, part, 0, count)
            keep_out[part, :, lanes] = lane_block(own_parted, block, part, 0, count)


def guess(interior, approx):
    size = interior.shape[1]
    real = interior[0].astype(F32)
    imag = interior[1].astype(F32)

    def on_diagonal(count):
        return lax.broadcasted_iota(jnp.int32, (count, count), 0) == lax.broadcasted_iota(
            jnp.int32, (count, count), 1
        )

    block_diag = on_diagonal(LANES)

    def diagonal(values, axis):
        found = []
        for first in range(0, size, LANES):
            span = slice(first, first + LANES)
            block = jnp.where(block_diag, values[span, span], 0.0)
            found.append(jnp.sum(block, axis=axis, keepdims=True))
        return jnp.concatenate(found, axis=1 - axis)

    def reciprocal(axis):
        diag_real = diagonal(real, axis)
        diag_imag = diagonal(imag, axis)
        denom = diag_real * diag_real + diag_imag * diag_imag
        return diag_real / denom, -diag_imag / denom

    col_real, col_imag = reciprocal(0)
    row_real, row_imag = reciprocal(1)
    temp_real = real * col_real - imag * col_imag
    temp_imag = real * col_imag + imag * col_real
    prod_real = row_real * temp_real - row_imag * temp_imag
    prod_imag = row_real * temp_imag + row_imag * temp_real
    on_diag = on_diagonal(size)
    approx[0] = (jnp.where(on_diag, 2.0 * row_real, 0.0) - prod_real).astype(BF16)
    approx[1] = (jnp.where(on_diag, 2.0 * row_imag, 0.0) - prod_imag).astype(BF16)


def eliminate(left, interior, approx):
    applied = product(left, approx[0], approx[1])
    middle = halved(product(halved(applied), interior[0], interior[1]))
    second = product(middle, approx[0], approx[1])
    return halved((2.0 * applied[0] - second[0], 2.0 * applied[1] - second[1]))


def spread(copies, pieces, columns, target):
    _, depth, core, _ = places()
    rows = pieces[0].shape[1]
    made = []
    for who, piece in enumerate(pieces):
        row = at(((depth ^ (who % 2)) * 2 + (core ^ (who // 2))) * rows, rows)
        made.append(copies.start(piece.at[:, :, columns], target.at[:, row]))
    return made


def first_level(*refs):
    owns, mixed = refs[0:4], refs[4:8]
    keep, got = refs[8:10]
    inner_out, cross_out, left_out, corner_out = refs[10:14]
    interior, approx, right, left, start, sems = refs[14:]
    side, _, _, _ = places()
    copies = Copies(sems)
    width = interior.shape[1]
    rows = keep.shape[1]
    lows, highs = pl.ds(0, width), pl.ds(width, width)
    from_inner = spread(copies, mixed, lows, interior)
    from_outer = [
        copies.start(keep.at[:, :, lows], left.at[side]),
        copies.start(got.at[:, :, lows], left.at[1 - side]),
    ]
    from_cross = spread(copies, owns, lows, right.at[side])
    from_cross += spread(copies, mixed, highs, right.at[1 - side])
    from_cross += [
        copies.start(keep.at[:, :, highs], start.at[side]),
        copies.start(got.at[:, :, highs], start.at[1 - side]),
    ]
    wait(from_inner)
    guess(interior, approx)
    wait(from_outer)
    both = jnp.concatenate([left[0, 0], left[1, 0], left[0, 1], left[1, 1]], axis=0)
    reduced = eliminate(both, interior, approx)
    wait(from_cross)
    low_taken = product(reduced, right[0, 0], right[0, 1])
    high_taken = product(reduced, right[1, 0], right[1, 1])
    for part in range(2):
        inner_out[part] = (start[0, part].astype(F32) - low_taken[part][:rows]).astype(BF16)
        cross_out[part] = (-high_taken[part][:rows]).astype(BF16)
        left_out[part] = (-low_taken[part][rows:]).astype(BF16)
        corner_out[part] = start[1, part].astype(F32) - high_taken[part][rows:]


def last_level(*refs):
    sums, owns, others = refs[0:4], refs[4:8], refs[8:12]
    left, corner, weights = refs[12:15]
    keep_out, send_out, diag_out = refs[15:18]
    interior, approx, right, total, sems = refs[18:]
    side, depth, core, pair = places()
    copies = Copies(sems)
    width = interior.shape[1]
    rows = corner.shape[1]
    few = rows // 2
    every = pl.ds(0, width)
    from_inner = spread(copies, sums, every, interior)
    from_cross = spread(copies, owns, every, right.at[pair])
    from_cross += spread(copies, others, every, right.at[1 - pair])
    wait(from_inner)
    guess(interior, approx)
    reduced = eliminate(stacked(left[...]), interior, approx)
    wait(from_cross)
    for owner in range(2):
        taken = product(reduced, right[owner, 0], right[owner, 1])
        for part in range(2):
            start = jnp.where(pair == owner, corner[part], 0.0)
            total[part, :, owner * width : (owner + 1) * width] = start - taken[part]
    block = total[1, :, at(pair * width + (depth * 2 + core) * LANES, LANES)]
    row_of = lax.broadcasted_iota(jnp.int32, (rows, LANES), 0)
    lane_of = lax.broadcasted_iota(jnp.int32, (rows, LANES), 1)
    found = jnp.sum(jnp.where(row_of == lane_of, block, 0.0), axis=0, keepdims=True)
    diag_out[...] = found * weights[side]
    keep_rows, send_rows = at(side * few, few), at((1 - side) * few, few)
    for part in range(2):
        send_out[part] = total[part, send_rows, :].astype(BF16)
        keep_out[part] = total[part, keep_rows, :]


def after(x, *others):
    return lax.optimization_barrier((x,) + others)[0]


def compute(boundary, column_source, energy_weights):
    _, _, rows, _, _, nodes = boundary.shape
    half = nodes // 2
    few = rows // 2
    side = lax.axis_index("cluster") % 2

    def bf16(*shape):
        return jax.ShapeDtypeStruct(shape, BF16)

    def f32(*shape):
        return jax.ShapeDtypeStruct(shape, F32)

    def total_of(x, y):
        return (x.astype(F32) + y.astype(F32)).astype(BF16)

    selector = pltpu.VMEM((nodes, nodes), BF16)
    column = pltpu.VMEM((1, nodes), jnp.int32)
    stage = pltpu.VMEM((rows, 2, nodes), BF16)
    parted = pltpu.VMEM((nodes // LANES, 2 * rows, LANES), F32)
    ordering = [column, stage, stage, selector, parted, parted]
    first, own_inner, own = call(
        order_first,
        [bf16(2, rows, nodes), bf16(2, rows, half), bf16(2, rows, half)],
        ordering,
        3,
        int(2e9),
        column_source,
        boundary,
        grant=62,
    )
    got = exchange(first, "cluster", 1)
    own_far = exchange(own, "tile", 2)
    outer, keep = call(
        order_second,
        [bf16(2, rows, nodes), bf16(2, rows, nodes)],
        ordering,
        3,
        int(2e9),
        after(column_source, own),
        boundary,
    )
    outer_got = exchange(after(outer, got), "cluster", 1)
    mixed = jnp.concatenate([total_of(own_inner, got[..., :half]), got[..., half:]], axis=2)
    mixed_far = exchange(mixed, "tile", 2)
    owns = [own, own_far]
    owns += [exchange(own, "tile", 1), exchange(own_far, "tile", 1)]
    mixes = [mixed, mixed_far]
    mixes += [exchange(mixed, "tile", 1), exchange(mixed_far, "tile", 1)]

    square = pltpu.VMEM((2, half, half), BF16)
    squares = pltpu.VMEM((2, 2, half, half), BF16)
    rim = pltpu.VMEM((2, 2, rows, half), BF16)
    inner, cross, left, corner = call(
        first_level,
        [bf16(2, rows, half), bf16(2, rows, half), bf16(2, rows, half), f32(2, rows, half)],
        [square, square, squares, rim, rim],
        16,
        int(2.7e9),
        *owns,
        *mixes,
        keep,
        outer_got,
    )
    inner_other = exchange(inner, "cluster", 2)
    cross_far = exchange(cross, "tile", 2)
    summed = total_of(inner, inner_other)
    summed_far = exchange(summed, "tile", 2)
    cross_other = exchange(after(cross, summed), "cluster", 2)
    cross_far_other = exchange(cross_far, "cluster", 2)

    def with_core(x, y):
        return [x, y, exchange(x, "tile", 1), exchange(y, "tile", 1)]

    kept, sent, diagonal = call(
        last_level,
        [f32(2, few, nodes), bf16(2, few, nodes), f32(1, LANES)],
        [square, square, squares, pltpu.VMEM((2, rows, nodes), F32)],
        12,
        int(1.4e9),
        *with_core(summed, summed_far),
        *with_core(cross, cross_far),
        *with_core(cross_other, cross_far_other),
        left,
        corner,
        energy_weights,
        in_vmem=(12, 13),
        in_smem=(14,),
    )
    density = diagonal + exchange(diagonal, "cluster", 1)
    got_rows = exchange(sent, "cluster", 1).astype(F32)
    for distance in (1, 2):
        density = density + exchange(density, "energy", distance)
    density = jnp.where(side == 0, density[:, :few], density[:, few:])
    low = jnp.where(side == 0, kept, got_rows)
    high = jnp.where(side == 0, got_rows, kept)
    final_rows = jnp.stack([low, high]).transpose(2, 0, 1, 3)
    return final_rows[None], density


def solution(mesh):
    placed = (P("cluster", None, "tile", "energy", None, None), P("cluster", None), P("energy"))
    return jax.shard_map(
        compute,
        mesh=mesh,
        in_specs=placed,
        out_specs=(P("cluster", "tile", "energy", None, None), P("cluster", "tile")),
        check_vma=False,
    )
```

time: 137 us -> 126 us (0.920)
  blocking collectives: 17.2 us -> 0 us
  waiting for transfers between devices: 59.5 us -> 72.2 us
  Pallas kernels: 16.7 us -> 14.2 us
  starting transfers between devices: 37 us -> 34.7 us
  local copies, waits for them, and re-layouts: 3.8 us -> 1.82 us
    psum x1 -> x0, blocking collectives: 17.2 us -> none  [compute(): density = lax.psum(kept_diag + got_diag, 'energy')]
    ppermute x18 -> x23, waiting for transfers between devices: 59.5 us -> 72.2 us  [exchange(): lax.ppermute(x, axis, [(i, i ^ distance) for i in range(lax.axis_size(axi...]
    pallas_call x4, Pallas kernels: 16.7 us -> 14.2 us  [call(): pl.pallas_call(body, out_shape=out_shape, in_specs=[pl.BlockSpec(memory_s...]
    ppermute x18 -> x23, starting transfers between devices: 37 us -> 34.7 us  [exchange(): lax.ppermute(x, axis, [(i, i ^ distance) for i in range(lax.axis_size(axi...]
    unnamed x9, local copies, waits for them, and re-layouts: 3.78 us -> 1.8 us
  transfers between devices with their start and end apart: 18 -> 23, of which waited for: 9 -> 11; matrix products, arithmetic and copies ran while one was open for 1% -> 1% of each run, Pallas kernels for 0% -> 2%
where the time goes in v3:
time: 126 us
  waiting for transfers between devices  72.2 us (57%)
  starting transfers between devices  34.7 us (28%)
  Pallas kernels  14.2 us (11%)
  other arithmetic  1.92 us (2%)
  local copies, waits for them, and re-layouts  1.82 us (1%)
    ppermute x23, waiting for transfers between devices, exchange(): lax.ppermute(x, axis, [(i, i ^ distance) for i in range(lax.axis_size(axi...  72.2 us
    ppermute x23, starting transfers between devices, exchange(): lax.ppermute(x, axis, [(i, i ^ distance) for i in range(lax.axis_size(axi...  34.7 us
    pallas_call x4, Pallas kernels, call(): pl.pallas_call(body, out_shape=out_shape, in_specs=[pl.BlockSpec(memory_s...  14.2 us
  transfers between devices with their start and end apart: 23, of which 11 were waited for; matrix products, arithmetic and copies ran while one was open for 1% of the time, Pallas kernels for 2%

profile of v3, /device:TPU:2, one launch (start us, length us, event | category | flops | bytes accessed | tf_op | source)
XLA Modules:
  0.0 125.7 jit_solution(9280494824105228338)
XLA Ops:
  0.6 3.8 %shard_map.50 = (bf16[2,128,1024]{2,1,0:T(8,128)(2,1)}, bf16[2,128,512]{2,1,0:T(8,128)(2,1)}, bf16[2,128,512]{2,1,0:T(8,128)(2,1)}) custom-call(s32[1,1024]{1,0:T(1,128)} %column_ref.2, bf16[1,2,128,2,2,1024]{5,4,3,2,1,0:T(2,128)(2,1)} %raw.3), custom_call_target="tpu_custom_call" | custom-call | flops 2000000000 | bytes 4194304 | tf_op jit(solution)/shard_map/pallas_call | solution.py:63
  4.5 1.7 %collective-permute-start.3 = (bf16[2,128,1024]{2,1,0:T(8,128)(2,1)}, bf16[2,128,1024]{2,1,0:T(8,128)(2,1)S(1)}, u32[]{:S(2)}, u32[]{:S(2)}) collective-permute-start(bf16[2,128,1024]{2,1,0:T(8,128)(2,1)} %get-tuple-element.19), channel_id=1, source_target_pairs={{0,4},{4,0},{8,12},{12,8},{16,20},{20,16},{24,28},{28,24},{32,36},... | collective-permute-start | bytes 1572872 | tf_op jit(solution)/shard_map/ppermute | solution.py:15
  6.1 12.3 %collective-permute-done.3 = bf16[2,128,1024]{2,1,0:T(8,128)(2,1)S(1)} collective-permute-done((bf16[2,128,1024]{2,1,0:T(8,128)(2,1)}, bf16[2,128,1024]{2,1,0:T(8,128)(2,1)S(1)}, u32[]{:S(2)}, u32[]{:S(2)}) %collective-permute-start.3) | collective-permute-done | bytes 524320 | tf_op jit(solution)/shard_map/ppermute | solution.py:15
  18.4 1.0 add_convert_fusion.1
  19.5 7.3 %collective-permute-start.4 = (bf16[2,128,1024]{2,1,0:T(8,128)(2,1)S(1)}, bf16[2,128,1024]{2,1,0:T(8,128)(2,1)S(1)}, u32[]{:S(2)}, u32[]{:S(2)}) collective-permute-start(bf16[2,128,1024]{2,1,0:T(8,128)(2,1)S(1)} %pad_maximum_fusion.refs_4_), channel_id=1, source_target_pairs={{0,2},{1,3},{2,0},{3,1},{4,6},{5,7},{6,4},{7,5},{8,10},{9,11},{10,... | collective-permute-start | bytes 1572872 | tf_op jit(solution)/shard_map/ppermute | solution.py:15
  26.9 2.3 %shard_map.51 = (bf16[2,128,1024]{2,1,0:T(8,128)(2,1)S(1)}, bf16[2,128,1024]{2,1,0:T(8,128)(2,1)S(1)}) custom-call(s32[1,1024]{1,0:T(1,128)S(1)} %copy-done.2, bf16[1,2,128,2,2,1024]{5,4,3,2,1,0:T(2,128)(2,1)S(1)} %copy-done), custom_call_target="tpu_custom_call" | custom-call | flops 2000000000 | bytes 4194304 | tf_op jit(solution)/shard_map/pallas_call | solution.py:63
  29.4 1.7 %collective-permute-start.7 = (bf16[2,128,1024]{2,1,0:T(8,128)(2,1)S(1)}, bf16[2,128,1024]{2,1,0:T(8,128)(2,1)S(1)}, u32[]{:S(2)}, u32[]{:S(2)}) collective-permute-start(bf16[2,128,1024]{2,1,0:T(8,128)(2,1)S(1)} %get-tuple-element.23), channel_id=1, source_target_pairs={{0,4},{4,0},{8,12},{12,8},{16,20},{20,16},{24,28},{28,24},{32,36},... | collective-permute-start | bytes 1572872 | tf_op jit(solution)/shard_map/ppermute | solution.py:15
  31.0 12.1 %collective-permute-done.4.refs_5_ = bf16[2,128,1024]{2,1,0:T(8,128)(2,1)S(1)} collective-permute-done((bf16[2,128,1024]{2,1,0:T(8,128)(2,1)S(1)}, bf16[2,128,1024]{2,1,0:T(8,128)(2,1)S(1)}, u32[]{:S(2)}, u32[]{:S(2)}) %collective-permute-start.4) | collective-permute-done | bytes 524320 | tf_op jit(solution)/shard_map/ppermute | solution.py:15
  43.6 15.4 %collective-permute-done.refs_1_ = bf16[2,128,512]{2,1,0:T(8,128)(2,1)S(1)} collective-permute-done((bf16[2,128,512]{2,1,0:T(8,128)(2,1)S(1)}, bf16[2,128,512]{2,1,0:T(8,128)(2,1)S(1)}, u32[]{:S(2)}, u32[]{:S(2)}) %collective-permute-start) | collective-permute-done | bytes 262176 | tf_op jit(solution)/shard_map/ppermute | solution.py:15
  59.0 1.5 %collective-permute-done.2.refs_3_ = bf16[2,128,512]{2,1,0:T(8,128)(2,1)S(1)} collective-permute-done((bf16[2,128,512]{2,1,0:T(8,128)(2,1)S(1)}, bf16[2,128,512]{2,1,0:T(8,128)(2,1)S(1)}, u32[]{:S(2)}, u32[]{:S(2)}) %collective-permute-start.2) | collective-permute-done | bytes 262176 | tf_op jit(solution)/shard_map/ppermute | solution.py:15
  60.6 4.5 %shard_map.52 = (bf16[2,128,512]{2,1,0:T(8,128)(2,1)S(1)}, bf16[2,128,512]{2,1,0:T(8,128)(2,1)S(1)}, bf16[2,128,512]{2,1,0:T(8,128)(2,1)S(1)}, f32[2,128,512]{2,1,0:T(8,128)S(1)}) custom-call(bf16[2,128,512]{2,1,0:T(8,128)(2,1)S(1)} %copy-done.1, bf16[2,128,512]{2,1,0:T(8,128)(2,1)S(1)} %collective-permute-done.refs_1_, ...), custom_call_target="tpu_custom_call" | custom-call | flops 2700000000 | bytes 4194304 | tf_op jit(solution)/shard_map/pallas_call | solution.py:63
  65.1 3.5 %collective-permute-start.8 = (bf16[2,128,512]{2,1,0:T(8,128)(2,1)S(1)}, bf16[2,128,512]{2,1,0:T(8,128)(2,1)S(1)}, u32[]{:S(2)}, u32[]{:S(2)}) collective-permute-start(bf16[2,128,512]{2,1,0:T(8,128)(2,1)S(1)} %get-tuple-element.24), channel_id=1, source_target_pairs={{0,8},{4,12},{8,0},{12,4},{16,24},{20,28},{24,16},{28,20},{32,40},... | collective-permute-start | bytes 786440 | tf_op jit(solution)/shard_map/ppermute | solution.py:15
  68.6 6.4 %collective-permute-start.12 = (bf16[2,128,512]{2,1,0:T(8,128)(2,1)S(1)}, bf16[2,128,512]{2,1,0:T(8,128)(2,1)S(1)}, u32[]{:S(2)}, u32[]{:S(2)}) collective-permute-start(bf16[2,128,512]{2,1,0:T(8,128)(2,1)S(1)} %get-tuple-element.26.refs_4_), channel_id=1, source_target_pairs={{0,2},{1,3},{2,0},{3,1},{4,6},{5,7},{6,4},{7,5},{8,10},{9,11},{10,... | collective-permute-start | bytes 786440 | tf_op jit(solution)/shard_map/ppermute | solution.py:15
  75.3 3.3 %collective-permute-start.15 = (bf16[2,128,512]{2,1,0:T(8,128)(2,1)S(1)}, bf16[2,128,512]{2,1,0:T(8,128)(2,1)S(1)}, u32[]{:S(2)}, u32[]{:S(2)}) collective-permute-start(bf16[2,128,512]{2,1,0:T(8,128)(2,1)S(1)} %get-tuple-element.26.refs_4_), channel_id=1, source_target_pairs={{0,8},{4,12},{8,0},{12,4},{16,24},{20,28},{24,16},{28,20},{32,40},... | collective-permute-start | bytes 786440 | tf_op jit(solution)/shard_map/ppermute | solution.py:15
  78.6 6.4 %collective-permute-start.9 = (bf16[2,128,512]{2,1,0:T(8,128)(2,1)S(1)}, bf16[2,128,512]{2,1,0:T(8,128)(2,1)S(1)}, u32[]{:S(2)}, u32[]{:S(2)}) collective-permute-start(bf16[2,128,512]{2,1,0:T(8,128)(2,1)S(1)} %add_convert_fusion.refs_0_), channel_id=1, source_target_pairs={{0,2},{1,3},{2,0},{3,1},{4,6},{5,7},{6,4},{7,5},{8,10},{9,11},{10,... | collective-permute-start | bytes 786440 | tf_op jit(solution)/shard_map/ppermute | solution.py:15
  86.0 15.1 %collective-permute-done.9.refs_1_ = bf16[2,128,512]{2,1,0:T(8,128)(2,1)S(1)} collective-permute-done((bf16[2,128,512]{2,1,0:T(8,128)(2,1)S(1)}, bf16[2,128,512]{2,1,0:T(8,128)(2,1)S(1)}, u32[]{:S(2)}, u32[]{:S(2)}) %collective-permute-start.9) | collective-permute-done | bytes 262176 | tf_op jit(solution)/shard_map/ppermute | solution.py:15
  101.6 1.0 collective-permute-done.11.refs_3_
  103.0 3.6 %shard_map.53 = (f32[2,64,1024]{2,1,0:T(8,128)S(1)}, bf16[2,64,1024]{2,1,0:T(8,128)(2,1)S(1)}, f32[1,128]{1,0:T(1,128)S(1)}) custom-call(bf16[2,128,512]{2,1,0:T(8,128)(2,1)S(1)} %add_convert_fusion.refs_0_, bf16[2,128,512]{2,1,0:T(8,128)(2,1)S(1)} %collective-permute-done.9.refs_1_, bf16[2,128,512]{2,1,0:T(8,128)(2,1)S(1)} %collective-permute-done.10.refs_2_, ...), custom_call_target="tpu_custom_call" | custom-call | flops 1400000000 | bytes 4194304 | tf_op jit(solution)/shard_map/pallas_call | solution.py:63
  106.6 0.8 collective-permute-start.19
  107.4 1.3 %collective-permute-start.20 = (f32[1,128]{1,0:T(1,128)S(1)}, f32[1,128]{1,0:T(1,128)S(1)}, u32[]{:S(2)}, u32[]{:S(2)}) collective-permute-start(f32[1,128]{1,0:T(1,128)S(1)} %get-tuple-element.31), channel_id=1, source_target_pairs={{0,4},{4,0},{8,12},{12,8},{16,20},{20,16},{24,28},{28,24},{32,36},... | collective-permute-start | bytes 1544 | tf_op jit(solution)/shard_map/ppermute | solution.py:15
  108.7 6.4 %collective-permute-done.20 = f32[1,128]{1,0:T(1,128)S(1)} collective-permute-done((f32[1,128]{1,0:T(1,128)S(1)}, f32[1,128]{1,0:T(1,128)S(1)}, u32[]{:S(2)}, u32[]{:S(2)}) %collective-permute-start.20) | collective-permute-done | bytes 544 | tf_op jit(solution)/shard_map/ppermute | solution.py:15
  115.1 3.6 %collective-permute-done.21 = f32[1,128]{1,0:T(1,128)S(1)} collective-permute-done((f32[1,128]{1,0:T(1,128)S(1)}, f32[1,128]{1,0:T(1,128)S(1)}, u32[]{:S(2)}, u32[]{:S(2)}) %collective-permute-start.21) | collective-permute-done | bytes 544 | tf_op jit(solution)/shard_map/ppermute | solution.py:15
  119.0 4.2 %collective-permute-done.22 = f32[1,128]{1,0:T(1,128)S(1)} collective-permute-done((f32[1,128]{1,0:T(1,128)S(1)}, f32[1,128]{1,0:T(1,128)S(1)}, u32[]{:S(2)}, u32[]{:S(2)}) %collective-permute-start.22) | collective-permute-done | bytes 544 | tf_op jit(solution)/shard_map/ppermute | solution.py:15
  123.9 1.8 %copy.5 = f32[1,64,2,2,1024]{4,3,2,1,0:T(2,128)} copy(f32[1,64,2,2,1024]{4,1,3,2,0:T(8,128)S(1)} %maximum_bitcast_fusion) | data formatting | bytes 2097152
  (45 shorter events, 4.1 us)
Async XLA Ops:
  4.5 14.0 %collective-permute-start.3 = (bf16[2,128,1024]{2,1,0:T(8,128)(2,1)}, bf16[2,128,1024]{2,1,0:T(8,128)(2,1)S(1)}, u32[]{:S(2)}, u32[]{:S(2)}) collective-permute-start(bf16[2,128,1024]{2,1,0:T(8,128)(2,1)} %get-tuple-element.19), channel_id=1, source_target_pairs={{0,4},{4,0},{8,12},{12,8},{16,20},{20,16},{24,28},{28,24},{32,36},... | collective-permute-start | bytes 1572872 | tf_op jit(solution)/shard_map/ppermute | solution.py:15
  19.5 23.6 %collective-permute-start.4 = (bf16[2,128,1024]{2,1,0:T(8,128)(2,1)S(1)}, bf16[2,128,1024]{2,1,0:T(8,128)(2,1)S(1)}, u32[]{:S(2)}, u32[]{:S(2)}) collective-permute-start(bf16[2,128,1024]{2,1,0:T(8,128)(2,1)S(1)} %pad_maximum_fusion.refs_4_), channel_id=1, source_target_pairs={{0,2},{1,3},{2,0},{3,1},{4,6},{5,7},{6,4},{7,5},{8,10},{9,11},{10,... | collective-permute-start | bytes 1572872 | tf_op jit(solution)/shard_map/ppermute | solution.py:15
  26.8 32.2 %collective-permute-start = (bf16[2,128,512]{2,1,0:T(8,128)(2,1)S(1)}, bf16[2,128,512]{2,1,0:T(8,128)(2,1)S(1)}, u32[]{:S(2)}, u32[]{:S(2)}) collective-permute-start(bf16[2,128,512]{2,1,0:T(8,128)(2,1)S(1)} %copy-done.1), channel_id=1, source_target_pairs={{0,2},{1,3},{2,0},{3,1},{4,6},{5,7},{6,4},{7,5},{8,10},{9,11},{10,... | collective-permute-start | bytes 786440 | tf_op jit(solution)/shard_map/ppermute | solution.py:15
  29.3 31.3 %collective-permute-start.5 = (bf16[2,128,1024]{2,1,0:T(8,128)(2,1)S(1)}, bf16[2,128,1024]{2,1,0:T(8,128)(2,1)S(1)}, u32[]{:S(2)}, u32[]{:S(2)}) collective-permute-start(bf16[2,128,1024]{2,1,0:T(8,128)(2,1)S(1)} %pad_maximum_fusion.refs_4_), channel_id=1, source_target_pairs={{0,1},{1,0},{2,3},{3,2},{4,5},{5,4},{6,7},{7,6},{8,9},{9,8},{10,11... | collective-permute-start | bytes 1572872 | tf_op jit(solution)/shard_map/ppermute | solution.py:15
  29.4 31.2 %collective-permute-start.7 = (bf16[2,128,1024]{2,1,0:T(8,128)(2,1)S(1)}, bf16[2,128,1024]{2,1,0:T(8,128)(2,1)S(1)}, u32[]{:S(2)}, u32[]{:S(2)}) collective-permute-start(bf16[2,128,1024]{2,1,0:T(8,128)(2,1)S(1)} %get-tuple-element.23), channel_id=1, source_target_pairs={{0,4},{4,0},{8,12},{12,8},{16,20},{20,16},{24,28},{28,24},{32,36},... | collective-permute-start | bytes 1572872 | tf_op jit(solution)/shard_map/ppermute | solution.py:15
  43.1 17.5 %collective-permute-start.6 = (bf16[2,128,1024]{2,1,0:T(8,128)(2,1)S(1)}, bf16[2,128,1024]{2,1,0:T(8,128)(2,1)S(1)}, u32[]{:S(2)}, u32[]{:S(2)}) collective-permute-start(bf16[2,128,1024]{2,1,0:T(8,128)(2,1)S(1)} %collective-permute-done.4.refs_5_), channel_id=1, source_target_pairs={{0,1},{1,0},{2,3},{3,2},{4,5},{5,4},{6,7},{7,6},{8,9},{9,8},{10,11... | collective-permute-start | bytes 1572872 | tf_op jit(solution)/shard_map/ppermute | solution.py:15
  43.1 15.9 %collective-permute-start.1 = (bf16[2,128,512]{2,1,0:T(8,128)(2,1)S(1)}, bf16[2,128,512]{2,1,0:T(8,128)(2,1)S(1)}, u32[]{:S(2)}, u32[]{:S(2)}) collective-permute-start(bf16[2,128,512]{2,1,0:T(8,128)(2,1)S(1)} %copy-done.1), channel_id=1, source_target_pairs={{0,1},{1,0},{2,3},{3,2},{4,5},{5,4},{6,7},{7,6},{8,9},{9,8},{10,11... | collective-permute-start | bytes 786440 | tf_op jit(solution)/shard_map/ppermute | solution.py:15
  59.0 1.5 %collective-permute-start.2 = (bf16[2,128,512]{2,1,0:T(8,128)(2,1)S(1)}, bf16[2,128,512]{2,1,0:T(8,128)(2,1)S(1)}, u32[]{:S(2)}, u32[]{:S(2)}) collective-permute-start(bf16[2,128,512]{2,1,0:T(8,128)(2,1)S(1)} %collective-permute-done.refs_1_), channel_id=1, source_target_pairs={{0,1},{1,0},{2,3},{3,2},{4,5},{5,4},{6,7},{7,6},{8,9},{9,8},{10,11... | collective-permute-start | bytes 786440 | tf_op jit(solution)/shard_map/ppermute | solution.py:15
  60.6 42.4 %copy-start.3 = (f32[2]{0:T(128)S(1)}, f32[2]{0:T(128)}, u32[]{:S(2)}) copy-start(f32[2]{0:T(128)} %refs_14_.1) | copy-start | bytes 28
  65.1 10.1 %collective-permute-start.8 = (bf16[2,128,512]{2,1,0:T(8,128)(2,1)S(1)}, bf16[2,128,512]{2,1,0:T(8,128)(2,1)S(1)}, u32[]{:S(2)}, u32[]{:S(2)}) collective-permute-start(bf16[2,128,512]{2,1,0:T(8,128)(2,1)S(1)} %get-tuple-element.24), channel_id=1, source_target_pairs={{0,8},{4,12},{8,0},{12,4},{16,24},{20,28},{24,16},{28,20},{32,40},... | collective-permute-start | bytes 786440 | tf_op jit(solution)/shard_map/ppermute | solution.py:15
  68.6 16.4 %collective-permute-start.12 = (bf16[2,128,512]{2,1,0:T(8,128)(2,1)S(1)}, bf16[2,128,512]{2,1,0:T(8,128)(2,1)S(1)}, u32[]{:S(2)}, u32[]{:S(2)}) collective-permute-start(bf16[2,128,512]{2,1,0:T(8,128)(2,1)S(1)} %get-tuple-element.26.refs_4_), channel_id=1, source_target_pairs={{0,2},{1,3},{2,0},{3,1},{4,6},{5,7},{6,4},{7,5},{8,10},{9,11},{10,... | collective-permute-start | bytes 786440 | tf_op jit(solution)/shard_map/ppermute | solution.py:15
  75.0 10.4 %collective-permute-start.13 = (bf16[2,128,512]{2,1,0:T(8,128)(2,1)S(1)}, bf16[2,128,512]{2,1,0:T(8,128)(2,1)S(1)}, u32[]{:S(2)}, u32[]{:S(2)}) collective-permute-start(bf16[2,128,512]{2,1,0:T(8,128)(2,1)S(1)} %get-tuple-element.26.refs_4_), channel_id=1, source_target_pairs={{0,1},{1,0},{2,3},{3,2},{4,5},{5,4},{6,7},{7,6},{8,9},{9,8},{10,11... | collective-permute-start | bytes 786440 | tf_op jit(solution)/shard_map/ppermute | solution.py:15
  75.3 10.6 %collective-permute-start.15 = (bf16[2,128,512]{2,1,0:T(8,128)(2,1)S(1)}, bf16[2,128,512]{2,1,0:T(8,128)(2,1)S(1)}, u32[]{:S(2)}, u32[]{:S(2)}) collective-permute-start(bf16[2,128,512]{2,1,0:T(8,128)(2,1)S(1)} %get-tuple-element.26.refs_4_), channel_id=1, source_target_pairs={{0,8},{4,12},{8,0},{12,4},{16,24},{20,28},{24,16},{28,20},{32,40},... | collective-permute-start | bytes 786440 | tf_op jit(solution)/shard_map/ppermute | solution.py:15
  78.6 22.5 %collective-permute-start.9 = (bf16[2,128,512]{2,1,0:T(8,128)(2,1)S(1)}, bf16[2,128,512]{2,1,0:T(8,128)(2,1)S(1)}, u32[]{:S(2)}, u32[]{:S(2)}) collective-permute-start(bf16[2,128,512]{2,1,0:T(8,128)(2,1)S(1)} %add_convert_fusion.refs_0_), channel_id=1, source_target_pairs={{0,2},{1,3},{2,0},{3,1},{4,6},{5,7},{6,4},{7,5},{8,10},{9,11},{10,... | collective-permute-start | bytes 786440 | tf_op jit(solution)/shard_map/ppermute | solution.py:15
  85.0 16.1 %collective-permute-start.16 = (bf16[2,128,512]{2,1,0:T(8,128)(2,1)S(1)}, bf16[2,128,512]{2,1,0:T(8,128)(2,1)S(1)}, u32[]{:S(2)}, u32[]{:S(2)}) collective-permute-start(bf16[2,128,512]{2,1,0:T(8,128)(2,1)S(1)} %collective-permute-done.12.refs_5_), channel_id=1, source_target_pairs={{0,8},{4,12},{8,0},{12,4},{16,24},{20,28},{24,16},{28,20},{32,40},... | collective-permute-start | bytes 786440 | tf_op jit(solution)/shard_map/ppermute | solution.py:15
  85.4 16.2 %collective-permute-start.10 = (bf16[2,128,512]{2,1,0:T(8,128)(2,1)S(1)}, bf16[2,128,512]{2,1,0:T(8,128)(2,1)S(1)}, u32[]{:S(2)}, u32[]{:S(2)}) collective-permute-start(bf16[2,128,512]{2,1,0:T(8,128)(2,1)S(1)} %add_convert_fusion.refs_0_), channel_id=1, source_target_pairs={{0,1},{1,0},{2,3},{3,2},{4,5},{5,4},{6,7},{7,6},{8,9},{9,8},{10,11... | collective-permute-start | bytes 786440 | tf_op jit(solution)/shard_map/ppermute | solution.py:15
  85.4 16.2 %collective-permute-start.14 = (bf16[2,128,512]{2,1,0:T(8,128)(2,1)S(1)}, bf16[2,128,512]{2,1,0:T(8,128)(2,1)S(1)}, u32[]{:S(2)}, u32[]{:S(2)}) collective-permute-start(bf16[2,128,512]{2,1,0:T(8,128)(2,1)S(1)} %collective-permute-done.12.refs_5_), channel_id=1, source_target_pairs={{0,1},{1,0},{2,3},{3,2},{4,5},{5,4},{6,7},{7,6},{8,9},{9,8},{10,11... | collective-permute-start | bytes 786440 | tf_op jit(solution)/shard_map/ppermute | solution.py:15
  85.9 15.7 %collective-permute-start.17 = (bf16[2,128,512]{2,1,0:T(8,128)(2,1)S(1)}, bf16[2,128,512]{2,1,0:T(8,128)(2,1)S(1)}, u32[]{:S(2)}, u32[]{:S(2)}) collective-permute-start(bf16[2,128,512]{2,1,0:T(8,128)(2,1)S(1)} %collective-permute-done.15.refs_8_), channel_id=1, source_target_pairs={{0,1},{1,0},{2,3},{3,2},{4,5},{5,4},{6,7},{7,6},{8,9},{9,8},{10,11... | collective-permute-start | bytes 786440 | tf_op jit(solution)/shard_map/ppermute | solution.py:15
  101.1 1.5 %collective-permute-start.11 = (bf16[2,128,512]{2,1,0:T(8,128)(2,1)S(1)}, bf16[2,128,512]{2,1,0:T(8,128)(2,1)S(1)}, u32[]{:S(2)}, u32[]{:S(2)}) collective-permute-start(bf16[2,128,512]{2,1,0:T(8,128)(2,1)S(1)} %collective-permute-done.9.refs_1_), channel_id=1, source_target_pairs={{0,1},{1,0},{2,3},{3,2},{4,5},{5,4},{6,7},{7,6},{8,9},{9,8},{10,11... | collective-permute-start | bytes 786440 | tf_op jit(solution)/shard_map/ppermute | solution.py:15
  101.1 1.9 %collective-permute-start.18 = (bf16[2,128,512]{2,1,0:T(8,128)(2,1)S(1)}, bf16[2,128,512]{2,1,0:T(8,128)(2,1)S(1)}, u32[]{:S(2)}, u32[]{:S(2)}) collective-permute-start(bf16[2,128,512]{2,1,0:T(8,128)(2,1)S(1)} %collective-permute-done.16.refs_9_), channel_id=1, source_target_pairs={{0,1},{1,0},{2,3},{3,2},{4,5},{5,4},{6,7},{7,6},{8,9},{9,8},{10,11... | collective-permute-start | bytes 786440 | tf_op jit(solution)/shard_map/ppermute | solution.py:15
  106.6 17.2 %collective-permute-start.19 = (bf16[2,64,1024]{2,1,0:T(8,128)(2,1)S(1)}, bf16[2,64,1024]{2,1,0:T(8,128)(2,1)S(1)}, u32[]{:S(2)}, u32[]{:S(2)}) collective-permute-start(bf16[2,64,1024]{2,1,0:T(8,128)(2,1)S(1)} %get-tuple-element.30), channel_id=1, source_target_pairs={{0,4},{4,0},{8,12},{12,8},{16,20},{20,16},{24,28},{28,24},{32,36},... | collective-permute-start | bytes 786440 | tf_op jit(solution)/shard_map/ppermute | solution.py:15
  107.4 7.8 %collective-permute-start.20 = (f32[1,128]{1,0:T(1,128)S(1)}, f32[1,128]{1,0:T(1,128)S(1)}, u32[]{:S(2)}, u32[]{:S(2)}) collective-permute-start(f32[1,128]{1,0:T(1,128)S(1)} %get-tuple-element.31), channel_id=1, source_target_pairs={{0,4},{4,0},{8,12},{12,8},{16,20},{20,16},{24,28},{28,24},{32,36},... | collective-permute-start | bytes 1544 | tf_op jit(solution)/shard_map/ppermute | solution.py:15
  115.1 3.6 %collective-permute-start.21 = (f32[1,128]{1,0:T(1,128)S(1)}, f32[1,128]{1,0:T(1,128)S(1)}, u32[]{:S(2)}, u32[]{:S(2)}) collective-permute-start(f32[1,128]{1,0:T(1,128)S(1)} %add.22), channel_id=1, source_target_pairs={{0,64},{64,0},{128,192},{192,128},{1,65},{65,1},{129,193},{193,129... | collective-permute-start | bytes 1544 | tf_op jit(solution)/shard_map/ppermute | solution.py:15
  118.7 4.5 %collective-permute-start.22 = (f32[1,128]{1,0:T(1,128)S(1)}, f32[1,128]{1,0:T(1,128)S(1)}, u32[]{:S(2)}, u32[]{:S(2)}) collective-permute-start(f32[1,128]{1,0:T(1,128)S(1)} %add.23), channel_id=1, source_target_pairs={{0,128},{64,192},{128,0},{192,64},{1,129},{65,193},{129,1},{193,65... | collective-permute-start | bytes 1544 | tf_op jit(solution)/shard_map/ppermute | solution.py:15
  (3 other events, 67.4 us)

commit v4 on v3

--- a/solution.py
+++ b/solution.py
@@ -77,17 +77,16 @@
     return cluster % 2, tile // 2, tile % 2, cluster // 2 % 2
 
 
-def fill_selector(column_ref, selector):
-    size = selector.shape[0]
-    source = lax.broadcasted_iota(jnp.int32, (size, size), 0)
-    selector[...] = jnp.where(source == column_ref[...], 1.0, 0.0).astype(BF16)
+def fill_selector(column, selector):
+    source = lax.broadcasted_iota(jnp.int32, selector.shape, 0)
+    selector[...] = jnp.where(source == column, 1.0, 0.0).astype(BF16)
 
 
 def reorder(stage, selector, parted):
     count, _, nodes = stage.shape
     flat = stage[...].reshape(2 * count, nodes)
     wide = 2 * LANES
-    for first in range(0, nodes, wide):
+    for first in range(0, selector.shape[1], wide):
         ordered = dot(flat, selector[:, first : first + wide])
         for turn in range(2):
             parted[first // LANES + turn] = ordered[:, turn * LANES : (turn + 1) * LANES]
@@ -97,8 +96,29 @@
     return parted[block, pl.ds(2 * first + part, count, stride=2), :].astype(BF16)
 
 
+def order_cross(column_ref, raw, both_out, column, own_stage, other_stage, selector, parted, sems):
+    side, _, _, _ = places()
+    copies = Copies(sems)
+    first = copies.start(column_ref, column)
+    owned = copies.start(raw.at[0, 0, :, side], own_stage)
+    other = copies.start(raw.at[0, 0, :, 1 - side], other_stage)
+    first.wait()
+    width = selector.shape[1]
+    fill_selector(column[:, width:], selector)
+    count = own_stage.shape[0]
+    for turn, (copy, stage) in enumerate(((owned, own_stage), (other, other_stage))):
+        copy.wait()
+        reorder(stage, selector, parted.at[turn])
+        for block in range(parted.shape[1]):
+            first_lane = turn * width + block * LANES
+            for part in range(2):
+                both_out[part, :, first_lane : first_lane + LANES] = lane_block(
+                    parted.at[turn], block, part, 0, count
+                )
+
+
 def order_first(
-    column_ref, raw, send_out, inner_out, cross_out,
+    column_ref, raw, send_out, inner_out,
     column, send_stage, own_stage, selector, send_parted, own_parted, sems,
 ):
     side, _, _, _ = places()
@@ -107,22 +127,18 @@
     sent = copies.start(raw.at[0, 0, :, 1 - side], send_stage)
     owned = copies.start(raw.at[0, 0, :, side], own_stage)
     first.wait()
-    fill_selector(column, selector)
+    fill_selector(column[...], selector)
     sent.wait()
     reorder(send_stage, selector, send_parted)
     owned.wait()
-    reorder(own_stage, selector, own_parted)
-    blocks = send_parted.shape[0]
+    reorder(own_stage, selector.at[:, : inner_out.shape[2]], own_parted)
     count = send_stage.shape[0]
-    for block in range(blocks):
+    for block in range(send_parted.shape[0]):
         lanes = slice(block * LANES, (block + 1) * LANES)
-        out = (inner_out, cross_out)[2 * block // blocks]
-        column_at = block % (blocks // 2) * LANES
         for part in range(2):
             send_out[part, :, lanes] = lane_block(send_parted, block, part, 0, count)
-            out[part, :, column_at : column_at + LANES] = lane_block(
-                own_parted, block, part, 0, count
-            )
+            if lanes.stop <= inner_out.shape[2]:
+                inner_out[part, :, lanes] = lane_block(own_parted, block, part, 0, count)
 
 
 def order_second(
@@ -135,7 +151,7 @@
     sent = copies.start(raw.at[0, 1, :, 1 - side], send_stage)
     owned = copies.start(raw.at[0, 1, :, side], own_stage)
     first.wait()
-    fill_selector(column, selector)
+    fill_selector(column[...], selector)
     sent.wait()
     reorder(send_stage, selector, send_parted)
     owned.wait()
@@ -198,27 +214,27 @@
     made = []
     for who, piece in enumerate(pieces):
         row = at(((depth ^ (who % 2)) * 2 + (core ^ (who // 2))) * rows, rows)
-        made.append(copies.start(piece.at[:, :, columns], target.at[:, row]))
+        made.append(copies.start(piece.at[:, :, columns[who]], target.at[:, row]))
     return made
 
 
 def first_level(*refs):
-    owns, mixed = refs[0:4], refs[4:8]
-    keep, got = refs[8:10]
-    inner_out, cross_out, left_out, corner_out = refs[10:14]
-    interior, approx, right, left, start, sems = refs[14:]
+    sums, owns = refs[0:4], refs[4:8]
+    others, keep, got = refs[8:12], refs[12], refs[13]
+    inner_out, cross_out, left_out, corner_out = refs[14:18]
+    interior, approx, right, left, start, sems = refs[18:]
     side, _, _, _ = places()
     copies = Copies(sems)
     width = interior.shape[1]
     rows = keep.shape[1]
     lows, highs = pl.ds(0, width), pl.ds(width, width)
-    from_inner = spread(copies, mixed, lows, interior)
+    from_inner = spread(copies, sums, [lows] * 4, interior)
     from_outer = [
         copies.start(keep.at[:, :, lows], left.at[side]),
         copies.start(got.at[:, :, lows], left.at[1 - side]),
     ]
-    from_cross = spread(copies, owns, lows, right.at[side])
-    from_cross += spread(copies, mixed, highs, right.at[1 - side])
+    from_cross = spread(copies, owns, [lows] * 4, right.at[side])
+    from_cross += spread(copies, others, [highs, lows] * 2, right.at[1 - side])
     from_cross += [
         copies.start(keep.at[:, :, highs], start.at[side]),
         copies.start(got.at[:, :, highs], start.at[1 - side]),
@@ -248,7 +264,7 @@
     width = interior.shape[1]
     rows = corner.shape[1]
     few = rows // 2
-    every = pl.ds(0, width)
+    every = [pl.ds(0, width)] * 4
     from_inner = spread(copies, sums, every, interior)
     from_cross = spread(copies, owns, every, right.at[pair])
     from_cross += spread(copies, others, every, right.at[1 - pair])
@@ -272,6 +288,13 @@
         keep_out[part] = total[part, keep_rows, :]
 
 
+def finish(kept, got, out, sems):
+    side, _, _, _ = places()
+    for part in range(2):
+        out[0, :, side, part, :] = kept[part]
+        out[0, :, 1 - side, part, :] = got[part].astype(F32)
+
+
 def after(x, *others):
     return lax.optimization_barrier((x,) + others)[0]
 
@@ -296,34 +319,51 @@
     stage = pltpu.VMEM((rows, 2, nodes), BF16)
     parted = pltpu.VMEM((nodes // LANES, 2 * rows, LANES), F32)
     ordering = [column, stage, stage, selector, parted, parted]
-    first, own_inner, own = call(
+    (both,) = call(
+        order_cross,
+        [bf16(2, rows, nodes)],
+        [
+            column,
+            stage,
+            stage,
+            pltpu.VMEM((nodes, half), BF16),
+            pltpu.VMEM((2, half // LANES, 2 * rows, LANES), F32),
+        ],
+        3,
+        int(1e9),
+        column_source,
+        boundary,
+        grant=62,
+    )
+    both_far = exchange(both, "tile", 2)
+    first, own_inner = call(
         order_first,
-        [bf16(2, rows, nodes), bf16(2, rows, half), bf16(2, rows, half)],
+        [bf16(2, rows, nodes), bf16(2, rows, half)],
         ordering,
         3,
         int(2e9),
-        column_source,
+        after(column_source, both),
         boundary,
-        grant=62,
+        grant=61,
     )
     got = exchange(first, "cluster", 1)
-    own_far = exchange(own, "tile", 2)
     outer, keep = call(
         order_second,
         [bf16(2, rows, nodes), bf16(2, rows, nodes)],
         ordering,
         3,
         int(2e9),
-        after(column_source, own),
+        after(column_source, own_inner),
         boundary,
+        grant=40,
     )
     outer_got = exchange(after(outer, got), "cluster", 1)
-    mixed = jnp.concatenate([total_of(own_inner, got[..., :half]), got[..., half:]], axis=2)
+    mixed = total_of(own_inner, got[..., :half])
     mixed_far = exchange(mixed, "tile", 2)
-    owns = [own, own_far]
-    owns += [exchange(own, "tile", 1), exchange(own_far, "tile", 1)]
-    mixes = [mixed, mixed_far]
-    mixes += [exchange(mixed, "tile", 1), exchange(mixed_far, "tile", 1)]
+    both_far_other = exchange(both_far[..., half:], "cluster", 1)
+
+    def with_core(x, y):
+        return [x, y, exchange(x, "tile", 1), exchange(y, "tile", 1)]
 
     square = pltpu.VMEM((2, half, half), BF16)
     squares = pltpu.VMEM((2, 2, half, half), BF16)
@@ -334,8 +374,9 @@
         [square, square, squares, rim, rim],
         16,
         int(2.7e9),
-        *owns,
-        *mixes,
+        *with_core(mixed, mixed_far),
+        *with_core(both, both_far),
+        *with_core(got, both_far_other),
         keep,
         outer_got,
     )
@@ -345,9 +386,6 @@
     summed_far = exchange(summed, "tile", 2)
     cross_other = exchange(after(cross, summed), "cluster", 2)
     cross_far_other = exchange(cross_far, "cluster", 2)
-
-    def with_core(x, y):
-        return [x, y, exchange(x, "tile", 1), exchange(y, "tile", 1)]
 
     kept, sent, diagonal = call(
         last_level,
@@ -365,14 +403,14 @@
         in_smem=(14,),
     )
     density = diagonal + exchange(diagonal, "cluster", 1)
-    got_rows = exchange(sent, "cluster", 1).astype(F32)
-    for distance in (1, 2):
-        density = density + exchange(density, "energy", distance)
+    got_rows = exchange(sent, "cluster", 1)
+    parts = [exchange(density, "energy", distance) for distance in (1, 2, 3)]
+    density = density + parts[0] + parts[1] + parts[2]
     density = jnp.where(side == 0, density[:, :few], density[:, few:])
-    low = jnp.where(side == 0, kept, got_rows)
-    high = jnp.where(side == 0, got_rows, kept)
-    final_rows = jnp.stack([low, high]).transpose(2, 0, 1, 3)
-    return final_rows[None], density
+    (final_rows,) = call(
+        finish, [f32(1, few, 2, 2, nodes)], [], 1, int(1e6), kept, got_rows, in_vmem=(0, 1)
+    )
+    return final_rows, density
 
 
 def solution(mesh):

time: 126 us -> 119 us (0.944)
  waiting for transfers between devices: 72.2 us -> 52.3 us
  starting transfers between devices: 34.7 us -> 40.9 us
  Pallas kernels: 14.2 us -> 18 us
  local copies, waits for them, and re-layouts: 1.82 us -> 5.34 us
    ppermute x23 -> x27, waiting for transfers between devices: 72.2 us -> 52.3 us  [exchange(): lax.ppermute(x, axis, [(i, i ^ distance) for i in range(lax.axis_size(axi...]
    ppermute x23 -> x27, starting transfers between devices: 34.7 us -> 40.9 us  [exchange(): lax.ppermute(x, axis, [(i, i ^ distance) for i in range(lax.axis_size(axi...]
    pallas_call x4 -> x6, Pallas kernels: 14.2 us -> 18 us  [call(): pl.pallas_call(body, out_shape=out_shape, in_specs=[pl.BlockSpec(memory_s...]
    unnamed x9 -> x24, local copies, waits for them, and re-layouts: 1.8 us -> 5.32 us
  transfers between devices with their start and end apart: 23 -> 27, of which waited for: 11 -> 11; matrix products, arithmetic and copies ran while one was open for 1% -> 1% of each run, Pallas kernels for 2% -> 2%
where the time goes in v4:
time: 119 us
  waiting for transfers between devices  52.3 us (44%)
  starting transfers between devices  40.9 us (34%)
  Pallas kernels  18 us (15%)
  local copies, waits for them, and re-layouts  5.34 us (4%)
  other arithmetic  1.68 us (1%)
    ppermute x27, waiting for transfers between devices, exchange(): lax.ppermute(x, axis, [(i, i ^ distance) for i in range(lax.axis_size(axi...  52.3 us
    ppermute x27, starting transfers between devices, exchange(): lax.ppermute(x, axis, [(i, i ^ distance) for i in range(lax.axis_size(axi...  40.9 us
    pallas_call x6, Pallas kernels, call(): pl.pallas_call(body, out_shape=out_shape, in_specs=[pl.BlockSpec(memory_s...  18 us
    unnamed x24, local copies, waits for them, and re-layouts  5.32 us
  transfers between devices with their start and end apart: 27, of which 11 were waited for; matrix products, arithmetic and copies ran while one was open for 1% of the time, Pallas kernels for 2%

profile of v4, /device:TPU:2, one launch (start us, length us, event | category | flops | bytes accessed | tf_op | source)
XLA Modules:
  0.0 119.2 jit_solution(5852811359950027092)
XLA Ops:
  0.6 2.8 %shard_map.50.refs_4_ = bf16[2,128,1024]{2,1,0:T(8,128)(2,1)} custom-call(s32[1,1024]{1,0:T(1,128)} %column_ref.3, bf16[1,2,128,2,2,1024]{5,4,3,2,1,0:T(2,128)(2,1)} %raw.5), custom_call_target="tpu_custom_call" | custom-call | flops 1000000000 | bytes 4194304 | tf_op jit(solution)/shard_map/pallas_call | solution.py:63
  3.5 3.6 %shard_map.51 = (bf16[2,128,1024]{2,1,0:T(8,128)(2,1)}, bf16[2,128,512]{2,1,0:T(8,128)(2,1)}) custom-call(s32[1,1024]{1,0:T(1,128)} %column_ref.3, bf16[1,2,128,2,2,1024]{5,4,3,2,1,0:T(2,128)(2,1)} %raw.5), custom_call_target="tpu_custom_call" | custom-call | flops 2000000000 | bytes 4194304 | tf_op jit(solution)/shard_map/pallas_call | solution.py:63
  7.1 1.7 %collective-permute-start = (bf16[2,128,1024]{2,1,0:T(8,128)(2,1)}, bf16[2,128,1024]{2,1,0:T(8,128)(2,1)S(1)}, u32[]{:S(2)}, u32[]{:S(2)}) collective-permute-start(bf16[2,128,1024]{2,1,0:T(8,128)(2,1)} %get-tuple-element.19), channel_id=1, source_target_pairs={{0,4},{4,0},{8,12},{12,8},{16,20},{20,16},{24,28},{28,24},{32,36},... | collective-permute-start | bytes 1572872 | tf_op jit(solution)/shard_map/ppermute | solution.py:15
  8.8 7.2 %collective-permute-start.4 = (bf16[2,128,1024]{2,1,0:T(8,128)(2,1)S(1)}, bf16[2,128,1024]{2,1,0:T(8,128)(2,1)S(1)}, u32[]{:S(2)}, u32[]{:S(2)}) collective-permute-start(bf16[2,128,1024]{2,1,0:T(8,128)(2,1)S(1)} %copy-done.1), channel_id=1, source_target_pairs={{0,2},{1,3},{2,0},{3,1},{4,6},{5,7},{6,4},{7,5},{8,10},{9,11},{10,... | collective-permute-start | bytes 1572872 | tf_op jit(solution)/shard_map/ppermute | solution.py:15
  16.0 5.1 %collective-permute-done.refs_8_ = bf16[2,128,1024]{2,1,0:T(8,128)(2,1)S(1)} collective-permute-done((bf16[2,128,1024]{2,1,0:T(8,128)(2,1)}, bf16[2,128,1024]{2,1,0:T(8,128)(2,1)S(1)}, u32[]{:S(2)}, u32[]{:S(2)}) %collective-permute-start) | collective-permute-done | bytes 524320 | tf_op jit(solution)/shard_map/ppermute | solution.py:15
  22.1 7.3 %collective-permute-start.1 = (bf16[2,128,512]{2,1,0:T(8,128)(2,1)S(1)}, bf16[2,128,512]{2,1,0:T(8,128)(2,1)S(1)}, u32[]{:S(2)}, u32[]{:S(2)}) collective-permute-start(bf16[2,128,512]{2,1,0:T(8,128)(2,1)S(1)} %add_convert_fusion.1.refs_0_), channel_id=1, source_target_pairs={{0,2},{1,3},{2,0},{3,1},{4,6},{5,7},{6,4},{7,5},{8,10},{9,11},{10,... | collective-permute-start | bytes 786440 | tf_op jit(solution)/shard_map/ppermute | solution.py:15
  29.4 2.3 %shard_map.52 = (bf16[2,128,1024]{2,1,0:T(8,128)(2,1)S(1)}, bf16[2,128,1024]{2,1,0:T(8,128)(2,1)S(1)}) custom-call(s32[1,1024]{1,0:T(1,128)S(1)} %copy-done.6, bf16[1,2,128,2,2,1024]{5,4,3,2,1,0:T(2,128)(2,1)S(1)} %copy-done), custom_call_target="tpu_custom_call" | custom-call | flops 2000000000 | bytes 4194304 | tf_op jit(solution)/shard_map/pallas_call | solution.py:63
  31.8 1.6 %collective-permute-start.10 = (bf16[2,128,1024]{2,1,0:T(8,128)(2,1)S(1)}, bf16[2,128,1024]{2,1,0:T(8,128)(2,1)S(1)}, u32[]{:S(2)}, u32[]{:S(2)}) collective-permute-start(bf16[2,128,1024]{2,1,0:T(8,128)(2,1)S(1)} %get-tuple-element.23), channel_id=1, source_target_pairs={{0,4},{4,0},{8,12},{12,8},{16,20},{20,16},{24,28},{28,24},{32,36},... | collective-permute-start | bytes 1572872 | tf_op jit(solution)/shard_map/ppermute | solution.py:15
  34.0 14.7 %collective-permute-done.1.refs_1_ = bf16[2,128,512]{2,1,0:T(8,128)(2,1)S(1)} collective-permute-done((bf16[2,128,512]{2,1,0:T(8,128)(2,1)S(1)}, bf16[2,128,512]{2,1,0:T(8,128)(2,1)S(1)}, u32[]{:S(2)}, u32[]{:S(2)}) %collective-permute-start.1) | collective-permute-done | bytes 262176 | tf_op jit(solution)/shard_map/ppermute | solution.py:15
  49.3 2.5 %collective-permute-done.7.refs_9_ = bf16[2,128,512]{2,1,0:T(8,128)(2,1)S(1)} collective-permute-done((bf16[2,128,512]{2,1,0:T(8,128)(2,1)S(1)}, bf16[2,128,512]{2,1,0:T(8,128)(2,1)S(1)}, u32[]{:S(2)}, u32[]{:S(2)}) %collective-permute-start.7) | collective-permute-done | bytes 262176 | tf_op jit(solution)/shard_map/ppermute | solution.py:15
  51.8 1.5 %collective-permute-done.9.refs_11_ = bf16[2,128,512]{2,1,0:T(8,128)(2,1)S(1)} collective-permute-done((bf16[2,128,512]{2,1,0:T(8,128)(2,1)S(1)}, bf16[2,128,512]{2,1,0:T(8,128)(2,1)S(1)}, u32[]{:S(2)}, u32[]{:S(2)}) %collective-permute-start.9) | collective-permute-done | bytes 262176 | tf_op jit(solution)/shard_map/ppermute | solution.py:15
  53.3 4.5 %shard_map.53 = (bf16[2,128,512]{2,1,0:T(8,128)(2,1)S(1)}, bf16[2,128,512]{2,1,0:T(8,128)(2,1)S(1)}, bf16[2,128,512]{2,1,0:T(8,128)(2,1)S(1)}, f32[2,128,512]{2,1,0:T(8,128)S(1)}) custom-call(bf16[2,128,512]{2,1,0:T(8,128)(2,1)S(1)} %add_convert_fusion.1.refs_0_, bf16[2,128,512]{2,1,0:T(8,128)(2,1)S(1)} %collective-permute-done.1.refs_1_, ...), custom_call_target="tpu_custom_call" | custom-call | flops 2700000000 | bytes 4194304 | tf_op jit(solution)/shard_map/pallas_call | solution.py:63
  57.8 3.3 %collective-permute-start.11 = (bf16[2,128,512]{2,1,0:T(8,128)(2,1)S(1)}, bf16[2,128,512]{2,1,0:T(8,128)(2,1)S(1)}, u32[]{:S(2)}, u32[]{:S(2)}) collective-permute-start(bf16[2,128,512]{2,1,0:T(8,128)(2,1)S(1)} %get-tuple-element.24), channel_id=1, source_target_pairs={{0,8},{4,12},{8,0},{12,4},{16,24},{20,28},{24,16},{28,20},{32,40},... | collective-permute-start | bytes 786440 | tf_op jit(solution)/shard_map/ppermute | solution.py:15
  61.1 4.3 %collective-permute-start.15 = (bf16[2,128,512]{2,1,0:T(8,128)(2,1)S(1)}, bf16[2,128,512]{2,1,0:T(8,128)(2,1)S(1)}, u32[]{:S(2)}, u32[]{:S(2)}) collective-permute-start(bf16[2,128,512]{2,1,0:T(8,128)(2,1)S(1)} %get-tuple-element.26.refs_4_), channel_id=1, source_target_pairs={{0,2},{1,3},{2,0},{3,1},{4,6},{5,7},{6,4},{7,5},{8,10},{9,11},{10,... | collective-permute-start | bytes 786440 | tf_op jit(solution)/shard_map/ppermute | solution.py:15
  65.4 2.4 %collective-permute-done.11 = bf16[2,128,512]{2,1,0:T(8,128)(2,1)S(1)} collective-permute-done((bf16[2,128,512]{2,1,0:T(8,128)(2,1)S(1)}, bf16[2,128,512]{2,1,0:T(8,128)(2,1)S(1)}, u32[]{:S(2)}, u32[]{:S(2)}) %collective-permute-start.11) | collective-permute-done | bytes 262176 | tf_op jit(solution)/shard_map/ppermute | solution.py:15
  67.8 3.3 %collective-permute-start.18 = (bf16[2,128,512]{2,1,0:T(8,128)(2,1)S(1)}, bf16[2,128,512]{2,1,0:T(8,128)(2,1)S(1)}, u32[]{:S(2)}, u32[]{:S(2)}) collective-permute-start(bf16[2,128,512]{2,1,0:T(8,128)(2,1)S(1)} %get-tuple-element.26.refs_4_), channel_id=1, source_target_pairs={{0,8},{4,12},{8,0},{12,4},{16,24},{20,28},{24,16},{28,20},{32,40},... | collective-permute-start | bytes 786440 | tf_op jit(solution)/shard_map/ppermute | solution.py:15
  71.1 4.3 %collective-permute-start.12 = (bf16[2,128,512]{2,1,0:T(8,128)(2,1)S(1)}, bf16[2,128,512]{2,1,0:T(8,128)(2,1)S(1)}, u32[]{:S(2)}, u32[]{:S(2)}) collective-permute-start(bf16[2,128,512]{2,1,0:T(8,128)(2,1)S(1)} %add_convert_fusion.refs_0_), channel_id=1, source_target_pairs={{0,2},{1,3},{2,0},{3,1},{4,6},{5,7},{6,4},{7,5},{8,10},{9,11},{10,... | collective-permute-start | bytes 786440 | tf_op jit(solution)/shard_map/ppermute | solution.py:15
  77.4 15.4 %collective-permute-done.12.refs_1_ = bf16[2,128,512]{2,1,0:T(8,128)(2,1)S(1)} collective-permute-done((bf16[2,128,512]{2,1,0:T(8,128)(2,1)S(1)}, bf16[2,128,512]{2,1,0:T(8,128)(2,1)S(1)}, u32[]{:S(2)}, u32[]{:S(2)}) %collective-permute-start.12) | collective-permute-done | bytes 262176 | tf_op jit(solution)/shard_map/ppermute | solution.py:15
  99.6 3.6 %shard_map.54 = (f32[2,64,1024]{2,1,0:T(8,128)S(1)}, bf16[2,64,1024]{2,1,0:T(8,128)(2,1)S(1)}, f32[1,128]{1,0:T(1,128)S(1)}) custom-call(bf16[2,128,512]{2,1,0:T(8,128)(2,1)S(1)} %add_convert_fusion.refs_0_, bf16[2,128,512]{2,1,0:T(8,128)(2,1)S(1)} %collective-permute-done.12.refs_1_, bf16[2,128,512]{2,1,0:T(8,128)(2,1)S(1)} %collective-permute-done.13.refs_2_, ...), custom_call_target="tpu_custom_call" | custom-call | flops 1400000000 | bytes 4194304 | tf_op jit(solution)/shard_map/pallas_call | solution.py:63
  103.8 3.3 %collective-permute-done.23 = f32[1,128]{1,0:T(1,128)S(1)} collective-permute-done((f32[1,128]{1,0:T(1,128)S(1)}, f32[1,128]{1,0:T(1,128)S(1)}, u32[]{:S(2)}, u32[]{:S(2)}) %collective-permute-start.23) | collective-permute-done | bytes 544 | tf_op jit(solution)/shard_map/ppermute | solution.py:15
  107.1 2.5 %collective-permute-start.25 = (f32[1,128]{1,0:T(1,128)S(1)}, f32[1,128]{1,0:T(1,128)S(1)}, u32[]{:S(2)}, u32[]{:S(2)}) collective-permute-start(f32[1,128]{1,0:T(1,128)S(1)} %add.25), channel_id=1, source_target_pairs={{0,128},{64,192},{128,0},{192,64},{1,129},{65,193},{129,1},{193,65... | collective-permute-start | bytes 1544 | tf_op jit(solution)/shard_map/ppermute | solution.py:15
  109.6 1.9 %collective-permute-start.26 = (f32[1,128]{1,0:T(1,128)S(1)}, f32[1,128]{1,0:T(1,128)S(1)}, u32[]{:S(2)}, u32[]{:S(2)}) collective-permute-start(f32[1,128]{1,0:T(1,128)S(1)} %add.25), channel_id=1, source_target_pairs={{0,192},{64,128},{128,64},{192,0},{1,193},{65,129},{129,65},{193,1... | collective-permute-start | bytes 1544 | tf_op jit(solution)/shard_map/ppermute | solution.py:15
  111.8 3.2 %collective-permute-done.26 = f32[1,128]{1,0:T(1,128)S(1)} collective-permute-done((f32[1,128]{1,0:T(1,128)S(1)}, f32[1,128]{1,0:T(1,128)S(1)}, u32[]{:S(2)}, u32[]{:S(2)}) %collective-permute-start.26) | collective-permute-done | bytes 544 | tf_op jit(solution)/shard_map/ppermute | solution.py:15
  115.6 2.3 %collective-permute-done.22.got = bf16[2,64,1024]{2,1,0:T(8,128)(2,1)S(1)} collective-permute-done((bf16[2,64,1024]{2,1,0:T(8,128)(2,1)S(1)}, bf16[2,64,1024]{2,1,0:T(8,128)(2,1)S(1)}, u32[]{:S(2)}, u32[]{:S(2)}) %collective-permute-start.22) | collective-permute-done | bytes 262176 | tf_op jit(solution)/shard_map/ppermute | solution.py:15
  (66 shorter events, 13.8 us)
Async XLA Ops:
  7.1 14.0 %collective-permute-start = (bf16[2,128,1024]{2,1,0:T(8,128)(2,1)}, bf16[2,128,1024]{2,1,0:T(8,128)(2,1)S(1)}, u32[]{:S(2)}, u32[]{:S(2)}) collective-permute-start(bf16[2,128,1024]{2,1,0:T(8,128)(2,1)} %get-tuple-element.19), channel_id=1, source_target_pairs={{0,4},{4,0},{8,12},{12,8},{16,20},{20,16},{24,28},{28,24},{32,36},... | collective-permute-start | bytes 1572872 | tf_op jit(solution)/shard_map/ppermute | solution.py:15
  8.8 24.7 %collective-permute-start.4 = (bf16[2,128,1024]{2,1,0:T(8,128)(2,1)S(1)}, bf16[2,128,1024]{2,1,0:T(8,128)(2,1)S(1)}, u32[]{:S(2)}, u32[]{:S(2)}) collective-permute-start(bf16[2,128,1024]{2,1,0:T(8,128)(2,1)S(1)} %copy-done.1), channel_id=1, source_target_pairs={{0,2},{1,3},{2,0},{3,1},{4,6},{5,7},{6,4},{7,5},{8,10},{9,11},{10,... | collective-permute-start | bytes 1572872 | tf_op jit(solution)/shard_map/ppermute | solution.py:15
  15.9 18.1 %collective-permute-start.5 = (bf16[2,128,1024]{2,1,0:T(8,128)(2,1)S(1)}, bf16[2,128,1024]{2,1,0:T(8,128)(2,1)S(1)}, u32[]{:S(2)}, u32[]{:S(2)}) collective-permute-start(bf16[2,128,1024]{2,1,0:T(8,128)(2,1)S(1)} %copy-done.1), channel_id=1, source_target_pairs={{0,1},{1,0},{2,3},{3,2},{4,5},{5,4},{6,7},{7,6},{8,9},{9,8},{10,11... | collective-permute-start | bytes 1572872 | tf_op jit(solution)/shard_map/ppermute | solution.py:15
  22.1 26.7 %collective-permute-start.1 = (bf16[2,128,512]{2,1,0:T(8,128)(2,1)S(1)}, bf16[2,128,512]{2,1,0:T(8,128)(2,1)S(1)}, u32[]{:S(2)}, u32[]{:S(2)}) collective-permute-start(bf16[2,128,512]{2,1,0:T(8,128)(2,1)S(1)} %add_convert_fusion.1.refs_0_), channel_id=1, source_target_pairs={{0,2},{1,3},{2,0},{3,1},{4,6},{5,7},{6,4},{7,5},{8,10},{9,11},{10,... | collective-permute-start | bytes 786440 | tf_op jit(solution)/shard_map/ppermute | solution.py:15
  31.7 17.0 %collective-permute-start.2 = (bf16[2,128,512]{2,1,0:T(8,128)(2,1)S(1)}, bf16[2,128,512]{2,1,0:T(8,128)(2,1)S(1)}, u32[]{:S(2)}, u32[]{:S(2)}) collective-permute-start(bf16[2,128,512]{2,1,0:T(8,128)(2,1)S(1)} %add_convert_fusion.1.refs_0_), channel_id=1, source_target_pairs={{0,1},{1,0},{2,3},{3,2},{4,5},{5,4},{6,7},{7,6},{8,9},{9,8},{10,11... | collective-permute-start | bytes 786440 | tf_op jit(solution)/shard_map/ppermute | solution.py:15
  31.8 20.0 %collective-permute-start.10 = (bf16[2,128,1024]{2,1,0:T(8,128)(2,1)S(1)}, bf16[2,128,1024]{2,1,0:T(8,128)(2,1)S(1)}, u32[]{:S(2)}, u32[]{:S(2)}) collective-permute-start(bf16[2,128,1024]{2,1,0:T(8,128)(2,1)S(1)} %get-tuple-element.23), channel_id=1, source_target_pairs={{0,4},{4,0},{8,12},{12,8},{16,20},{20,16},{24,28},{28,24},{32,36},... | collective-permute-start | bytes 1572872 | tf_op jit(solution)/shard_map/ppermute | solution.py:15
  33.5 18.3 %collective-permute-start.7 = (bf16[2,128,512]{2,1,0:T(8,128)(2,1)S(1)}, bf16[2,128,512]{2,1,0:T(8,128)(2,1)S(1)}, u32[]{:S(2)}, u32[]{:S(2)}) collective-permute-start(bf16[2,128,512]{2,1,0:T(8,128)(2,1)S(1)} %slice.17), channel_id=1, source_target_pairs={{0,4},{4,0},{8,12},{12,8},{16,20},{20,16},{24,28},{28,24},{32,36},... | collective-permute-start | bytes 786440 | tf_op jit(solution)/shard_map/ppermute | solution.py:15
  34.0 17.7 %collective-permute-start.8 = (bf16[2,128,1024]{2,1,0:T(8,128)(2,1)S(1)}, bf16[2,128,1024]{2,1,0:T(8,128)(2,1)S(1)}, u32[]{:S(2)}, u32[]{:S(2)}) collective-permute-start(bf16[2,128,1024]{2,1,0:T(8,128)(2,1)S(1)} %collective-permute-done.refs_8_), channel_id=1, source_target_pairs={{0,1},{1,0},{2,3},{3,2},{4,5},{5,4},{6,7},{7,6},{8,9},{9,8},{10,11... | collective-permute-start | bytes 1572872 | tf_op jit(solution)/shard_map/ppermute | solution.py:15
  48.8 4.5 %collective-permute-start.6 = (bf16[2,128,1024]{2,1,0:T(8,128)(2,1)S(1)}, bf16[2,128,1024]{2,1,0:T(8,128)(2,1)S(1)}, u32[]{:S(2)}, u32[]{:S(2)}) collective-permute-start(bf16[2,128,1024]{2,1,0:T(8,128)(2,1)S(1)} %collective-permute-done.4.refs_5_), channel_id=1, source_target_pairs={{0,1},{1,0},{2,3},{3,2},{4,5},{5,4},{6,7},{7,6},{8,9},{9,8},{10,11... | collective-permute-start | bytes 1572872 | tf_op jit(solution)/shard_map/ppermute | solution.py:15
  48.8 3.0 %collective-permute-start.3 = (bf16[2,128,512]{2,1,0:T(8,128)(2,1)S(1)}, bf16[2,128,512]{2,1,0:T(8,128)(2,1)S(1)}, u32[]{:S(2)}, u32[]{:S(2)}) collective-permute-start(bf16[2,128,512]{2,1,0:T(8,128)(2,1)S(1)} %collective-permute-done.1.refs_1_), channel_id=1, source_target_pairs={{0,1},{1,0},{2,3},{3,2},{4,5},{5,4},{6,7},{7,6},{8,9},{9,8},{10,11... | collective-permute-start | bytes 786440 | tf_op jit(solution)/shard_map/ppermute | solution.py:15
  57.8 9.9 %collective-permute-start.11 = (bf16[2,128,512]{2,1,0:T(8,128)(2,1)S(1)}, bf16[2,128,512]{2,1,0:T(8,128)(2,1)S(1)}, u32[]{:S(2)}, u32[]{:S(2)}) collective-permute-start(bf16[2,128,512]{2,1,0:T(8,128)(2,1)S(1)} %get-tuple-element.24), channel_id=1, source_target_pairs={{0,8},{4,12},{8,0},{12,4},{16,24},{20,28},{24,16},{28,20},{32,40},... | collective-permute-start | bytes 786440 | tf_op jit(solution)/shard_map/ppermute | solution.py:15
  61.1 14.3 %collective-permute-start.15 = (bf16[2,128,512]{2,1,0:T(8,128)(2,1)S(1)}, bf16[2,128,512]{2,1,0:T(8,128)(2,1)S(1)}, u32[]{:S(2)}, u32[]{:S(2)}) collective-permute-start(bf16[2,128,512]{2,1,0:T(8,128)(2,1)S(1)} %get-tuple-element.26.refs_4_), channel_id=1, source_target_pairs={{0,2},{1,3},{2,0},{3,1},{4,6},{5,7},{6,4},{7,5},{8,10},{9,11},{10,... | collective-permute-start | bytes 786440 | tf_op jit(solution)/shard_map/ppermute | solution.py:15
  65.4 10.7 %collective-permute-start.16 = (bf16[2,128,512]{2,1,0:T(8,128)(2,1)S(1)}, bf16[2,128,512]{2,1,0:T(8,128)(2,1)S(1)}, u32[]{:S(2)}, u32[]{:S(2)}) collective-permute-start(bf16[2,128,512]{2,1,0:T(8,128)(2,1)S(1)} %get-tuple-element.26.refs_4_), channel_id=1, source_target_pairs={{0,1},{1,0},{2,3},{3,2},{4,5},{5,4},{6,7},{7,6},{8,9},{9,8},{10,11... | collective-permute-start | bytes 786440 | tf_op jit(solution)/shard_map/ppermute | solution.py:15
  67.8 9.6 %collective-permute-start.18 = (bf16[2,128,512]{2,1,0:T(8,128)(2,1)S(1)}, bf16[2,128,512]{2,1,0:T(8,128)(2,1)S(1)}, u32[]{:S(2)}, u32[]{:S(2)}) collective-permute-start(bf16[2,128,512]{2,1,0:T(8,128)(2,1)S(1)} %get-tuple-element.26.refs_4_), channel_id=1, source_target_pairs={{0,8},{4,12},{8,0},{12,4},{16,24},{20,28},{24,16},{28,20},{32,40},... | collective-permute-start | bytes 786440 | tf_op jit(solution)/shard_map/ppermute | solution.py:15
  71.1 21.6 %collective-permute-start.12 = (bf16[2,128,512]{2,1,0:T(8,128)(2,1)S(1)}, bf16[2,128,512]{2,1,0:T(8,128)(2,1)S(1)}, u32[]{:S(2)}, u32[]{:S(2)}) collective-permute-start(bf16[2,128,512]{2,1,0:T(8,128)(2,1)S(1)} %add_convert_fusion.refs_0_), channel_id=1, source_target_pairs={{0,2},{1,3},{2,0},{3,1},{4,6},{5,7},{6,4},{7,5},{8,10},{9,11},{10,... | collective-permute-start | bytes 786440 | tf_op jit(solution)/shard_map/ppermute | solution.py:15
  75.4 17.4 %collective-permute-start.19 = (bf16[2,128,512]{2,1,0:T(8,128)(2,1)S(1)}, bf16[2,128,512]{2,1,0:T(8,128)(2,1)S(1)}, u32[]{:S(2)}, u32[]{:S(2)}) collective-permute-start(bf16[2,128,512]{2,1,0:T(8,128)(2,1)S(1)} %collective-permute-done.15.refs_5_), channel_id=1, source_target_pairs={{0,8},{4,12},{8,0},{12,4},{16,24},{20,28},{24,16},{28,20},{32,40},... | collective-permute-start | bytes 786440 | tf_op jit(solution)/shard_map/ppermute | solution.py:15
  76.0 17.3 %collective-permute-start.13 = (bf16[2,128,512]{2,1,0:T(8,128)(2,1)S(1)}, bf16[2,128,512]{2,1,0:T(8,128)(2,1)S(1)}, u32[]{:S(2)}, u32[]{:S(2)}) collective-permute-start(bf16[2,128,512]{2,1,0:T(8,128)(2,1)S(1)} %add_convert_fusion.refs_0_), channel_id=1, source_target_pairs={{0,1},{1,0},{2,3},{3,2},{4,5},{5,4},{6,7},{7,6},{8,9},{9,8},{10,11... | collective-permute-start | bytes 786440 | tf_op jit(solution)/shard_map/ppermute | solution.py:15
  76.0 17.3 %collective-permute-start.17 = (bf16[2,128,512]{2,1,0:T(8,128)(2,1)S(1)}, bf16[2,128,512]{2,1,0:T(8,128)(2,1)S(1)}, u32[]{:S(2)}, u32[]{:S(2)}) collective-permute-start(bf16[2,128,512]{2,1,0:T(8,128)(2,1)S(1)} %collective-permute-done.15.refs_5_), channel_id=1, source_target_pairs={{0,1},{1,0},{2,3},{3,2},{4,5},{5,4},{6,7},{7,6},{8,9},{9,8},{10,11... | collective-permute-start | bytes 786440 | tf_op jit(solution)/shard_map/ppermute | solution.py:15
  77.4 15.9 %collective-permute-start.20 = (bf16[2,128,512]{2,1,0:T(8,128)(2,1)S(1)}, bf16[2,128,512]{2,1,0:T(8,128)(2,1)S(1)}, u32[]{:S(2)}, u32[]{:S(2)}) collective-permute-start(bf16[2,128,512]{2,1,0:T(8,128)(2,1)S(1)} %collective-permute-done.18.refs_8_), channel_id=1, source_target_pairs={{0,1},{1,0},{2,3},{3,2},{4,5},{5,4},{6,7},{7,6},{8,9},{9,8},{10,11... | collective-permute-start | bytes 786440 | tf_op jit(solution)/shard_map/ppermute | solution.py:15
  103.2 3.9 %collective-permute-start.23 = (f32[1,128]{1,0:T(1,128)S(1)}, f32[1,128]{1,0:T(1,128)S(1)}, u32[]{:S(2)}, u32[]{:S(2)}) collective-permute-start(f32[1,128]{1,0:T(1,128)S(1)} %get-tuple-element.31), channel_id=1, source_target_pairs={{0,4},{4,0},{8,12},{12,8},{16,20},{20,16},{24,28},{28,24},{32,36},... | collective-permute-start | bytes 1544 | tf_op jit(solution)/shard_map/ppermute | solution.py:15
  107.1 4.7 %collective-permute-start.24 = (f32[1,128]{1,0:T(1,128)S(1)}, f32[1,128]{1,0:T(1,128)S(1)}, u32[]{:S(2)}, u32[]{:S(2)}) collective-permute-start(f32[1,128]{1,0:T(1,128)S(1)} %add.25), channel_id=1, source_target_pairs={{0,64},{64,0},{128,192},{192,128},{1,65},{65,1},{129,193},{193,129... | collective-permute-start | bytes 1544 | tf_op jit(solution)/shard_map/ppermute | solution.py:15
  107.1 4.7 %collective-permute-start.25 = (f32[1,128]{1,0:T(1,128)S(1)}, f32[1,128]{1,0:T(1,128)S(1)}, u32[]{:S(2)}, u32[]{:S(2)}) collective-permute-start(f32[1,128]{1,0:T(1,128)S(1)} %add.25), channel_id=1, source_target_pairs={{0,128},{64,192},{128,0},{192,64},{1,129},{65,193},{129,1},{193,65... | collective-permute-start | bytes 1544 | tf_op jit(solution)/shard_map/ppermute | solution.py:15
  109.6 5.4 %collective-permute-start.26 = (f32[1,128]{1,0:T(1,128)S(1)}, f32[1,128]{1,0:T(1,128)S(1)}, u32[]{:S(2)}, u32[]{:S(2)}) collective-permute-start(f32[1,128]{1,0:T(1,128)S(1)} %add.25), channel_id=1, source_target_pairs={{0,192},{64,128},{128,64},{192,0},{1,193},{65,129},{129,65},{193,1... | collective-permute-start | bytes 1544 | tf_op jit(solution)/shard_map/ppermute | solution.py:15
  111.5 6.4 %collective-permute-start.22 = (bf16[2,64,1024]{2,1,0:T(8,128)(2,1)S(1)}, bf16[2,64,1024]{2,1,0:T(8,128)(2,1)S(1)}, u32[]{:S(2)}, u32[]{:S(2)}) collective-permute-start(bf16[2,64,1024]{2,1,0:T(8,128)(2,1)S(1)} %get-tuple-element.30), channel_id=1, source_target_pairs={{0,4},{4,0},{8,12},{12,8},{16,20},{20,16},{24,28},{28,24},{32,36},... | collective-permute-start | bytes 786440 | tf_op jit(solution)/shard_map/ppermute | solution.py:15
  (15 other events, 180.5 us)

commit v5 on v4

--- a/solution.py
+++ b/solution.py
@@ -96,29 +96,24 @@
     return parted[block, pl.ds(2 * first + part, count, stride=2), :].astype(BF16)
 
 
-def order_cross(column_ref, raw, both_out, column, own_stage, other_stage, selector, parted, sems):
+def order_cross(column_ref, raw, other_out, column, stage, selector, parted, sems):
     side, _, _, _ = places()
     copies = Copies(sems)
     first = copies.start(column_ref, column)
-    owned = copies.start(raw.at[0, 0, :, side], own_stage)
-    other = copies.start(raw.at[0, 0, :, 1 - side], other_stage)
+    other = copies.start(raw.at[0, 0, :, 1 - side], stage)
     first.wait()
-    width = selector.shape[1]
-    fill_selector(column[:, width:], selector)
-    count = own_stage.shape[0]
-    for turn, (copy, stage) in enumerate(((owned, own_stage), (other, other_stage))):
-        copy.wait()
-        reorder(stage, selector, parted.at[turn])
-        for block in range(parted.shape[1]):
-            first_lane = turn * width + block * LANES
-            for part in range(2):
-                both_out[part, :, first_lane : first_lane + LANES] = lane_block(
-                    parted.at[turn], block, part, 0, count
-                )
+    fill_selector(column[:, selector.shape[1] :], selector)
+    other.wait()
+    reorder(stage, selector, parted)
+    for block in range(parted.shape[0]):
+        for part in range(2):
+            other_out[part, :, block * LANES : (block + 1) * LANES] = lane_block(
+                parted, block, part, 0, stage.shape[0]
+            )
 
 
 def order_first(
-    column_ref, raw, send_out, inner_out,
+    column_ref, raw, send_out, own_out,
     column, send_stage, own_stage, selector, send_parted, own_parted, sems,
 ):
     side, _, _, _ = places()
@@ -131,27 +126,31 @@
     sent.wait()
     reorder(send_stage, selector, send_parted)
     owned.wait()
-    reorder(own_stage, selector.at[:, : inner_out.shape[2]], own_parted)
+    reorder(own_stage, selector.at[:, own_out.shape[2] :], own_parted)
     count = send_stage.shape[0]
     for block in range(send_parted.shape[0]):
         lanes = slice(block * LANES, (block + 1) * LANES)
         for part in range(2):
             send_out[part, :, lanes] = lane_block(send_parted, block, part, 0, count)
-            if lanes.stop <= inner_out.shape[2]:
-                inner_out[part, :, lanes] = lane_block(own_parted, block, part, 0, count)
+            if lanes.stop <= own_out.shape[2]:
+                own_out[part, :, lanes] = lane_block(own_parted, block, part, 0, count)
 
 
 def order_second(
-    column_ref, raw, send_out, keep_out,
-    column, send_stage, own_stage, selector, send_parted, own_parted, sems,
+    column_ref, raw, send_out, keep_out, inner_out,
+    column, send_stage, own_stage, inner_stage, selector, send_parted, own_parted, inner_parted, sems,
 ):
     side, _, _, _ = places()
     copies = Copies(sems)
     first = copies.start(column_ref, column)
+    inner = copies.start(raw.at[0, 0, :, side], inner_stage)
     sent = copies.start(raw.at[0, 1, :, 1 - side], send_stage)
     owned = copies.start(raw.at[0, 1, :, side], own_stage)
     first.wait()
     fill_selector(column[...], selector)
+    inner.wait()
+    width = inner_out.shape[2]
+    reorder(inner_stage, selector.at[:, :width], inner_parted)
     sent.wait()
     reorder(send_stage, selector, send_parted)
     owned.wait()
@@ -162,6 +161,8 @@
         for part in range(2):
             send_out[part, :, lanes] = lane_block(send_parted, block, part, 0, count)
             keep_out[part, :, lanes] = lane_block(own_parted, block, part, 0, count)
+            if lanes.stop <= width:
+                inner_out[part, :, lanes] = lane_block(inner_parted, block, part, 0, count)
 
 
 def guess(interior, approx):
@@ -318,49 +319,47 @@
     column = pltpu.VMEM((1, nodes), jnp.int32)
     stage = pltpu.VMEM((rows, 2, nodes), BF16)
     parted = pltpu.VMEM((nodes // LANES, 2 * rows, LANES), F32)
-    ordering = [column, stage, stage, selector, parted, parted]
-    (both,) = call(
+    (other,) = call(
         order_cross,
-        [bf16(2, rows, nodes)],
+        [bf16(2, rows, half)],
         [
             column,
             stage,
-            stage,
             pltpu.VMEM((nodes, half), BF16),
-            pltpu.VMEM((2, half // LANES, 2 * rows, LANES), F32),
+            pltpu.VMEM((half // LANES, 2 * rows, LANES), F32),
         ],
-        3,
+        2,
         int(1e9),
         column_source,
         boundary,
         grant=62,
     )
-    both_far = exchange(both, "tile", 2)
-    first, own_inner = call(
+    other_far = exchange(other, "tile", 2)
+    first, own = call(
         order_first,
         [bf16(2, rows, nodes), bf16(2, rows, half)],
-        ordering,
+        [column, stage, stage, selector, parted, parted],
         3,
         int(2e9),
-        after(column_source, both),
+        after(column_source, other),
         boundary,
         grant=61,
     )
+    own_far = exchange(own, "tile", 2)
     got = exchange(first, "cluster", 1)
-    outer, keep = call(
+    outer, keep, own_inner = call(
         order_second,
-        [bf16(2, rows, nodes), bf16(2, rows, nodes)],
-        ordering,
-        3,
-        int(2e9),
-        after(column_source, own_inner),
+        [bf16(2, rows, nodes), bf16(2, rows, nodes), bf16(2, rows, half)],
+        [column, stage, stage, stage, selector, parted, parted, parted],
+        4,
+        int(3e9),
+        after(column_source, first),
         boundary,
-        grant=40,
     )
     outer_got = exchange(after(outer, got), "cluster", 1)
     mixed = total_of(own_inner, got[..., :half])
     mixed_far = exchange(mixed, "tile", 2)
-    both_far_other = exchange(both_far[..., half:], "cluster", 1)
+    sibling_far = exchange(other_far, "cluster", 1)
 
     def with_core(x, y):
         return [x, y, exchange(x, "tile", 1), exchange(y, "tile", 1)]
@@ -375,8 +374,8 @@
         16,
         int(2.7e9),
         *with_core(mixed, mixed_far),
-        *with_core(both, both_far),
-        *with_core(got, both_far_other),
+        *with_core(own, own_far),
+        *with_core(got, sibling_far),
         keep,
         outer_got,
     )

time: 119 us -> 119 us (level)
  starting transfers between devices: 40.9 us -> 51 us
  waiting for transfers between devices: 52.3 us -> 42.7 us
    ppermute x27 -> x28, starting transfers between devices: 40.9 us -> 51 us  [exchange(): lax.ppermute(x, axis, [(i, i ^ distance) for i in range(lax.axis_size(axi...]
    ppermute x27 -> x28, waiting for transfers between devices: 52.3 us -> 42.7 us  [exchange(): lax.ppermute(x, axis, [(i, i ^ distance) for i in range(lax.axis_size(axi...]
    unnamed x24 -> x26, local copies, waits for them, and re-layouts: 5.32 us -> 5.36 us
  transfers between devices with their start and end apart: 27 -> 28, of which waited for: 11 -> 11; matrix products, arithmetic and copies ran while one was open for 1% -> 1% of each run, Pallas kernels for 2% -> 2%
where the time goes in v5:
time: 119 us
  starting transfers between devices  51 us (43%)
  waiting for transfers between devices  42.7 us (36%)
  Pallas kernels  18 us (15%)
  local copies, waits for them, and re-layouts  5.36 us (5%)
    ppermute x28, starting transfers between devices, exchange(): lax.ppermute(x, axis, [(i, i ^ distance) for i in range(lax.axis_size(axi...  51 us
    ppermute x28, waiting for transfers between devices, exchange(): lax.ppermute(x, axis, [(i, i ^ distance) for i in range(lax.axis_size(axi...  42.7 us
    pallas_call x6, Pallas kernels, call(): pl.pallas_call(body, out_shape=out_shape, in_specs=[pl.BlockSpec(memory_s...  18 us
    unnamed x26, local copies, waits for them, and re-layouts  5.36 us
  transfers between devices with their start and end apart: 28, of which 11 were waited for; matrix products, arithmetic and copies ran while one was open for 1% of the time, Pallas kernels for 2%

profile of v5, /device:TPU:2, one launch (start us, length us, event | category | flops | bytes accessed | tf_op | source)
XLA Modules:
  0.0 118.7 jit_solution(2895173891535863961)
XLA Ops:
  0.6 2.3 %shard_map.50 = bf16[2,128,512]{2,1,0:T(8,128)(2,1)} custom-call(s32[1,1024]{1,0:T(1,128)} %column_ref.3, bf16[1,2,128,2,2,1024]{5,4,3,2,1,0:T(2,128)(2,1)} %raw.5), custom_call_target="tpu_custom_call" | custom-call | flops 1000000000 | bytes 4194304 | tf_op jit(solution)/shard_map/pallas_call | solution.py:63
  2.9 3.6 %shard_map.51 = (bf16[2,128,1024]{2,1,0:T(8,128)(2,1)}, bf16[2,128,512]{2,1,0:T(8,128)(2,1)}) custom-call(s32[1,1024]{1,0:T(1,128)} %column_ref.3, bf16[1,2,128,2,2,1024]{5,4,3,2,1,0:T(2,128)(2,1)} %raw.5), custom_call_target="tpu_custom_call" | custom-call | flops 2000000000 | bytes 4194304 | tf_op jit(solution)/shard_map/pallas_call | solution.py:63
  6.5 1.7 %collective-permute-start = (bf16[2,128,1024]{2,1,0:T(8,128)(2,1)}, bf16[2,128,1024]{2,1,0:T(8,128)(2,1)S(1)}, u32[]{:S(2)}, u32[]{:S(2)}) collective-permute-start(bf16[2,128,1024]{2,1,0:T(8,128)(2,1)} %get-tuple-element.19), channel_id=1, source_target_pairs={{0,4},{4,0},{8,12},{12,8},{16,20},{20,16},{24,28},{28,24},{32,36},... | collective-permute-start | bytes 1572872 | tf_op jit(solution)/shard_map/ppermute | solution.py:15
  8.2 7.2 %collective-permute-start.4 = (bf16[2,128,512]{2,1,0:T(8,128)(2,1)}, bf16[2,128,512]{2,1,0:T(8,128)(2,1)S(1)}, u32[]{:S(2)}, u32[]{:S(2)}) collective-permute-start(bf16[2,128,512]{2,1,0:T(8,128)(2,1)} %get-tuple-element.22.refs_4_), channel_id=1, source_target_pairs={{0,2},{1,3},{2,0},{3,1},{4,6},{5,7},{6,4},{7,5},{8,10},{9,11},{10,... | collective-permute-start | bytes 786440 | tf_op jit(solution)/shard_map/ppermute | solution.py:15
  15.5 2.9 %shard_map.52 = (bf16[2,128,1024]{2,1,0:T(8,128)(2,1)S(1)}, bf16[2,128,1024]{2,1,0:T(8,128)(2,1)S(1)}, bf16[2,128,512]{2,1,0:T(8,128)(2,1)S(1)}) custom-call(s32[1,1024]{1,0:T(1,128)S(1)} %copy-done.6, bf16[1,2,128,2,2,1024]{5,4,3,2,1,0:T(2,128)(2,1)S(1)} %copy-done), custom_call_target="tpu_custom_call" | custom-call | flops 3000000000 | bytes 4194304 | tf_op jit(solution)/shard_map/pallas_call | solution.py:63
  18.4 5.1 %collective-permute-done.4.refs_5_ = bf16[2,128,512]{2,1,0:T(8,128)(2,1)S(1)} collective-permute-done((bf16[2,128,512]{2,1,0:T(8,128)(2,1)}, bf16[2,128,512]{2,1,0:T(8,128)(2,1)S(1)}, u32[]{:S(2)}, u32[]{:S(2)}) %collective-permute-start.4) | collective-permute-done | bytes 262176 | tf_op jit(solution)/shard_map/ppermute | solution.py:15
  23.5 6.1 %collective-permute-done.7 = bf16[2,128,512]{2,1,0:T(8,128)(2,1)S(1)} collective-permute-done((bf16[2,128,512]{2,1,0:T(8,128)(2,1)S(1)}, bf16[2,128,512]{2,1,0:T(8,128)(2,1)S(1)}, u32[]{:S(2)}, u32[]{:S(2)}) %collective-permute-start.7) | collective-permute-done | bytes 262176 | tf_op jit(solution)/shard_map/ppermute | solution.py:15
  30.1 14.1 %collective-permute-start.1 = (bf16[2,128,512]{2,1,0:T(8,128)(2,1)S(1)}, bf16[2,128,512]{2,1,0:T(8,128)(2,1)S(1)}, u32[]{:S(2)}, u32[]{:S(2)}) collective-permute-start(bf16[2,128,512]{2,1,0:T(8,128)(2,1)S(1)} %add_convert_fusion.1.refs_0_), channel_id=1, source_target_pairs={{0,2},{1,3},{2,0},{3,1},{4,6},{5,7},{6,4},{7,5},{8,10},{9,11},{10,... | collective-permute-start | bytes 786440 | tf_op jit(solution)/shard_map/ppermute | solution.py:15
  44.2 1.6 %collective-permute-start.11 = (bf16[2,128,1024]{2,1,0:T(8,128)(2,1)S(1)}, bf16[2,128,1024]{2,1,0:T(8,128)(2,1)S(1)}, u32[]{:S(2)}, u32[]{:S(2)}) collective-permute-start(bf16[2,128,1024]{2,1,0:T(8,128)(2,1)S(1)} %get-tuple-element.25), channel_id=1, source_target_pairs={{0,4},{4,0},{8,12},{12,8},{16,20},{20,16},{24,28},{28,24},{32,36},... | collective-permute-start | bytes 1572872 | tf_op jit(solution)/shard_map/ppermute | solution.py:15
  46.3 7.1 %collective-permute-done.1.refs_1_ = bf16[2,128,512]{2,1,0:T(8,128)(2,1)S(1)} collective-permute-done((bf16[2,128,512]{2,1,0:T(8,128)(2,1)S(1)}, bf16[2,128,512]{2,1,0:T(8,128)(2,1)S(1)}, u32[]{:S(2)}, u32[]{:S(2)}) %collective-permute-start.1) | collective-permute-done | bytes 262176 | tf_op jit(solution)/shard_map/ppermute | solution.py:15
  53.4 1.5 %collective-permute-done.3.refs_3_ = bf16[2,128,512]{2,1,0:T(8,128)(2,1)S(1)} collective-permute-done((bf16[2,128,512]{2,1,0:T(8,128)(2,1)S(1)}, bf16[2,128,512]{2,1,0:T(8,128)(2,1)S(1)}, u32[]{:S(2)}, u32[]{:S(2)}) %collective-permute-start.3) | collective-permute-done | bytes 262176 | tf_op jit(solution)/shard_map/ppermute | solution.py:15
  55.0 4.5 %shard_map.53 = (bf16[2,128,512]{2,1,0:T(8,128)(2,1)S(1)}, bf16[2,128,512]{2,1,0:T(8,128)(2,1)S(1)}, bf16[2,128,512]{2,1,0:T(8,128)(2,1)S(1)}, f32[2,128,512]{2,1,0:T(8,128)S(1)}) custom-call(bf16[2,128,512]{2,1,0:T(8,128)(2,1)S(1)} %add_convert_fusion.1.refs_0_, bf16[2,128,512]{2,1,0:T(8,128)(2,1)S(1)} %collective-permute-done.1.refs_1_, ...), custom_call_target="tpu_custom_call" | custom-call | flops 2700000000 | bytes 4194304 | tf_op jit(solution)/shard_map/pallas_call | solution.py:63
  59.5 2.9 %collective-permute-start.12 = (bf16[2,128,512]{2,1,0:T(8,128)(2,1)S(1)}, bf16[2,128,512]{2,1,0:T(8,128)(2,1)S(1)}, u32[]{:S(2)}, u32[]{:S(2)}) collective-permute-start(bf16[2,128,512]{2,1,0:T(8,128)(2,1)S(1)} %get-tuple-element.26), channel_id=1, source_target_pairs={{0,8},{4,12},{8,0},{12,4},{16,24},{20,28},{24,16},{28,20},{32,40},... | collective-permute-start | bytes 786440 | tf_op jit(solution)/shard_map/ppermute | solution.py:15
  62.4 6.4 %collective-permute-start.16 = (bf16[2,128,512]{2,1,0:T(8,128)(2,1)S(1)}, bf16[2,128,512]{2,1,0:T(8,128)(2,1)S(1)}, u32[]{:S(2)}, u32[]{:S(2)}) collective-permute-start(bf16[2,128,512]{2,1,0:T(8,128)(2,1)S(1)} %get-tuple-element.28.refs_4_), channel_id=1, source_target_pairs={{0,2},{1,3},{2,0},{3,1},{4,6},{5,7},{6,4},{7,5},{8,10},{9,11},{10,... | collective-permute-start | bytes 786440 | tf_op jit(solution)/shard_map/ppermute | solution.py:15
  69.5 2.9 %collective-permute-start.19 = (bf16[2,128,512]{2,1,0:T(8,128)(2,1)S(1)}, bf16[2,128,512]{2,1,0:T(8,128)(2,1)S(1)}, u32[]{:S(2)}, u32[]{:S(2)}) collective-permute-start(bf16[2,128,512]{2,1,0:T(8,128)(2,1)S(1)} %get-tuple-element.28.refs_4_), channel_id=1, source_target_pairs={{0,8},{4,12},{8,0},{12,4},{16,24},{20,28},{24,16},{28,20},{32,40},... | collective-permute-start | bytes 786440 | tf_op jit(solution)/shard_map/ppermute | solution.py:15
  72.4 6.4 %collective-permute-start.13 = (bf16[2,128,512]{2,1,0:T(8,128)(2,1)S(1)}, bf16[2,128,512]{2,1,0:T(8,128)(2,1)S(1)}, u32[]{:S(2)}, u32[]{:S(2)}) collective-permute-start(bf16[2,128,512]{2,1,0:T(8,128)(2,1)S(1)} %add_convert_fusion.refs_0_), channel_id=1, source_target_pairs={{0,2},{1,3},{2,0},{3,1},{4,6},{5,7},{6,4},{7,5},{8,10},{9,11},{10,... | collective-permute-start | bytes 786440 | tf_op jit(solution)/shard_map/ppermute | solution.py:15
  80.2 12.1 %collective-permute-done.13.refs_1_ = bf16[2,128,512]{2,1,0:T(8,128)(2,1)S(1)} collective-permute-done((bf16[2,128,512]{2,1,0:T(8,128)(2,1)S(1)}, bf16[2,128,512]{2,1,0:T(8,128)(2,1)S(1)}, u32[]{:S(2)}, u32[]{:S(2)}) %collective-permute-start.13) | collective-permute-done | bytes 262176 | tf_op jit(solution)/shard_map/ppermute | solution.py:15
  99.1 3.6 %shard_map.54 = (f32[2,64,1024]{2,1,0:T(8,128)S(1)}, bf16[2,64,1024]{2,1,0:T(8,128)(2,1)S(1)}, f32[1,128]{1,0:T(1,128)S(1)}) custom-call(bf16[2,128,512]{2,1,0:T(8,128)(2,1)S(1)} %add_convert_fusion.refs_0_, bf16[2,128,512]{2,1,0:T(8,128)(2,1)S(1)} %collective-permute-done.13.refs_1_, bf16[2,128,512]{2,1,0:T(8,128)(2,1)S(1)} %collective-permute-done.14.refs_2_, ...), custom_call_target="tpu_custom_call" | custom-call | flops 1400000000 | bytes 4194304 | tf_op jit(solution)/shard_map/pallas_call | solution.py:63
  103.1 3.4 %collective-permute-done.24 = f32[1,128]{1,0:T(1,128)S(1)} collective-permute-done((f32[1,128]{1,0:T(1,128)S(1)}, f32[1,128]{1,0:T(1,128)S(1)}, u32[]{:S(2)}, u32[]{:S(2)}) %collective-permute-start.24) | collective-permute-done | bytes 544 | tf_op jit(solution)/shard_map/ppermute | solution.py:15
  106.6 1.3 %collective-permute-start.25 = (f32[1,128]{1,0:T(1,128)S(1)}, f32[1,128]{1,0:T(1,128)S(1)}, u32[]{:S(2)}, u32[]{:S(2)}) collective-permute-start(f32[1,128]{1,0:T(1,128)S(1)} %add.25), channel_id=1, source_target_pairs={{0,64},{64,0},{128,192},{192,128},{1,65},{65,1},{129,193},{193,129... | collective-permute-start | bytes 1544 | tf_op jit(solution)/shard_map/ppermute | solution.py:15
  108.4 2.6 %collective-permute-start.27 = (f32[1,128]{1,0:T(1,128)S(1)}, f32[1,128]{1,0:T(1,128)S(1)}, u32[]{:S(2)}, u32[]{:S(2)}) collective-permute-start(f32[1,128]{1,0:T(1,128)S(1)} %add.25), channel_id=1, source_target_pairs={{0,192},{64,128},{128,64},{192,0},{1,193},{65,129},{129,65},{193,1... | collective-permute-start | bytes 1544 | tf_op jit(solution)/shard_map/ppermute | solution.py:15
  111.1 1.3 %collective-permute-done.26 = f32[1,128]{1,0:T(1,128)S(1)} collective-permute-done((f32[1,128]{1,0:T(1,128)S(1)}, f32[1,128]{1,0:T(1,128)S(1)}, u32[]{:S(2)}, u32[]{:S(2)}) %collective-permute-start.26) | collective-permute-done | bytes 544 | tf_op jit(solution)/shard_map/ppermute | solution.py:15
  112.4 1.4 %collective-permute-done.27 = f32[1,128]{1,0:T(1,128)S(1)} collective-permute-done((f32[1,128]{1,0:T(1,128)S(1)}, f32[1,128]{1,0:T(1,128)S(1)}, u32[]{:S(2)}, u32[]{:S(2)}) %collective-permute-start.27) | collective-permute-done | bytes 544 | tf_op jit(solution)/shard_map/ppermute | solution.py:15
  114.3 3.0 %collective-permute-done.23.got = bf16[2,64,1024]{2,1,0:T(8,128)(2,1)S(1)} collective-permute-done((bf16[2,64,1024]{2,1,0:T(8,128)(2,1)S(1)}, bf16[2,64,1024]{2,1,0:T(8,128)(2,1)S(1)}, u32[]{:S(2)}, u32[]{:S(2)}) %collective-permute-start.23) | collective-permute-done | bytes 262176 | tf_op jit(solution)/shard_map/ppermute | solution.py:15
  (69 shorter events, 13.0 us)
Async XLA Ops:
  6.5 23.5 %collective-permute-start = (bf16[2,128,1024]{2,1,0:T(8,128)(2,1)}, bf16[2,128,1024]{2,1,0:T(8,128)(2,1)S(1)}, u32[]{:S(2)}, u32[]{:S(2)}) collective-permute-start(bf16[2,128,1024]{2,1,0:T(8,128)(2,1)} %get-tuple-element.19), channel_id=1, source_target_pairs={{0,4},{4,0},{8,12},{12,8},{16,20},{20,16},{24,28},{28,24},{32,36},... | collective-permute-start | bytes 1572872 | tf_op jit(solution)/shard_map/ppermute | solution.py:15
  8.2 15.3 %collective-permute-start.4 = (bf16[2,128,512]{2,1,0:T(8,128)(2,1)}, bf16[2,128,512]{2,1,0:T(8,128)(2,1)S(1)}, u32[]{:S(2)}, u32[]{:S(2)}) collective-permute-start(bf16[2,128,512]{2,1,0:T(8,128)(2,1)} %get-tuple-element.22.refs_4_), channel_id=1, source_target_pairs={{0,2},{1,3},{2,0},{3,1},{4,6},{5,7},{6,4},{7,5},{8,10},{9,11},{10,... | collective-permute-start | bytes 786440 | tf_op jit(solution)/shard_map/ppermute | solution.py:15
  15.4 30.3 %collective-permute-start.5 = (bf16[2,128,512]{2,1,0:T(8,128)(2,1)}, bf16[2,128,512]{2,1,0:T(8,128)(2,1)S(1)}, u32[]{:S(2)}, u32[]{:S(2)}) collective-permute-start(bf16[2,128,512]{2,1,0:T(8,128)(2,1)} %get-tuple-element.22.refs_4_), channel_id=1, source_target_pairs={{0,1},{1,0},{2,3},{3,2},{4,5},{5,4},{6,7},{7,6},{8,9},{9,8},{10,11... | collective-permute-start | bytes 786440 | tf_op jit(solution)/shard_map/ppermute | solution.py:15
  15.4 14.2 %collective-permute-start.7 = (bf16[2,128,512]{2,1,0:T(8,128)(2,1)S(1)}, bf16[2,128,512]{2,1,0:T(8,128)(2,1)S(1)}, u32[]{:S(2)}, u32[]{:S(2)}) collective-permute-start(bf16[2,128,512]{2,1,0:T(8,128)(2,1)S(1)} %copy-done.12), channel_id=1, source_target_pairs={{0,2},{1,3},{2,0},{3,1},{4,6},{5,7},{6,4},{7,5},{8,10},{9,11},{10,... | collective-permute-start | bytes 786440 | tf_op jit(solution)/shard_map/ppermute | solution.py:15
  23.5 22.3 %collective-permute-start.6 = (bf16[2,128,512]{2,1,0:T(8,128)(2,1)S(1)}, bf16[2,128,512]{2,1,0:T(8,128)(2,1)S(1)}, u32[]{:S(2)}, u32[]{:S(2)}) collective-permute-start(bf16[2,128,512]{2,1,0:T(8,128)(2,1)S(1)} %collective-permute-done.4.refs_5_), channel_id=1, source_target_pairs={{0,1},{1,0},{2,3},{3,2},{4,5},{5,4},{6,7},{7,6},{8,9},{9,8},{10,11... | collective-permute-start | bytes 786440 | tf_op jit(solution)/shard_map/ppermute | solution.py:15
  29.6 16.7 %collective-permute-start.8 = (bf16[2,128,512]{2,1,0:T(8,128)(2,1)S(1)}, bf16[2,128,512]{2,1,0:T(8,128)(2,1)S(1)}, u32[]{:S(2)}, u32[]{:S(2)}) collective-permute-start(bf16[2,128,512]{2,1,0:T(8,128)(2,1)S(1)} %collective-permute-done.7), channel_id=1, source_target_pairs={{0,4},{4,0},{8,12},{12,8},{16,20},{20,16},{24,28},{28,24},{32,36},... | collective-permute-start | bytes 786440 | tf_op jit(solution)/shard_map/ppermute | solution.py:15
  30.1 23.3 %collective-permute-start.1 = (bf16[2,128,512]{2,1,0:T(8,128)(2,1)S(1)}, bf16[2,128,512]{2,1,0:T(8,128)(2,1)S(1)}, u32[]{:S(2)}, u32[]{:S(2)}) collective-permute-start(bf16[2,128,512]{2,1,0:T(8,128)(2,1)S(1)} %add_convert_fusion.1.refs_0_), channel_id=1, source_target_pairs={{0,2},{1,3},{2,0},{3,1},{4,6},{5,7},{6,4},{7,5},{8,10},{9,11},{10,... | collective-permute-start | bytes 786440 | tf_op jit(solution)/shard_map/ppermute | solution.py:15
  44.2 10.8 %collective-permute-start.11 = (bf16[2,128,1024]{2,1,0:T(8,128)(2,1)S(1)}, bf16[2,128,1024]{2,1,0:T(8,128)(2,1)S(1)}, u32[]{:S(2)}, u32[]{:S(2)}) collective-permute-start(bf16[2,128,1024]{2,1,0:T(8,128)(2,1)S(1)} %get-tuple-element.25), channel_id=1, source_target_pairs={{0,4},{4,0},{8,12},{12,8},{16,20},{20,16},{24,28},{28,24},{32,36},... | collective-permute-start | bytes 1572872 | tf_op jit(solution)/shard_map/ppermute | solution.py:15
  45.7 9.2 %collective-permute-start.9 = (bf16[2,128,1024]{2,1,0:T(8,128)(2,1)S(1)}, bf16[2,128,1024]{2,1,0:T(8,128)(2,1)S(1)}, u32[]{:S(2)}, u32[]{:S(2)}) collective-permute-start(bf16[2,128,1024]{2,1,0:T(8,128)(2,1)S(1)} %collective-permute-done.refs_8_), channel_id=1, source_target_pairs={{0,1},{1,0},{2,3},{3,2},{4,5},{5,4},{6,7},{7,6},{8,9},{9,8},{10,11... | collective-permute-start | bytes 1572872 | tf_op jit(solution)/shard_map/ppermute | solution.py:15
  45.7 7.7 %collective-permute-start.2 = (bf16[2,128,512]{2,1,0:T(8,128)(2,1)S(1)}, bf16[2,128,512]{2,1,0:T(8,128)(2,1)S(1)}, u32[]{:S(2)}, u32[]{:S(2)}) collective-permute-start(bf16[2,128,512]{2,1,0:T(8,128)(2,1)S(1)} %add_convert_fusion.1.refs_0_), channel_id=1, source_target_pairs={{0,1},{1,0},{2,3},{3,2},{4,5},{5,4},{6,7},{7,6},{8,9},{9,8},{10,11... | collective-permute-start | bytes 786440 | tf_op jit(solution)/shard_map/ppermute | solution.py:15
  46.2 7.2 %collective-permute-start.10 = (bf16[2,128,512]{2,1,0:T(8,128)(2,1)S(1)}, bf16[2,128,512]{2,1,0:T(8,128)(2,1)S(1)}, u32[]{:S(2)}, u32[]{:S(2)}) collective-permute-start(bf16[2,128,512]{2,1,0:T(8,128)(2,1)S(1)} %collective-permute-done.8.refs_9_), channel_id=1, source_target_pairs={{0,1},{1,0},{2,3},{3,2},{4,5},{5,4},{6,7},{7,6},{8,9},{9,8},{10,11... | collective-permute-start | bytes 786440 | tf_op jit(solution)/shard_map/ppermute | solution.py:15
  59.5 9.9 %collective-permute-start.12 = (bf16[2,128,512]{2,1,0:T(8,128)(2,1)S(1)}, bf16[2,128,512]{2,1,0:T(8,128)(2,1)S(1)}, u32[]{:S(2)}, u32[]{:S(2)}) collective-permute-start(bf16[2,128,512]{2,1,0:T(8,128)(2,1)S(1)} %get-tuple-element.26), channel_id=1, source_target_pairs={{0,8},{4,12},{8,0},{12,4},{16,24},{20,28},{24,16},{28,20},{32,40},... | collective-permute-start | bytes 786440 | tf_op jit(solution)/shard_map/ppermute | solution.py:15
  62.4 16.4 %collective-permute-start.16 = (bf16[2,128,512]{2,1,0:T(8,128)(2,1)S(1)}, bf16[2,128,512]{2,1,0:T(8,128)(2,1)S(1)}, u32[]{:S(2)}, u32[]{:S(2)}) collective-permute-start(bf16[2,128,512]{2,1,0:T(8,128)(2,1)S(1)} %get-tuple-element.28.refs_4_), channel_id=1, source_target_pairs={{0,2},{1,3},{2,0},{3,1},{4,6},{5,7},{6,4},{7,5},{8,10},{9,11},{10,... | collective-permute-start | bytes 786440 | tf_op jit(solution)/shard_map/ppermute | solution.py:15
  68.8 10.8 %collective-permute-start.17 = (bf16[2,128,512]{2,1,0:T(8,128)(2,1)S(1)}, bf16[2,128,512]{2,1,0:T(8,128)(2,1)S(1)}, u32[]{:S(2)}, u32[]{:S(2)}) collective-permute-start(bf16[2,128,512]{2,1,0:T(8,128)(2,1)S(1)} %get-tuple-element.28.refs_4_), channel_id=1, source_target_pairs={{0,1},{1,0},{2,3},{3,2},{4,5},{5,4},{6,7},{7,6},{8,9},{9,8},{10,11... | collective-permute-start | bytes 786440 | tf_op jit(solution)/shard_map/ppermute | solution.py:15
  69.5 10.5 %collective-permute-start.19 = (bf16[2,128,512]{2,1,0:T(8,128)(2,1)S(1)}, bf16[2,128,512]{2,1,0:T(8,128)(2,1)S(1)}, u32[]{:S(2)}, u32[]{:S(2)}) collective-permute-start(bf16[2,128,512]{2,1,0:T(8,128)(2,1)S(1)} %get-tuple-element.28.refs_4_), channel_id=1, source_target_pairs={{0,8},{4,12},{8,0},{12,4},{16,24},{20,28},{24,16},{28,20},{32,40},... | collective-permute-start | bytes 786440 | tf_op jit(solution)/shard_map/ppermute | solution.py:15
  72.4 19.8 %collective-permute-start.13 = (bf16[2,128,512]{2,1,0:T(8,128)(2,1)S(1)}, bf16[2,128,512]{2,1,0:T(8,128)(2,1)S(1)}, u32[]{:S(2)}, u32[]{:S(2)}) collective-permute-start(bf16[2,128,512]{2,1,0:T(8,128)(2,1)S(1)} %add_convert_fusion.refs_0_), channel_id=1, source_target_pairs={{0,2},{1,3},{2,0},{3,1},{4,6},{5,7},{6,4},{7,5},{8,10},{9,11},{10,... | collective-permute-start | bytes 786440 | tf_op jit(solution)/shard_map/ppermute | solution.py:15
  78.8 13.4 %collective-permute-start.20 = (bf16[2,128,512]{2,1,0:T(8,128)(2,1)S(1)}, bf16[2,128,512]{2,1,0:T(8,128)(2,1)S(1)}, u32[]{:S(2)}, u32[]{:S(2)}) collective-permute-start(bf16[2,128,512]{2,1,0:T(8,128)(2,1)S(1)} %collective-permute-done.16.refs_5_), channel_id=1, source_target_pairs={{0,8},{4,12},{8,0},{12,4},{16,24},{20,28},{24,16},{28,20},{32,40},... | collective-permute-start | bytes 786440 | tf_op jit(solution)/shard_map/ppermute | solution.py:15
  79.5 13.2 %collective-permute-start.14 = (bf16[2,128,512]{2,1,0:T(8,128)(2,1)S(1)}, bf16[2,128,512]{2,1,0:T(8,128)(2,1)S(1)}, u32[]{:S(2)}, u32[]{:S(2)}) collective-permute-start(bf16[2,128,512]{2,1,0:T(8,128)(2,1)S(1)} %add_convert_fusion.refs_0_), channel_id=1, source_target_pairs={{0,1},{1,0},{2,3},{3,2},{4,5},{5,4},{6,7},{7,6},{8,9},{9,8},{10,11... | collective-permute-start | bytes 786440 | tf_op jit(solution)/shard_map/ppermute | solution.py:15
  79.6 13.2 %collective-permute-start.18 = (bf16[2,128,512]{2,1,0:T(8,128)(2,1)S(1)}, bf16[2,128,512]{2,1,0:T(8,128)(2,1)S(1)}, u32[]{:S(2)}, u32[]{:S(2)}) collective-permute-start(bf16[2,128,512]{2,1,0:T(8,128)(2,1)S(1)} %collective-permute-done.16.refs_5_), channel_id=1, source_target_pairs={{0,1},{1,0},{2,3},{3,2},{4,5},{5,4},{6,7},{7,6},{8,9},{9,8},{10,11... | collective-permute-start | bytes 786440 | tf_op jit(solution)/shard_map/ppermute | solution.py:15
  80.1 12.7 %collective-permute-start.21 = (bf16[2,128,512]{2,1,0:T(8,128)(2,1)S(1)}, bf16[2,128,512]{2,1,0:T(8,128)(2,1)S(1)}, u32[]{:S(2)}, u32[]{:S(2)}) collective-permute-start(bf16[2,128,512]{2,1,0:T(8,128)(2,1)S(1)} %collective-permute-done.19.refs_8_), channel_id=1, source_target_pairs={{0,1},{1,0},{2,3},{3,2},{4,5},{5,4},{6,7},{7,6},{8,9},{9,8},{10,11... | collective-permute-start | bytes 786440 | tf_op jit(solution)/shard_map/ppermute | solution.py:15
  106.6 4.5 %collective-permute-start.25 = (f32[1,128]{1,0:T(1,128)S(1)}, f32[1,128]{1,0:T(1,128)S(1)}, u32[]{:S(2)}, u32[]{:S(2)}) collective-permute-start(f32[1,128]{1,0:T(1,128)S(1)} %add.25), channel_id=1, source_target_pairs={{0,64},{64,0},{128,192},{192,128},{1,65},{65,1},{129,193},{193,129... | collective-permute-start | bytes 1544 | tf_op jit(solution)/shard_map/ppermute | solution.py:15
  107.9 4.5 %collective-permute-start.26 = (f32[1,128]{1,0:T(1,128)S(1)}, f32[1,128]{1,0:T(1,128)S(1)}, u32[]{:S(2)}, u32[]{:S(2)}) collective-permute-start(f32[1,128]{1,0:T(1,128)S(1)} %add.25), channel_id=1, source_target_pairs={{0,128},{64,192},{128,0},{192,64},{1,129},{65,193},{129,1},{193,65... | collective-permute-start | bytes 1544 | tf_op jit(solution)/shard_map/ppermute | solution.py:15
  108.4 5.4 %collective-permute-start.27 = (f32[1,128]{1,0:T(1,128)S(1)}, f32[1,128]{1,0:T(1,128)S(1)}, u32[]{:S(2)}, u32[]{:S(2)}) collective-permute-start(f32[1,128]{1,0:T(1,128)S(1)} %add.25), channel_id=1, source_target_pairs={{0,192},{64,128},{128,64},{192,0},{1,193},{65,129},{129,65},{193,1... | collective-permute-start | bytes 1544 | tf_op jit(solution)/shard_map/ppermute | solution.py:15
  111.0 6.4 %collective-permute-start.23 = (bf16[2,64,1024]{2,1,0:T(8,128)(2,1)S(1)}, bf16[2,64,1024]{2,1,0:T(8,128)(2,1)S(1)}, u32[]{:S(2)}, u32[]{:S(2)}) collective-permute-start(bf16[2,64,1024]{2,1,0:T(8,128)(2,1)S(1)} %get-tuple-element.32), channel_id=1, source_target_pairs={{0,4},{4,0},{8,12},{12,8},{16,20},{20,16},{24,28},{28,24},{32,36},... | collective-permute-start | bytes 786440 | tf_op jit(solution)/shard_map/ppermute | solution.py:15
  (17 other events, 205.1 us)
